TPU v7x, 256 devices: a whole 4x4x8 slice. The times are simulated.
256 devices in a mesh: expert: 64 (over z, x, core), mp: 4 (over y).
Axes of the slice: x: 4, y: 4, z: 8, core: 2. Of those that a mesh axis runs over, the one named last changes fastest.
Arguments:
- tokens: bfloat16 [16384, 1024], P('expert'), may hold values from -6 to 6
- cotangent: bfloat16 [16384, 1024], P('expert'), may hold values from -16 to 16
- routes: int32 [16384, 2], P('expert'), may hold values from 0 to 63, all different within a row; in each aligned block of 256 rows (0 to 255, 256 to 511, ...) at most 12 rows name the same one
- router_weight: bfloat16 [1024, 64], replicated, may hold values from -0.1875 to 0.1875
- gate_weight: bfloat16 [64, 1024, 3584], P('expert', None, 'mp'), may hold values from -0.1875 to 0.1875
- up_weight: bfloat16 [64, 1024, 3584], P('expert', None, 'mp'), may hold values from -0.6875 to 0.6875
- down_weight: bfloat16 [64, 3584, 1024], P('expert', 'mp'), may hold values from -0.3674842 to 0.3674842
- mlp_in: float32 [3, 16], replicated, may hold values from -3.5 to 3.5
- mlp_bias: float32 [16], replicated, may hold values from -2 to 2
- mlp_out: float32 [16], replicated, may hold values from -1.5 to 1.5
Outputs:
- mixed: bfloat16 [16384, 1024], P('expert', 'mp')
- gate_update: bfloat16 [64, 1024, 3584], P('expert', None, 'mp')
- up_update: bfloat16 [64, 1024, 3584], P('expert', None, 'mp')
- down_update: bfloat16 [64, 3584, 1024], P('expert', 'mp')
- router_update: bfloat16 [1024, 64], replicated
Inputs may be any that keep to these rules, and one draw needn't show every extreme that they name: `routes`: in the rows of one index of the expert axis each expert is named at most 12 times; the two experts of a row differ.
All inputs are finite; a program needn't handle non-finite values.
Results may differ from a plain program's by a relative error of at most 0.0057.
Values may be sent and summed in bfloat16 or wider, within the bound.
No kernel may reach another device: no remote copies, remote signals or barrier semaphores. Data moves between devices by JAX's collectives and lax.ppermute only.
A program may use at most 128 MiB of HBM per device.

v0:
```python
import functools

import jax
import jax.numpy as jnp
from jax import lax
from jax.experimental import pallas as pl
from jax.experimental.pallas import tpu as pltpu
from jax.sharding import Mesh
from jax.sharding import PartitionSpec as P

D = 1024
FF = 3584
UNITS = 16
EXPERT = ("expert_0", "expert_1", "expert_2")
EPSILON = 1e-06

CAP = 12
GROUP = 16
GROUPS = 4
BLOCK = GROUP * CAP
LANES = 128
BF = jnp.bfloat16
F32 = jnp.float32
HIGHEST = lax.Precision.HIGHEST


def params(**kw):
    return pltpu.CompilerParams(vmem_limit_bytes=48 << 20, **kw)


def in_hbm(x):
    return pltpu.with_memory_space_constraint(x, pltpu.HBM)


def iota(shape, dim):
    return lax.broadcasted_iota(jnp.int32, shape, dim)


def dot(a, b, dims=((1,), (0,)), **kw):
    return lax.dot_general(a, b, (dims, ((), ())), preferred_element_type=F32, **kw)


def row_sum(x):
    return jnp.sum(x, axis=1, keepdims=True)


DATA = 2 * CAP
SIDE = 8


def routing(routes, experts):
    across = routes[...].astype(F32).T
    n = across.shape[0]
    ids = [across[:, k : k + 1].astype(jnp.int32) for k in range(2)]
    hits = [(ids[k] == iota((n, experts), 1)).astype(F32) for k in range(2)]
    earlier = (iota((n, n), 0) > iota((n, n), 1)).astype(F32).astype(BF)
    before = dot(earlier, (hits[0] + hits[1]).astype(BF))
    places = [row_sum(before * hits[k]).astype(jnp.int32) for k in range(2)]
    return ids, places, hits


def one_hot(index, size):
    return (index == iota((index.shape[0], size), 1)).astype(F32).astype(BF)


def send_x_kernel(mp, tok_cols, routes, x_out, *, experts):
    del mp
    ids, places, _ = routing(routes, experts)
    rows = x_out.shape[0]
    total = jnp.zeros((rows, LANES), F32)
    for h in range(2):
        picks = [one_hot(ids[k] * DATA + places[k] + h * CAP, rows) for k in range(2)]
        total = total + dot(
            picks[0] + picks[1], tok_cols[:, h * LANES : (h + 1) * LANES], ((0,), (0,))
        )
    x_out[...] = total.astype(BF)


def send_dy_kernel(mp, tok, cot_cols, routes, router, dy_out, aux_out):
    del mp
    n = tok.shape[0]
    experts = router.shape[0]
    rows = dy_out.shape[0]
    size = DATA + SIDE
    ids, places, hits = routing(routes, experts)
    logits = dot(tok[...], router[...], ((1,), (1,)))
    sig = [1.0 / (1.0 + jnp.exp(-row_sum(logits * hits[k]))) for k in range(2)]
    denominator = sig[0] + sig[1]
    gates = [s / denominator for s in sig]
    cot = cot_cols[...].astype(F32)
    total = jnp.zeros((rows, LANES), F32)
    sides = [jnp.zeros((experts, LANES), F32) for _ in range(5)]
    for k in range(2):
        scaled = (gates[k] * cot).astype(BF)
        for h in range(2):
            pick = one_hot(ids[k] * size + places[k] + h * CAP, rows)
            total = total + dot(pick, scaled[:, h * LANES : (h + 1) * LANES], ((0,), (0,)))
        own = gates[1 - k] * (1.0 - sig[k])
        other = -gates[1 - k] * (1.0 - sig[1 - k])
        values = two_parts(own) + two_parts(other) + (ids[1 - k],)
        slot = one_hot(places[k], LANES).astype(F32)
        for i, value in enumerate(values):
            placed = (slot * value.astype(F32)).astype(BF)
            sides[i] = sides[i] + dot(hits[k].astype(BF), placed, ((0,), (0,)))
    expert = iota((experts, rows), 0) * size + DATA
    for i in range(5):
        row = (expert + i == iota((experts, rows), 1)).astype(F32).astype(BF)
        total = total + dot(row, sides[i].astype(BF), ((0,), (0,)))
    dy_out[...] = total.astype(BF)
    lane = iota((n, LANES), 1)
    aux = jnp.zeros((n, LANES), F32)
    for i, column in enumerate(gates + [i.astype(F32) for i in ids + places]):
        aux = jnp.where(lane == i, column, aux)
    aux_out[...] = aux


def send_x(tokens, routes, experts, index):
    n, _ = tokens.shape
    rows = experts * DATA
    return pl.pallas_call(
        functools.partial(send_x_kernel, experts=experts),
        grid_spec=pltpu.PrefetchScalarGridSpec(
            num_scalar_prefetch=1,
            grid=(1,),
            in_specs=[
                pl.BlockSpec((n, 2 * LANES), lambda i, at: (0, at[0])),
                pl.BlockSpec((2, n), lambda i, at: (0, 0)),
            ],
            out_specs=pl.BlockSpec((rows, LANES), lambda i, at: (0, 0)),
        ),
        out_shape=jax.ShapeDtypeStruct((rows, LANES), BF),
        compiler_params=params(),
        name="send_x",
    )(index, tokens, routes)


def send_dy(tokens, cotangent, routes, router, index):
    n, width = tokens.shape
    experts = router.shape[0]
    rows = experts * (DATA + SIDE)
    whole = lambda *shape: pl.BlockSpec(shape, lambda i, at: (0,) * len(shape))
    return pl.pallas_call(
        send_dy_kernel,
        grid_spec=pltpu.PrefetchScalarGridSpec(
            num_scalar_prefetch=1,
            grid=(1,),
            in_specs=[
                whole(n, width),
                pl.BlockSpec((n, 2 * LANES), lambda i, at: (0, at[0])),
                whole(2, n),
                whole(experts, width),
            ],
            out_specs=[whole(rows, LANES), whole(n, LANES)],
        ),
        out_shape=[
            jax.ShapeDtypeStruct((rows, LANES), BF),
            jax.ShapeDtypeStruct((n, LANES), F32),
        ],
        compiler_params=params(),
        name="send_dy",
    )(index, tokens, cotangent, routes, router)


def column_of(mp, k, h):
    member = lax.rem(mp + k + GROUPS, GROUPS)
    return pl.multiple_of((2 * member + h) * LANES, LANES)


def unpack_rows(perm, mp, messages, to, blocks):
    for b in range(blocks):
        at = slice(b * 2 * BLOCK, (b + 1) * 2 * BLOCK)
        both = dot(perm, jnp.concatenate([m[at, :] for m in messages], axis=1)).astype(BF)
        for h in range(2):
            for k in range(GROUPS):
                to[b * BLOCK : (b + 1) * BLOCK, pl.ds(column_of(mp, -k, h), LANES)] = both[
                    h * BLOCK : (h + 1) * BLOCK, k * LANES : (k + 1) * LANES
                ]


def forward_kernel(mp, perm, perm_t, m0, m1, m2, m3, gate, up, down, *refs):
    rows_x, hidden, by_gate, by_up = refs[:4]
    parts = refs[4 : 4 + GROUPS]
    outs = refs[4 + GROUPS]
    step = pl.program_id(0)
    blocks = rows_x.shape[0] // BLOCK

    @pl.when(step == 0)
    def _():
        unpack_rows(perm[...], mp[0], (m0, m1, m2, m3), rows_x, blocks)

    acts = dot(rows_x[...], jnp.concatenate([gate[...], up[...]], axis=1))
    act_gate = acts[:, :LANES]
    act_up = acts[:, LANES:]
    s = 1.0 / (1.0 + jnp.exp(-act_gate))
    silu = act_gate * s
    hidden[:, pl.ds(pl.multiple_of(step * LANES, LANES), LANES)] = (silu * act_up).astype(BF)
    by_gate[...] = act_up * s * (1.0 + act_gate * (1.0 - s))
    by_up[...] = silu

    @pl.when(step == pl.num_programs(0) - 1)
    def _():
        outs[...] = dot(hidden[...], down[...]).astype(BF)
        for b in range(blocks):
            halves = [
                jnp.concatenate(
                    [
                        outs[b * BLOCK : (b + 1) * BLOCK, pl.ds(column_of(mp[0], k, h), LANES)]
                        for k in range(GROUPS)
                    ],
                    axis=1,
                )
                for h in range(2)
            ]
            packed = dot(perm_t[...], jnp.concatenate(halves, axis=0)).astype(BF)
            for k in range(GROUPS):
                parts[k][b * 2 * BLOCK : (b + 1) * 2 * BLOCK, :] = packed[
                    :, k * LANES : (k + 1) * LANES
                ]


def expert_forward(mp_index, perm, perm_t, messages, w_gate, w_up, w_down):
    sent, _ = messages[0].shape
    rows = sent // 2
    width, ff = w_gate.shape
    whole = lambda *shape: pl.BlockSpec(shape, lambda i, mp: (0,) * len(shape))
    column = lambda n: pl.BlockSpec((n, LANES), lambda i, mp: (0, i))
    return pl.pallas_call(
        forward_kernel,
        grid_spec=pltpu.PrefetchScalarGridSpec(
            num_scalar_prefetch=1,
            grid=(ff // LANES,),
            in_specs=[whole(*perm.shape), whole(*perm.shape)]
            + [whole(sent, LANES)] * GROUPS
            + [column(width), column(width), whole(ff, width)],
            out_specs=[whole(rows, width), whole(rows, ff), column(rows), column(rows)]
            + [whole(sent, LANES)] * GROUPS,
            scratch_shapes=[pltpu.VMEM((rows, width), BF)],
        ),
        out_shape=[
            jax.ShapeDtypeStruct((rows, width), BF),
            jax.ShapeDtypeStruct((rows, ff), BF),
            jax.ShapeDtypeStruct((rows, ff), F32),
            jax.ShapeDtypeStruct((rows, ff), F32),
        ]
        + [jax.ShapeDtypeStruct((sent, LANES), BF)] * GROUPS,
        compiler_params=params(),
        name="expert_forward",
    )(mp_index, perm, perm_t, *messages, w_gate, w_up, w_down)


def backward_kernel(
    at, perm, m0, m1, m2, m3, side, down, hidden, by_gate, by_up, rows_x,
    rows_dy, d_gate, d_up, router, total,
):
    part = rows_dy.shape[0]
    experts = router.shape[0]
    unpack_rows(perm[...], at[0], (m0, m1, m2, m3), rows_dy, part // BLOCK)
    grad_hidden = dot(rows_dy[...], down[...], ((1,), (1,)))
    d_gate[...] = (grad_hidden * by_gate[...]).astype(BF)
    d_up[...] = (grad_hidden * by_up[...]).astype(BF)
    q = row_sum(hidden[...].astype(F32) * grad_hidden)
    row = iota((part, part // CAP), 0)
    first = iota((part, part // CAP), 1) * CAP
    source = ((row >= first) & (row < first + CAP)).astype(F32)
    place = (iota((part, 1), 0).astype(F32) - row_sum(source * first.astype(F32))).astype(jnp.int32)
    slot = (place == iota((part, LANES), 1)).astype(F32)
    spread = dot(source.astype(BF), jnp.concatenate([side[i] for i in range(5)], axis=1))
    values = [row_sum(spread[:, i * LANES : (i + 1) * LANES] * slot) for i in range(5)]
    own = q * (values[0] + values[1])
    other = q * (values[2] + values[3])
    lane = iota((part, experts), 1)
    grads = jnp.where(lane == at[1], own, 0.0)
    grads = jnp.where(lane == values[4].astype(jnp.int32), other, grads)
    both = dot(jnp.concatenate(two_parts(grads), axis=1), rows_x[...], ((0,), (0,)))
    grad = both[:experts] + both[experts:]

    @pl.when(pl.program_id(0) == 0)
    def _():
        total[...] = grad

    @pl.when(pl.program_id(0) == pl.num_programs(0) - 1)
    def _():
        whole = total[...] + grad
        for j in range(router.shape[1]):
            router[:, j, :] = whole[:, j * LANES : (j + 1) * LANES]


def expert_backward(index, perm, messages, side, w_down, hidden, by_gate, by_up, rows_x):
    sent, _ = messages[0].shape
    steps = 2
    rows = sent // 2
    part = rows // steps
    experts = rows // CAP
    ff, width = w_down.shape
    whole = lambda *shape: pl.BlockSpec(shape, lambda i, at: (0,) * len(shape))
    row = lambda n, m: pl.BlockSpec((n, m), lambda i, at: (i, 0))
    return pl.pallas_call(
        backward_kernel,
        grid_spec=pltpu.PrefetchScalarGridSpec(
            num_scalar_prefetch=1,
            grid=(steps,),
            in_specs=[whole(*perm.shape)]
            + [row(sent // steps, LANES)] * GROUPS
            + [pl.BlockSpec((SIDE, part // CAP, LANES), lambda i, at: (0, i, 0))]
            + [whole(ff, width), row(part, ff), row(part, ff), row(part, ff), row(part, width)],
            out_specs=[
                row(part, width),
                row(part, ff),
                row(part, ff),
                whole(experts, width // LANES, LANES),
            ],
            scratch_shapes=[pltpu.VMEM((experts, width), F32)],
        ),
        out_shape=[
            jax.ShapeDtypeStruct((rows, width), BF),
            jax.ShapeDtypeStruct((rows, ff), BF),
            jax.ShapeDtypeStruct((rows, ff), BF),
            jax.ShapeDtypeStruct((experts, width // LANES, LANES), F32),
        ],
        compiler_params=params(),
        name="expert_backward",
    )(index, perm, *messages, side, w_down, hidden, by_gate, by_up, rows_x)


def add_squares(total, grad, to):
    step = pl.program_id(0)
    squares = jnp.sum(grad * grad, axis=0, keepdims=True)

    @pl.when(step == 0)
    def _():
        total[...] = squares

    @pl.when(step > 0)
    def _():
        total[...] += squares

    @pl.when(step == pl.num_programs(0) - 1)
    def _():
        to[...] = jnp.broadcast_to(row_sum(total[...]), to.shape)


def grad_in_kernel(rows_x, d_gate, d_up, g_gate, g_up, s_gate, s_up, t_gate, t_up):
    across = rows_x[...].T
    for d, g, s, t in ((d_gate, g_gate, s_gate, t_gate), (d_up, g_up, s_up, t_up)):
        grad = dot(across, d[...])
        g[...] = grad
        add_squares(t, grad, s)


def grad_in(rows_x, d_gate, d_up):
    rows, width = rows_x.shape
    ff = d_gate.shape[1]
    chunk = 256
    whole = lambda *shape: pl.BlockSpec(shape, lambda i: (0,) * len(shape))
    return pl.pallas_call(
        grad_in_kernel,
        grid=(width // chunk,),
        in_specs=[pl.BlockSpec((rows, chunk), lambda i: (0, i)), whole(rows, ff), whole(rows, ff)],
        out_specs=[pl.BlockSpec((chunk, ff), lambda i: (i, 0))] * 2 + [whole(1, LANES)] * 2,
        out_shape=[jax.ShapeDtypeStruct((width, ff), F32)] * 2
        + [jax.ShapeDtypeStruct((1, LANES), F32)] * 2,
        scratch_shapes=[pltpu.VMEM((1, ff), F32)] * 2,
        compiler_params=params(),
        name="grad_in",
    )(rows_x, d_gate, d_up)


def grad_down_kernel(hidden, rows_dy, g_down, s_down, across, total):
    @pl.when(pl.program_id(0) == 0)
    def _():
        across[...] = hidden[...].T

    grad = dot(across[...], rows_dy[...])
    g_down[...] = grad
    add_squares(total, grad, s_down)


def grad_down(hidden, rows_dy):
    rows, ff = hidden.shape
    width = rows_dy.shape[1]
    chunk = 256
    whole = lambda *shape: pl.BlockSpec(shape, lambda i: (0,) * len(shape))
    return pl.pallas_call(
        grad_down_kernel,
        grid=(width // chunk,),
        in_specs=[whole(rows, ff), pl.BlockSpec((rows, chunk), lambda i: (0, i))],
        out_specs=[pl.BlockSpec((ff, chunk), lambda i: (0, i)), whole(1, LANES)],
        out_shape=[
            jax.ShapeDtypeStruct((ff, width), F32),
            jax.ShapeDtypeStruct((1, LANES), F32),
        ],
        scratch_shapes=[pltpu.VMEM((ff, rows), BF), pltpu.VMEM((1, chunk), F32)],
        compiler_params=params(),
        name="grad_down",
    )(hidden, rows_dy)


NET_ROWS = 32


def two_parts(x):
    high = x.astype(BF)
    return high, (x - high.astype(F32)).astype(BF)


def spread_kernel(coef, to):
    k = UNITS * NET_ROWS
    c = 8 * NET_ROWS
    same = iota((k, c), 0) % NET_ROWS == iota((k, c), 1) % NET_ROWS
    feature = iota((k, c), 1) // NET_ROWS
    value = jnp.zeros((k, c), F32)
    for part in range(3):
        a = coef[:, part : part + 1]
        high = a.astype(BF).astype(F32)
        low = a - high
        if part < 2:
            values = (high, low, high)
        else:
            values = (high, low)
        for i, v in enumerate(values):
            value = jnp.where(feature == part * 3 + i, v, value)
    to[...] = jnp.where(same, value, 0.0).astype(BF)


def spread_weights(mlp_in, weight_scale):
    coef = jnp.stack([mlp_in[0], mlp_in[2], mlp_in[1] * weight_scale], axis=1)
    coef = jnp.repeat(coef, NET_ROWS, axis=0)
    return pl.pallas_call(
        spread_kernel,
        out_shape=jax.ShapeDtypeStruct((UNITS * NET_ROWS, 8 * NET_ROWS), BF),
        compiler_params=params(),
        name="spread_weights",
    )(coef)


def step_kernel(scalars, rms, spread, grad, weight, out, *, rows):
    n = NET_ROWS
    height, width = grad.shape
    inverse = rms[0]
    constant = scalars[2, 0]

    def features(r, c, lanes):
        w = weight[pl.ds(r, n), c : c + lanes]
        f0 = grad[pl.ds(r, n), c : c + lanes] * inverse
        h0, l0 = two_parts(f0)
        h2, l2 = two_parts(jnp.tanh(f0))
        return jnp.concatenate([h0, h0, l0, h2, h2, l2, w, w], axis=0)

    def network(feats):
        y = dot(spread[...], feats)
        total = jnp.full((n, feats.shape[1]), constant, F32)
        for j in range(UNITS):
            total = total + scalars[1, j] * jnp.maximum(y[j * n : (j + 1) * n], scalars[0, j])
        return total.astype(BF)

    def body(i, carry):
        r = pl.multiple_of(i * rows, rows)
        for pair in range(0, rows, 2 * n):
            at = [r + pair, r + pair + n]
            whole = width // 256 * 256
            for c in range(0, whole, 256):
                for a in at:
                    out[pl.ds(a, n), c : c + 256] = network(features(a, c, 256))
            if whole < width:
                u = network(jnp.concatenate([features(a, whole, 128) for a in at], axis=1))
                for i, a in enumerate(at):
                    out[pl.ds(a, n), whole:width] = u[:, i * 128 : (i + 1) * 128]
        return carry

    lax.fori_loop(0, height // rows, body, 0)


def learned_step(grad, weight, rms, spread, scalars):
    height, width = grad.shape
    block = 128
    tile = pl.BlockSpec((block, width), lambda i: (i, 0))
    return pl.pallas_call(
        functools.partial(step_kernel, rows=128),
        grid=(height // block,),
        in_specs=[
            pl.BlockSpec(memory_space=pltpu.SMEM),
            pl.BlockSpec(memory_space=pltpu.SMEM),
            pl.BlockSpec(spread.shape, lambda i: (0, 0)),
            tile,
            tile,
        ],
        out_specs=tile,
        out_shape=jax.ShapeDtypeStruct((height, width), BF),
        compiler_params=params(),
        name="learned_step",
    )(scalars, rms, spread, in_hbm(grad), in_hbm(weight))


def mix_kernel(at, aux, tok_cols, back, out, *, size):
    del at
    rows = back.shape[0]
    for h in range(2):
        cols = slice(h * LANES, (h + 1) * LANES)
        total = tok_cols[:, cols].astype(F32)
        for k in range(2):
            base = aux[:, 2 + k : 3 + k] * size + aux[:, 4 + k : 5 + k] + h * CAP
            total = total + aux[:, k : k + 1] * dot(
                one_hot(base.astype(jnp.int32), rows), back[...]
            )
        out[:, cols] = total.astype(BF)


def mix(index, aux, tokens, back, experts):
    n = tokens.shape[0]
    cols = 2 * LANES
    whole = lambda *shape: pl.BlockSpec(shape, lambda i, at: (0,) * len(shape))
    mine = pl.BlockSpec((n, cols), lambda i, at: (0, at[0]))
    return pl.pallas_call(
        functools.partial(mix_kernel, size=back.shape[0] // experts),
        grid_spec=pltpu.PrefetchScalarGridSpec(
            num_scalar_prefetch=1,
            grid=(1,),
            in_specs=[whole(n, LANES), mine, whole(*back.shape)],
            out_specs=whole(n, cols),
        ),
        out_shape=jax.ShapeDtypeStruct((n, cols), BF),
        compiler_params=params(),
        name="mix",
    )(index, aux, tokens, back)


def router_step_kernel(net, columns, weight, out):
    experts, width = weight.shape
    grad = jnp.concatenate([columns[:, j, :] for j in range(width // LANES)], axis=1)
    mean = jnp.sum(row_sum(grad * grad), axis=0, keepdims=True) * (1.0 / grad.size)
    f0 = grad / jnp.sqrt(mean + EPSILON)
    f1 = weight[...].astype(F32) * D**0.5
    f2 = jnp.tanh(f0)
    total = jnp.zeros_like(f0)
    for j in range(UNITS):
        total = total + net[4, j] * jnp.maximum(
            net[0, j] * f0 + net[1, j] * f1 + net[2, j] * f2 + net[3, j], 0.0
        )
    out[...] = total.astype(BF)


def router_step(net, parts, weight):
    return pl.pallas_call(
        router_step_kernel,
        in_specs=[
            pl.BlockSpec(memory_space=pltpu.SMEM),
            pl.BlockSpec(memory_space=pltpu.VMEM),
            pl.BlockSpec(memory_space=pltpu.VMEM),
        ],
        out_shape=jax.ShapeDtypeStruct(weight.shape, BF),
        compiler_params=params(),
        name="router_step",
    )(net, parts, weight)


def to_experts(x, peers):
    sent = x.reshape(peers, -1, x.shape[-1])
    return lax.all_to_all(sent, EXPERT, 0, 0, tiled=True)


def from_members(pieces):
    return [pieces[0]] + [
        lax.ppermute(pieces[k], "mp", [(i, (i + k) % GROUPS) for i in range(GROUPS)])
        for k in range(1, GROUPS)
    ]


def together(values):
    return lax.optimization_barrier(values)


def to_all_experts(x, peers):
    return lax.all_to_all(jnp.broadcast_to(x[None], (peers, *x.shape)), EXPERT, 0, 0, tiled=True)


def on_device(
    tokens,
    cotangent,
    routes,
    router_weight,
    gate_weight,
    up_weight,
    down_weight,
    mlp_in,
    mlp_bias,
    mlp_out,
):
    experts = lax.axis_size(EXPERT)
    groups = lax.axis_size("mp")
    width = tokens.shape[1]
    index = jnp.stack([lax.axis_index("mp"), lax.axis_index(EXPERT)]).astype(jnp.int32)
    w_gate = gate_weight[0]
    w_up = up_weight[0]
    w_down = down_weight[0]

    pos = jnp.arange(2 * BLOCK, dtype=jnp.int32)
    inner = pos % BLOCK
    source_row = inner + inner // CAP * CAP + pos // BLOCK * CAP
    perm = (source_row[:, None] == pos[None, :]).astype(BF)
    perm_t = (source_row[None, :] == pos[:, None]).astype(BF)
    spread_in = spread_weights(mlp_in, D**0.5)
    spread_down = spread_weights(mlp_in, FF**0.5)
    scalars = jnp.stack(
        [-mlp_bias, mlp_out, jnp.broadcast_to(jnp.sum(mlp_bias * mlp_out), mlp_out.shape)]
    )
    net = jnp.concatenate([mlp_in, mlp_bias[None], mlp_out[None]], axis=0)
    router_across = router_weight.T

    routes_across = routes.T
    sent_x = send_x(tokens, routes_across, experts, index)
    own_x = to_experts(sent_x, experts).reshape(-1, LANES)
    sent_dy, aux = send_dy(tokens, cotangent, routes_across, router_across, index)
    msg_x = from_members([own_x] * GROUPS)
    own_dy = to_experts(sent_dy, experts)
    side = own_dy[:, DATA:].transpose(1, 0, 2)
    own_dy = own_dy[:, :DATA].reshape(-1, LANES)
    msg_x, own_dy = together((msg_x, own_dy))
    msg_dy = from_members([own_dy] * GROUPS)

    rows_x, hidden, by_gate, by_up, *parts = expert_forward(
        index, perm, perm_t, msg_x, w_gate, w_up, w_down
    )
    swapped = from_members(parts)

    rows_dy, d_gate, d_up, router_part = expert_backward(
        index, perm, msg_dy, side, w_down, hidden, by_gate, by_up, rows_x
    )
    g_down, s_down = grad_down(hidden, rows_dy)
    g_gate, g_up, s_gate, s_up = grad_in(rows_x, d_gate, d_up)
    lane = iota((SIDE, LANES), 1)
    squares = jnp.where(lane == 0, s_gate, jnp.where(lane == 1, s_up, s_down))
    high = lax.reduce_precision(squares, 8, 7)
    squares = jnp.where(iota((SIDE, LANES), 0) == 0, high, squares - high)
    swapped, squares = together((swapped, squares))
    expert_out = sum(p.astype(F32) for p in swapped).astype(BF).reshape(experts, DATA, LANES)
    squares = jnp.broadcast_to(squares.astype(BF)[None], (experts, SIDE, LANES))
    back = to_experts(
        jnp.concatenate([expert_out, router_part.astype(BF), squares], axis=1), experts
    )
    sums = jnp.sum(back[:, DATA:].astype(F32), axis=0)
    mixed = mix(index, aux, tokens, back.reshape(-1, LANES), experts)
    sums = sum(from_members([sums] * GROUPS))
    total_count = experts * width * w_gate.shape[1] * groups
    inverse = 1.0 / jnp.sqrt((sums[SIDE] + sums[SIDE + 1]) / total_count + EPSILON)
    columns = to_all_experts(sums[:SIDE], experts)

    down_update = learned_step(g_down, w_down, inverse[2:3], spread_down, scalars)
    gate_update = learned_step(g_gate, w_gate, inverse[0:1], spread_in, scalars)
    up_update = learned_step(g_up, w_up, inverse[1:2], spread_in, scalars)
    columns, up_update = together((columns, up_update))
    router_update = router_step(net, columns, router_across).T
    return (mixed, gate_update[None], up_update[None], down_update[None], router_update)


def solution(mesh):
    torus = Mesh(
        mesh.devices.reshape(8, 4, 2, mesh.shape["mp"]), ("expert_0", "expert_1", "expert_2", "mp")
    )
    placed = (
        P(EXPERT, None),
        P(EXPERT, None),
        P(EXPERT, None),
        P(),
        P(EXPERT, None, "mp"),
        P(EXPERT, None, "mp"),
        P(EXPERT, "mp", None),
        P(),
        P(),
        P(),
    )
    return jax.shard_map(
        on_device,
        mesh=torus,
        in_specs=placed,
        out_specs=(
            P(EXPERT, "mp"),
            P(EXPERT, None, "mp"),
            P(EXPERT, None, "mp"),
            P(EXPERT, "mp", None),
            P(),
        ),
        check_vma=False,
    )
```

profile of v0, /device:TPU:1, one launch (start us, length us, event | category | flops | bytes accessed | tf_op | source)
XLA Modules:
  0.0 196.2 jit_solution(1452583425159555880)
XLA Ops:
  0.7 1.0 copy-done.3
  2.4 2.9 %send_x.1 = bf16[1536,128]{1,0:T(8,128)(2,1)} custom-call(s32[2]{0:T(128)S(1)} %pad_add_fusion.mp.at, bf16[256,1024]{1,0:T(8,128)(2,1)S(1)} %copy-done.3, s32[2,256]{1,0:T(2,128)S(1)} %bitcast.55), custom_call_target="tpu_custom_call" | custom-call | tf_op jit(solution)/shard_map/send_x/pallas_call | solution.py:120
  5.3 13.0 %all-to-all-start = ((bf16[64,24,128]{2,1,0:T(8,128)(2,1)}), bf16[64,24,128]{2,1,0:T(8,128)(2,1)S(1)}, u32[]{:S(2)}, u32[]{:S(2)}) async-start(bf16[64,24,128]{2,1,0:T(8,128)(2,1)} %bitcast.4), calls=%async_computation | async-start | bytes 786432 | tf_op jit(solution)/shard_map/all_to_all | solution.py:558
  19.9 4.8 %send_dy.1 = (bf16[2048,128]{1,0:T(8,128)(2,1)}, f32[256,128]{1,0:T(8,128)S(1)}) custom-call(s32[2]{0:T(128)S(1)} %pad_add_fusion.mp.at, bf16[256,1024]{1,0:T(8,128)(2,1)S(1)} %copy-done.4, bf16[256,1024]{1,0:T(8,128)(2,1)S(1)} %copy-done.6, s32[2,256]{1,0:T(2,128)S(1)} %bitcast.56, bf16[64,1024]{1,0:T(8,128)(2,1)S(1)} %bitcast.53), custom_call_target="tpu_custom_call" | custom-call | tf_op jit(solution)/shard_map/send_dy/pallas_call | solution.py:142
  24.7 8.7 %all-to-all-done = bf16[64,24,128]{2,1,0:T(8,128)(2,1)S(1)} async-done(((bf16[64,24,128]{2,1,0:T(8,128)(2,1)}), bf16[64,24,128]{2,1,0:T(8,128)(2,1)S(1)}, u32[]{:S(2)}, u32[]{:S(2)}) %all-to-all-start) | async-done | bytes 393248 | tf_op jit(solution)/shard_map/all_to_all | solution.py:558
  33.4 5.6 %all-to-all-start.1 = ((bf16[64,32,128]{2,1,0:T(8,128)(2,1)}), bf16[64,32,128]{2,1,0:T(8,128)(2,1)S(1)}, u32[]{:S(2)}, u32[]{:S(2)}) async-start(bf16[64,32,128]{2,1,0:T(8,128)(2,1)} %bitcast.6), calls=%async_computation.1 | async-start | bytes 1048576 | tf_op jit(solution)/shard_map/all_to_all | solution.py:558
  39.0 1.4 collective-permute-start
  40.4 2.6 %collective-permute-start.1 = (bf16[1536,128]{1,0:T(8,128)(2,1)S(1)}, bf16[1536,128]{1,0:T(8,128)(2,1)S(1)}, u32[]{:S(2)}, u32[]{:S(2)}) collective-permute-start(bf16[1536,128]{1,0:T(8,128)(2,1)S(1)} %bitcast.47), channel_id=1, source_target_pairs={{0,2},{1,3},{2,0},{3,1},{4,6},{5,7},{6,4},{7,5},{8,10},{9,11},{10,... | collective-permute-start | bytes 1179656 | tf_op jit(solution)/shard_map/ppermute | solution.py:563
  43.0 1.1 collective-permute-start.2
  44.1 12.7 %all-to-all-done.1 = bf16[64,32,128]{2,1,0:T(8,128)(2,1)S(1)} async-done(((bf16[64,32,128]{2,1,0:T(8,128)(2,1)}), bf16[64,32,128]{2,1,0:T(8,128)(2,1)S(1)}, u32[]{:S(2)}, u32[]{:S(2)}) %all-to-all-start.1) | async-done | bytes 524320 | tf_op jit(solution)/shard_map/all_to_all | solution.py:558
  56.8 3.4 %collective-permute-done.1.m2 = bf16[1536,128]{1,0:T(8,128)(2,1)S(1)} collective-permute-done((bf16[1536,128]{1,0:T(8,128)(2,1)S(1)}, bf16[1536,128]{1,0:T(8,128)(2,1)S(1)}, u32[]{:S(2)}, u32[]{:S(2)}) %collective-permute-start.1) | collective-permute-done | bytes 393248 | tf_op jit(solution)/shard_map/ppermute | solution.py:563
  60.2 1.0 collective-permute-start.6
  61.2 2.9 %collective-permute-start.7 = (bf16[1536,128]{1,0:T(8,128)(2,1)S(1)}, bf16[1536,128]{1,0:T(8,128)(2,1)S(1)}, u32[]{:S(2)}, u32[]{:S(2)}) collective-permute-start(bf16[1536,128]{1,0:T(8,128)(2,1)S(1)} %bitcast.43), channel_id=1, source_target_pairs={{0,2},{1,3},{2,0},{3,1},{4,6},{5,7},{6,4},{7,5},{8,10},{9,11},{10,... | collective-permute-start | bytes 1179656 | tf_op jit(solution)/shard_map/ppermute | solution.py:563
  64.6 14.0 %expert_forward.1 = (bf16[768,1024]{1,0:T(8,128)(2,1)}, bf16[768,896]{1,0:T(8,128)(2,1)S(1)}, f32[768,896]{1,0:T(8,128)}, f32[768,896]{1,0:T(8,128)}, bf16[1536,...) custom-call(s32[2]{0:T(128)S(1)} %pad_add_fusion.mp.at, ...), custom_call_target="tpu_custom_call" | custom-call | tf_op jit(solution)/shard_map/expert_forward/pallas_call | solution.py:227
  78.6 1.1 copy-done.1
  79.7 1.2 collective-permute-start.3
  81.2 2.1 %collective-permute-start.5 = (bf16[1536,128]{1,0:T(8,128)(2,1)S(1)}, bf16[1536,128]{1,0:T(8,128)(2,1)S(1)}, u32[]{:S(2)}, u32[]{:S(2)}) collective-permute-start(bf16[1536,128]{1,0:T(8,128)(2,1)S(1)} %get-tuple-element.46), channel_id=1, source_target_pairs={{0,3},{1,0},{2,1},{3,2},{4,7},{5,4},{6,5},{7,6},{8,11},{9,8},{10,9... | collective-permute-start | bytes 1179656 | tf_op jit(solution)/shard_map/ppermute | solution.py:563
  83.4 9.2 %expert_backward.1 = (bf16[768,1024]{1,0:T(8,128)(2,1)}, bf16[768,896]{1,0:T(8,128)(2,1)S(1)}, bf16[768,896]{1,0:T(8,128)(2,1)S(1)}, f32[64,8,128]{2,1,0:T(8,128)S(1)}) custom-call(s32[2]{0:T(128)S(1)} %pad_add_fusion.mp.at, bf16[384,384]{1,0:T(8,128)(2,1)S(1)} %get-tuple-element.74.perm, bf16[1536,128]{1,0:T(8,128)(2,1)S(1)} %bitcast.45, ...), custom_call_target="tpu_custom_call" | custom-call | tf_op jit(solution)/shard_map/expert_backward/pallas_call | solution.py:297
  92.7 1.5 copy-done.5
  94.2 4.3 %grad_down.1 = (f32[896,1024]{1,0:T(8,128)}, f32[1,128]{1,0:T(1,128)S(1)}) custom-call(bf16[768,896]{1,0:T(8,128)(2,1)S(1)} %copy-done.2, bf16[768,1024]{1,0:T(8,128)(2,1)S(1)} %copy-done.5), custom_call_target="tpu_custom_call" | custom-call | tf_op jit(solution)/shard_map/grad_down/pallas_call | solution.py:383
  98.5 6.6 %grad_in.1 = (f32[1024,896]{1,0:T(8,128)}, f32[1024,896]{1,0:T(8,128)}, f32[1,128]{1,0:T(1,128)S(1)}, f32[1,128]{1,0:T(1,128)S(1)}) custom-call(bf16[768,1024]{1,0:T(8,128)(2,1)S(1)} %copy-done, bf16[768,896]{1,0:T(8,128)(2,1)S(1)} %get-tuple-element.52.d_gate, bf16[768,896]{1,0:T(8,128)(2,1)S(1)} %get-tuple-element.53.d_up), custom_call_target="tpu_custom_call" | custom-call | tf_op jit(solution)/shard_map/grad_in/pallas_call | solution.py:355
  105.5 0.9 pad_maximum_fusion
  106.4 12.3 %all-to-all-start.2 = ((bf16[64,40,128]{2,1,0:T(8,128)(2,1)}), bf16[64,40,128]{2,1,0:T(8,128)(2,1)S(1)}, u32[]{:S(2)}, u32[]{:S(2)}) async-start(bf16[64,40,128]{2,1,0:T(8,128)(2,1)} %pad_maximum_fusion), calls=%async_computation.2 | async-start | bytes 1310720 | tf_op jit(solution)/shard_map/all_to_all | solution.py:558
  119.4 19.7 %all-to-all-done.2 = bf16[64,40,128]{2,1,0:T(8,128)(2,1)S(1)} async-done(((bf16[64,40,128]{2,1,0:T(8,128)(2,1)}), bf16[64,40,128]{2,1,0:T(8,128)(2,1)S(1)}, u32[]{:S(2)}, u32[]{:S(2)}) %all-to-all-start.2) | async-done | bytes 655392 | tf_op jit(solution)/shard_map/all_to_all | solution.py:558
  139.2 2.4 %collective-permute-start.10 = (f32[16,128]{1,0:T(8,128)S(1)}, f32[16,128]{1,0:T(8,128)S(1)}, u32[]{:S(2)}, u32[]{:S(2)}) collective-permute-start(f32[16,128]{1,0:T(8,128)S(1)} %convert_reduce_fusion), channel_id=1, source_target_pairs={{0,2},{1,3},{2,0},{3,1},{4,6},{5,7},{6,4},{7,5},{8,10},{9,11},{10,... | collective-permute-start | bytes 24584 | tf_op jit(solution)/shard_map/ppermute | solution.py:563
  141.9 1.1 collective-permute-start.9
  146.3 7.6 %all-to-all-start.3 = ((f32[64,8,128]{2,1,0:T(8,128)}), f32[64,8,128]{2,1,0:T(8,128)S(1)}, u32[]{:S(2)}, u32[]{:S(2)}) async-start(f32[64,8,128]{2,1,0:T(8,128)} %broadcast_in_dim.74), calls=%async_computation.3 | async-start | bytes 524288 | tf_op jit(solution)/shard_map/all_to_all | solution.py:573
  154.0 2.9 %mix.1 = bf16[256,256]{1,0:T(8,128)(2,1)} custom-call(s32[2]{0:T(128)S(1)} %pad_add_fusion.mp.at, f32[256,128]{1,0:T(8,128)S(1)} %get-tuple-element.37.aux, bf16[256,1024]{1,0:T(8,128)(2,1)S(1)} %copy-done.4, bf16[2560,128]{1,0:T(8,128)(2,1)S(1)} %bitcast.41), custom_call_target="tpu_custom_call" | custom-call | tf_op jit(solution)/shard_map/mix/pallas_call | solution.py:513
  157.5 11.8 %learned_step.4 = bf16[1024,896]{1,0:T(8,128)(2,1)} custom-call(f32[3,16]{1,0:T(4,128)S(1)} %maximum_maximum_fusion.scalars, f32[1]{0:T(128)} %bitcast.25.rms, bf16[512,256]{1,0:T(8,128)(2,1)S(1)} %spread_weights.2.spread, f32[1024,896]{1,0:T(8,128)} %get-tuple-element.65.grad, bf16[1024,896]{1,0:T(8,128)(2,1)} %bitcast.64), custom_call_target="tpu_custom_call" | custom-call | tf_op jit(solution)/shard_map/learned_step/pallas_call | solution.py:477
  169.3 11.7 %learned_step.3 = bf16[1024,896]{1,0:T(8,128)(2,1)} custom-call(f32[3,16]{1,0:T(4,128)S(1)} %maximum_maximum_fusion.scalars, f32[1]{0:T(128)} %bitcast.19.rms, bf16[512,256]{1,0:T(8,128)(2,1)S(1)} %spread_weights.2.spread, f32[1024,896]{1,0:T(8,128)} %get-tuple-element.64.grad, bf16[1024,896]{1,0:T(8,128)(2,1)} %bitcast.66), custom_call_target="tpu_custom_call" | custom-call | tf_op jit(solution)/shard_map/learned_step/pallas_call | solution.py:477
  181.1 11.6 %learned_step.5 = bf16[896,1024]{1,0:T(8,128)(2,1)} custom-call(f32[3,16]{1,0:T(4,128)S(1)} %maximum_maximum_fusion.scalars, f32[1]{0:T(128)} %bitcast.27.rms, bf16[512,256]{1,0:T(8,128)(2,1)S(1)} %spread_weights.3.spread, f32[896,1024]{1,0:T(8,128)} %get-tuple-element.67.grad, bf16[896,1024]{1,0:T(8,128)(2,1)} %bitcast.62), custom_call_target="tpu_custom_call" | custom-call | tf_op jit(solution)/shard_map/learned_step/pallas_call | solution.py:477
  192.7 3.5 %router_step.1 = bf16[64,1024]{1,0:T(8,128)(2,1)} custom-call(f32[5,16]{1,0:T(8,128)S(1)} %pad_maximum_fusion.1.net, f32[64,8,128]{2,1,0:T(8,128)S(1)} %all-to-all-done.3.columns, bf16[64,1024]{1,0:T(8,128)(2,1)S(1)} %bitcast.54), custom_call_target="tpu_custom_call" | custom-call | tf_op jit(solution)/shard_map/router_step/pallas_call | solution.py:543
  (70 shorter events, 8.5 us)
Async XLA Ops:
  0.7 1.0 copy-start.3
  1.8 0.7 copy-start.9
  2.4 15.9 %copy-start.4 = (bf16[256,1024]{1,0:T(8,128)(2,1)S(1)}, bf16[256,1024]{1,0:T(8,128)(2,1)}, u32[]{:S(2)}) copy-start(bf16[256,1024]{1,0:T(8,128)(2,1)} %tok_cols.3) | copy-start | bytes 1572868
  2.4 15.9 %copy-start.6 = (bf16[256,1024]{1,0:T(8,128)(2,1)S(1)}, bf16[256,1024]{1,0:T(8,128)(2,1)}, u32[]{:S(2)}) copy-start(bf16[256,1024]{1,0:T(8,128)(2,1)} %cot_cols.1) | copy-start | bytes 1572868
  5.3 28.1 %all-to-all-start = ((bf16[64,24,128]{2,1,0:T(8,128)(2,1)}), bf16[64,24,128]{2,1,0:T(8,128)(2,1)S(1)}, u32[]{:S(2)}, u32[]{:S(2)}) async-start(bf16[64,24,128]{2,1,0:T(8,128)(2,1)} %bitcast.4), calls=%async_computation | async-start | bytes 786432 | tf_op jit(solution)/shard_map/all_to_all | solution.py:558
  18.3 0.9 copy-start.7
  19.3 0.7 copy-start.10
  33.4 23.3 %all-to-all-start.1 = ((bf16[64,32,128]{2,1,0:T(8,128)(2,1)}), bf16[64,32,128]{2,1,0:T(8,128)(2,1)S(1)}, u32[]{:S(2)}, u32[]{:S(2)}) async-start(bf16[64,32,128]{2,1,0:T(8,128)(2,1)} %bitcast.6), calls=%async_computation.1 | async-start | bytes 1048576 | tf_op jit(solution)/shard_map/all_to_all | solution.py:558
  39.0 17.8 %collective-permute-start = (bf16[1536,128]{1,0:T(8,128)(2,1)S(1)}, bf16[1536,128]{1,0:T(8,128)(2,1)S(1)}, u32[]{:S(2)}, u32[]{:S(2)}) collective-permute-start(bf16[1536,128]{1,0:T(8,128)(2,1)S(1)} %bitcast.46), channel_id=1, source_target_pairs={{0,1},{1,2},{2,3},{3,0},{4,5},{5,6},{6,7},{7,4},{8,9},{9,10},{10,1... | collective-permute-start | bytes 1179656 | tf_op jit(solution)/shard_map/ppermute | solution.py:563
  40.4 19.8 %collective-permute-start.1 = (bf16[1536,128]{1,0:T(8,128)(2,1)S(1)}, bf16[1536,128]{1,0:T(8,128)(2,1)S(1)}, u32[]{:S(2)}, u32[]{:S(2)}) collective-permute-start(bf16[1536,128]{1,0:T(8,128)(2,1)S(1)} %bitcast.47), channel_id=1, source_target_pairs={{0,2},{1,3},{2,0},{3,1},{4,6},{5,7},{6,4},{7,5},{8,10},{9,11},{10,... | collective-permute-start | bytes 1179656 | tf_op jit(solution)/shard_map/ppermute | solution.py:563
  43.0 17.2 %collective-permute-start.2 = (bf16[1536,128]{1,0:T(8,128)(2,1)S(1)}, bf16[1536,128]{1,0:T(8,128)(2,1)S(1)}, u32[]{:S(2)}, u32[]{:S(2)}) collective-permute-start(bf16[1536,128]{1,0:T(8,128)(2,1)S(1)} %bitcast.48), channel_id=1, source_target_pairs={{0,3},{1,0},{2,1},{3,2},{4,7},{5,4},{6,5},{7,6},{8,11},{9,8},{10,9... | collective-permute-start | bytes 1179656 | tf_op jit(solution)/shard_map/ppermute | solution.py:563
  60.2 21.0 %collective-permute-start.6 = (bf16[1536,128]{1,0:T(8,128)(2,1)S(1)}, bf16[1536,128]{1,0:T(8,128)(2,1)S(1)}, u32[]{:S(2)}, u32[]{:S(2)}) collective-permute-start(bf16[1536,128]{1,0:T(8,128)(2,1)S(1)} %bitcast.42), channel_id=1, source_target_pairs={{0,1},{1,2},{2,3},{3,0},{4,5},{5,6},{6,7},{7,4},{8,9},{9,10},{10,1... | collective-permute-start | bytes 1179656 | tf_op jit(solution)/shard_map/ppermute | solution.py:563
  61.2 22.2 %collective-permute-start.7 = (bf16[1536,128]{1,0:T(8,128)(2,1)S(1)}, bf16[1536,128]{1,0:T(8,128)(2,1)S(1)}, u32[]{:S(2)}, u32[]{:S(2)}) collective-permute-start(bf16[1536,128]{1,0:T(8,128)(2,1)S(1)} %bitcast.43), channel_id=1, source_target_pairs={{0,2},{1,3},{2,0},{3,1},{4,6},{5,7},{6,4},{7,5},{8,10},{9,11},{10,... | collective-permute-start | bytes 1179656 | tf_op jit(solution)/shard_map/ppermute | solution.py:563
  64.2 19.2 %collective-permute-start.8 = (bf16[1536,128]{1,0:T(8,128)(2,1)S(1)}, bf16[1536,128]{1,0:T(8,128)(2,1)S(1)}, u32[]{:S(2)}, u32[]{:S(2)}) collective-permute-start(bf16[1536,128]{1,0:T(8,128)(2,1)S(1)} %bitcast.44), channel_id=1, source_target_pairs={{0,3},{1,0},{2,1},{3,2},{4,7},{5,4},{6,5},{7,6},{8,11},{9,8},{10,9... | collective-permute-start | bytes 1179656 | tf_op jit(solution)/shard_map/ppermute | solution.py:563
  78.6 1.1 copy-start.1
  79.7 25.5 %collective-permute-start.3 = (bf16[1536,128]{1,0:T(8,128)(2,1)S(1)}, bf16[1536,128]{1,0:T(8,128)(2,1)S(1)}, u32[]{:S(2)}, u32[]{:S(2)}) collective-permute-start(bf16[1536,128]{1,0:T(8,128)(2,1)S(1)} %get-tuple-element.44), channel_id=1, source_target_pairs={{0,1},{1,2},{2,3},{3,0},{4,5},{5,6},{6,7},{7,4},{8,9},{9,10},{10,1... | collective-permute-start | bytes 1179656 | tf_op jit(solution)/shard_map/ppermute | solution.py:563
  80.9 24.3 %collective-permute-start.4 = (bf16[1536,128]{1,0:T(8,128)(2,1)S(1)}, bf16[1536,128]{1,0:T(8,128)(2,1)S(1)}, u32[]{:S(2)}, u32[]{:S(2)}) collective-permute-start(bf16[1536,128]{1,0:T(8,128)(2,1)S(1)} %get-tuple-element.45), channel_id=1, source_target_pairs={{0,2},{1,3},{2,0},{3,1},{4,6},{5,7},{6,4},{7,5},{8,10},{9,11},{10,... | collective-permute-start | bytes 1179656 | tf_op jit(solution)/shard_map/ppermute | solution.py:563
  81.2 24.0 %collective-permute-start.5 = (bf16[1536,128]{1,0:T(8,128)(2,1)S(1)}, bf16[1536,128]{1,0:T(8,128)(2,1)S(1)}, u32[]{:S(2)}, u32[]{:S(2)}) collective-permute-start(bf16[1536,128]{1,0:T(8,128)(2,1)S(1)} %get-tuple-element.46), channel_id=1, source_target_pairs={{0,3},{1,0},{2,1},{3,2},{4,7},{5,4},{6,5},{7,6},{8,11},{9,8},{10,9... | collective-permute-start | bytes 1179656 | tf_op jit(solution)/shard_map/ppermute | solution.py:563
  83.4 9.2 %copy-start.2 = (bf16[768,896]{1,0:T(8,128)(2,1)S(1)}, bf16[768,896]{1,0:T(8,128)(2,1)}, u32[]{:S(2)}) copy-start(bf16[768,896]{1,0:T(8,128)(2,1)} %copy-done.1) | copy-start | bytes 4128772
  92.6 5.8 %copy-start = (bf16[768,1024]{1,0:T(8,128)(2,1)S(1)}, bf16[768,1024]{1,0:T(8,128)(2,1)}, u32[]{:S(2)}) copy-start(bf16[768,1024]{1,0:T(8,128)(2,1)} %get-tuple-element.47.rows_x) | copy-start | bytes 4718596
  92.6 1.5 copy-start.5
  105.5 13.3 %copy-start.11 = (f32[3,16]{1,0:T(4,128)S(1)}, f32[3,16]{1,0:T(4,128)}, u32[]{:S(2)}) copy-start(f32[3,16]{1,0:T(4,128)} %param.17) | copy-start | bytes 580
  105.5 13.3 %copy-start.12 = (f32[16]{0:T(128)S(1)}, f32[16]{0:T(128)}, u32[]{:S(2)}) copy-start(f32[16]{0:T(128)} %param.19) | copy-start | bytes 196
  105.5 13.3 %copy-start.13 = (f32[16]{0:T(128)S(1)}, f32[16]{0:T(128)}, u32[]{:S(2)}) copy-start(f32[16]{0:T(128)} %param.18) | copy-start | bytes 196
  106.4 32.7 %all-to-all-start.2 = ((bf16[64,40,128]{2,1,0:T(8,128)(2,1)}), bf16[64,40,128]{2,1,0:T(8,128)(2,1)S(1)}, u32[]{:S(2)}, u32[]{:S(2)}) async-start(bf16[64,40,128]{2,1,0:T(8,128)(2,1)} %pad_maximum_fusion), calls=%async_computation.2 | async-start | bytes 1310720 | tf_op jit(solution)/shard_map/all_to_all | solution.py:558
  139.2 5.5 %collective-permute-start.10 = (f32[16,128]{1,0:T(8,128)S(1)}, f32[16,128]{1,0:T(8,128)S(1)}, u32[]{:S(2)}, u32[]{:S(2)}) collective-permute-start(f32[16,128]{1,0:T(8,128)S(1)} %convert_reduce_fusion), channel_id=1, source_target_pairs={{0,2},{1,3},{2,0},{3,1},{4,6},{5,7},{6,4},{7,5},{8,10},{9,11},{10,... | collective-permute-start | bytes 24584 | tf_op jit(solution)/shard_map/ppermute | solution.py:563
  141.5 3.1 %collective-permute-start.11 = (f32[16,128]{1,0:T(8,128)S(1)}, f32[16,128]{1,0:T(8,128)S(1)}, u32[]{:S(2)}, u32[]{:S(2)}) collective-permute-start(f32[16,128]{1,0:T(8,128)S(1)} %convert_reduce_fusion), channel_id=1, source_target_pairs={{0,3},{1,0},{2,1},{3,2},{4,7},{5,4},{6,5},{7,6},{8,11},{9,8},{10,9... | collective-permute-start | bytes 24584 | tf_op jit(solution)/shard_map/ppermute | solution.py:563
  141.9 3.7 %collective-permute-start.9 = (f32[16,128]{1,0:T(8,128)S(1)}, f32[16,128]{1,0:T(8,128)S(1)}, u32[]{:S(2)}, u32[]{:S(2)}) collective-permute-start(f32[16,128]{1,0:T(8,128)S(1)} %convert_reduce_fusion), channel_id=1, source_target_pairs={{0,1},{1,2},{2,3},{3,0},{4,5},{5,6},{6,7},{7,4},{8,9},{9,10},{10,1... | collective-permute-start | bytes 24584 | tf_op jit(solution)/shard_map/ppermute | solution.py:563
  146.3 46.4 %all-to-all-start.3 = ((f32[64,8,128]{2,1,0:T(8,128)}), f32[64,8,128]{2,1,0:T(8,128)S(1)}, u32[]{:S(2)}, u32[]{:S(2)}) async-start(f32[64,8,128]{2,1,0:T(8,128)} %broadcast_in_dim.74), calls=%async_computation.3 | async-start | bytes 524288 | tf_op jit(solution)/shard_map/all_to_all | solution.py:573
  181.1 11.6 %copy-start.8 = (bf16[1024,64]{0,1:T(8,128)(2,1)S(1)}, bf16[1024,64]{0,1:T(8,128)(2,1)}, u32[]{:S(2)}) copy-start(bf16[1024,64]{0,1:T(8,128)(2,1)} %param.13) | copy-start | bytes 393220
where the time goes:
time: 197 us; the launch traced here: 196 us
  Pallas kernels  84.1 us (43%)
  starting transfers between devices  55.1 us (28%)
  waiting for transfers between devices  45.4 us (23%)
  local copies, waits for them, and re-layouts  8.35 us (4%)
  other arithmetic  2.29 us (1%)
    all_to_all x3, waiting for transfers between devices, to_experts(): return lax.all_to_all(sent, EXPERT, 0, 0, tiled=True)  41 us
    pallas_call x3, Pallas kernels, learned_step(): pl.pallas_call(functools.partial(step_kernel, rows=128), grid=(height //...  35.2 us
    all_to_all x3, starting transfers between devices, to_experts(): return lax.all_to_all(sent, EXPERT, 0, 0, tiled=True)  30.9 us
    ppermute x12, starting transfers between devices, from_members(): lax.ppermute(pieces[k], 'mp', [(i, (i + k) % GROUPS) for i in range(GROUP...  16.7 us
    pallas_call x1, Pallas kernels, expert_forward(): pl.pallas_call(forward_kernel, grid_spec=pltpu.PrefetchScalarGridSpec(num...  14 us
    pallas_call x1, Pallas kernels, expert_backward(): pl.pallas_call(backward_kernel, grid_spec=pltpu.PrefetchScalarGridSpec(nu...  9.22 us
    all_to_all x1, starting transfers between devices, to_all_experts(): lax.all_to_all(jnp.broadcast_to(x[None], (peers, *x.shape)), EXPERT, 0, 0...  7.57 us
    pallas_call x1, Pallas kernels, grad_in(): pl.pallas_call(grad_in_kernel, grid=(width // chunk,), in_specs=[pl.Block...  6.64 us
  transfers between devices with their start and end apart: 16, of which 5 were waited for; matrix products, arithmetic and copies ran while one was open for 1% of the time, Pallas kernels for 40%

commit v1 on v0

--- a/solution.py
+++ b/solution.py
@@ -167,14 +167,18 @@
 
 
 def unpack_rows(perm, mp, messages, to, blocks):
-    for b in range(blocks):
-        at = slice(b * 2 * BLOCK, (b + 1) * 2 * BLOCK)
-        both = dot(perm, jnp.concatenate([m[at, :] for m in messages], axis=1)).astype(BF)
+    def body(b, carry):
+        at = pl.ds(pl.multiple_of(b * 2 * BLOCK, 2 * BLOCK), 2 * BLOCK)
+        rows = pl.ds(pl.multiple_of(b * BLOCK, BLOCK), BLOCK)
+        both = dot(perm[...], jnp.concatenate([m[at, :] for m in messages], axis=1)).astype(BF)
         for h in range(2):
             for k in range(GROUPS):
-                to[b * BLOCK : (b + 1) * BLOCK, pl.ds(column_of(mp, -k, h), LANES)] = both[
+                to[rows, pl.ds(column_of(mp, -k, h), LANES)] = both[
                     h * BLOCK : (h + 1) * BLOCK, k * LANES : (k + 1) * LANES
                 ]
+        return carry
+
+    lax.fori_loop(0, blocks, body, 0)
 
 
 def forward_kernel(mp, perm, perm_t, m0, m1, m2, m3, gate, up, down, *refs):
@@ -186,7 +190,7 @@
 
     @pl.when(step == 0)
     def _():
-        unpack_rows(perm[...], mp[0], (m0, m1, m2, m3), rows_x, blocks)
+        unpack_rows(perm, mp[0], (m0, m1, m2, m3), rows_x, blocks)
 
     acts = dot(rows_x[...], jnp.concatenate([gate[...], up[...]], axis=1))
     act_gate = acts[:, :LANES]
@@ -200,22 +204,23 @@
     @pl.when(step == pl.num_programs(0) - 1)
     def _():
         outs[...] = dot(hidden[...], down[...]).astype(BF)
-        for b in range(blocks):
+
+        def body(b, carry):
+            at = pl.ds(pl.multiple_of(b * 2 * BLOCK, 2 * BLOCK), 2 * BLOCK)
+            rows = pl.ds(pl.multiple_of(b * BLOCK, BLOCK), BLOCK)
             halves = [
                 jnp.concatenate(
-                    [
-                        outs[b * BLOCK : (b + 1) * BLOCK, pl.ds(column_of(mp[0], k, h), LANES)]
-                        for k in range(GROUPS)
-                    ],
+                    [outs[rows, pl.ds(column_of(mp[0], k, h), LANES)] for k in range(GROUPS)],
                     axis=1,
                 )
                 for h in range(2)
             ]
             packed = dot(perm_t[...], jnp.concatenate(halves, axis=0)).astype(BF)
             for k in range(GROUPS):
-                parts[k][b * 2 * BLOCK : (b + 1) * 2 * BLOCK, :] = packed[
-                    :, k * LANES : (k + 1) * LANES
-                ]
+                parts[k][at, :] = packed[:, k * LANES : (k + 1) * LANES]
+            return carry
+
+        lax.fori_loop(0, blocks, body, 0)
 
 
 def expert_forward(mp_index, perm, perm_t, messages, w_gate, w_up, w_down):
@@ -248,17 +253,12 @@
     )(mp_index, perm, perm_t, *messages, w_gate, w_up, w_down)
 
 
-def backward_kernel(
-    at, perm, m0, m1, m2, m3, side, down, hidden, by_gate, by_up, rows_x,
-    rows_dy, d_gate, d_up, router, total,
-):
-    part = rows_dy.shape[0]
-    experts = router.shape[0]
-    unpack_rows(perm[...], at[0], (m0, m1, m2, m3), rows_dy, part // BLOCK)
-    grad_hidden = dot(rows_dy[...], down[...], ((1,), (1,)))
-    d_gate[...] = (grad_hidden * by_gate[...]).astype(BF)
-    d_up[...] = (grad_hidden * by_up[...]).astype(BF)
-    q = row_sum(hidden[...].astype(F32) * grad_hidden)
+HALVES = 2
+CHUNKS = 4
+
+
+def logit_terms(q, side, expert, experts):
+    part = q.shape[0]
     row = iota((part, part // CAP), 0)
     first = iota((part, part // CAP), 1) * CAP
     source = ((row >= first) & (row < first + CAP)).astype(F32)
@@ -269,130 +269,116 @@
     own = q * (values[0] + values[1])
     other = q * (values[2] + values[3])
     lane = iota((part, experts), 1)
-    grads = jnp.where(lane == at[1], own, 0.0)
-    grads = jnp.where(lane == values[4].astype(jnp.int32), other, grads)
-    both = dot(jnp.concatenate(two_parts(grads), axis=1), rows_x[...], ((0,), (0,)))
-    grad = both[:experts] + both[experts:]
-
-    @pl.when(pl.program_id(0) == 0)
+    grads = jnp.where(lane == expert, own, 0.0)
+    return jnp.where(lane == values[4].astype(jnp.int32), other, grads)
+
+
+def backward_kernel(
+    at, perm, m0, m1, m2, m3, side, down, hidden, by_gate, by_up, rows_x,
+    g_gate, g_up, g_down, squares, router,
+    rows_dy, d_gate, d_up, x_across, hidden_across, router_total, sums,
+):
+    step = pl.program_id(0)
+    part = rows_x.shape[0]
+    experts = router.shape[0]
+
+    @pl.when(step < HALVES)
     def _():
-        total[...] = grad
-
-    @pl.when(pl.program_id(0) == pl.num_programs(0) - 1)
+        at_rows = pl.ds(pl.multiple_of(step * part, part), part)
+        dy = rows_dy.at[at_rows]
+        unpack_rows(perm, at[0], (m0, m1, m2, m3), dy, part // BLOCK)
+        grad_hidden = dot(dy[...], down[...], ((1,), (1,)))
+        d_gate[at_rows, :] = (grad_hidden * by_gate[...]).astype(BF)
+        d_up[at_rows, :] = (grad_hidden * by_up[...]).astype(BF)
+        x_across[:, at_rows] = rows_x[...].T
+        hidden_across[:, at_rows] = hidden[...].T
+        q = row_sum(hidden[...].astype(F32) * grad_hidden)
+        grads = logit_terms(q, side, at[1], experts)
+        both = dot(jnp.concatenate(two_parts(grads), axis=1), rows_x[...], ((0,), (0,)))
+        grad = both[:experts] + both[experts:]
+
+        @pl.when(step == 0)
+        def _():
+            router_total[...] = grad
+            sums[...] = jnp.zeros_like(sums)
+
+        @pl.when(step == HALVES - 1)
+        def _():
+            whole = router_total[...] + grad
+            for j in range(router.shape[1]):
+                router[:, j, :] = whole[:, j * LANES : (j + 1) * LANES]
+
+    @pl.when(step >= HALVES)
     def _():
-        whole = total[...] + grad
-        for j in range(router.shape[1]):
-            router[:, j, :] = whole[:, j * LANES : (j + 1) * LANES]
+        chunk = step - HALVES
+        outs = (
+            (g_gate, x_across, d_gate),
+            (g_up, x_across, d_up),
+            (g_down, hidden_across, rows_dy),
+        )
+        for i, (out, left, right) in enumerate(outs):
+            n = out.shape[0]
+            grad = dot(left[pl.ds(pl.multiple_of(chunk * n, n), n), :], right[...])
+            out[...] = grad
+            total = jnp.sum(grad * grad, axis=0, keepdims=True)
+            sums[i : i + 1, : grad.shape[1]] += total
+
+    @pl.when(step == pl.num_programs(0) - 1)
+    def _():
+        lane = iota(squares.shape, 1)
+        values = jnp.zeros(squares.shape, F32)
+        for i in range(3):
+            values = jnp.where(lane == i, row_sum(sums[i : i + 1, :]), values)
+        squares[...] = values
 
 
 def expert_backward(index, perm, messages, side, w_down, hidden, by_gate, by_up, rows_x):
     sent, _ = messages[0].shape
-    steps = 2
     rows = sent // 2
-    part = rows // steps
+    part = rows // HALVES
     experts = rows // CAP
     ff, width = w_down.shape
+    first = lambda i: jnp.minimum(i, HALVES - 1)
+    then = lambda i: jnp.maximum(i - HALVES, 0)
     whole = lambda *shape: pl.BlockSpec(shape, lambda i, at: (0,) * len(shape))
-    row = lambda n, m: pl.BlockSpec((n, m), lambda i, at: (i, 0))
+    row = lambda n, m: pl.BlockSpec((n, m), lambda i, at: (first(i), 0))
+    out = lambda n, m: pl.BlockSpec((n // CHUNKS, m), lambda i, at: (then(i), 0))
     return pl.pallas_call(
         backward_kernel,
         grid_spec=pltpu.PrefetchScalarGridSpec(
             num_scalar_prefetch=1,
-            grid=(steps,),
+            grid=(HALVES + CHUNKS,),
             in_specs=[whole(*perm.shape)]
-            + [row(sent // steps, LANES)] * GROUPS
-            + [pl.BlockSpec((SIDE, part // CAP, LANES), lambda i, at: (0, i, 0))]
+            + [row(sent // HALVES, LANES)] * GROUPS
+            + [pl.BlockSpec((SIDE, part // CAP, LANES), lambda i, at: (0, first(i), 0))]
             + [whole(ff, width), row(part, ff), row(part, ff), row(part, ff), row(part, width)],
             out_specs=[
-                row(part, width),
-                row(part, ff),
-                row(part, ff),
+                out(width, ff),
+                out(width, ff),
+                out(ff, width),
+                whole(1, LANES),
                 whole(experts, width // LANES, LANES),
             ],
-            scratch_shapes=[pltpu.VMEM((experts, width), F32)],
+            scratch_shapes=[
+                pltpu.VMEM((rows, width), BF),
+                pltpu.VMEM((rows, ff), BF),
+                pltpu.VMEM((rows, ff), BF),
+                pltpu.VMEM((width, rows), BF),
+                pltpu.VMEM((ff, rows), BF),
+                pltpu.VMEM((experts, width), F32),
+                pltpu.VMEM((SIDE, width), F32),
+            ],
         ),
         out_shape=[
-            jax.ShapeDtypeStruct((rows, width), BF),
-            jax.ShapeDtypeStruct((rows, ff), BF),
-            jax.ShapeDtypeStruct((rows, ff), BF),
+            jax.ShapeDtypeStruct((width, ff), F32),
+            jax.ShapeDtypeStruct((width, ff), F32),
+            jax.ShapeDtypeStruct((ff, width), F32),
+            jax.ShapeDtypeStruct((1, LANES), F32),
             jax.ShapeDtypeStruct((experts, width // LANES, LANES), F32),
         ],
         compiler_params=params(),
         name="expert_backward",
     )(index, perm, *messages, side, w_down, hidden, by_gate, by_up, rows_x)
-
-
-def add_squares(total, grad, to):
-    step = pl.program_id(0)
-    squares = jnp.sum(grad * grad, axis=0, keepdims=True)
-
-    @pl.when(step == 0)
-    def _():
-        total[...] = squares
-
-    @pl.when(step > 0)
-    def _():
-        total[...] += squares
-
-    @pl.when(step == pl.num_programs(0) - 1)
-    def _():
-        to[...] = jnp.broadcast_to(row_sum(total[...]), to.shape)
-
-
-def grad_in_kernel(rows_x, d_gate, d_up, g_gate, g_up, s_gate, s_up, t_gate, t_up):
-    across = rows_x[...].T
-    for d, g, s, t in ((d_gate, g_gate, s_gate, t_gate), (d_up, g_up, s_up, t_up)):
-        grad = dot(across, d[...])
-        g[...] = grad
-        add_squares(t, grad, s)
-
-
-def grad_in(rows_x, d_gate, d_up):
-    rows, width = rows_x.shape
-    ff = d_gate.shape[1]
-    chunk = 256
-    whole = lambda *shape: pl.BlockSpec(shape, lambda i: (0,) * len(shape))
-    return pl.pallas_call(
-        grad_in_kernel,
-        grid=(width // chunk,),
-        in_specs=[pl.BlockSpec((rows, chunk), lambda i: (0, i)), whole(rows, ff), whole(rows, ff)],
-        out_specs=[pl.BlockSpec((chunk, ff), lambda i: (i, 0))] * 2 + [whole(1, LANES)] * 2,
-        out_shape=[jax.ShapeDtypeStruct((width, ff), F32)] * 2
-        + [jax.ShapeDtypeStruct((1, LANES), F32)] * 2,
-        scratch_shapes=[pltpu.VMEM((1, ff), F32)] * 2,
-        compiler_params=params(),
-        name="grad_in",
-    )(rows_x, d_gate, d_up)
-
-
-def grad_down_kernel(hidden, rows_dy, g_down, s_down, across, total):
-    @pl.when(pl.program_id(0) == 0)
-    def _():
-        across[...] = hidden[...].T
-
-    grad = dot(across[...], rows_dy[...])
-    g_down[...] = grad
-    add_squares(total, grad, s_down)
-
-
-def grad_down(hidden, rows_dy):
-    rows, ff = hidden.shape
-    width = rows_dy.shape[1]
-    chunk = 256
-    whole = lambda *shape: pl.BlockSpec(shape, lambda i: (0,) * len(shape))
-    return pl.pallas_call(
-        grad_down_kernel,
-        grid=(width // chunk,),
-        in_specs=[whole(rows, ff), pl.BlockSpec((rows, chunk), lambda i: (0, i))],
-        out_specs=[pl.BlockSpec((ff, chunk), lambda i: (0, i)), whole(1, LANES)],
-        out_shape=[
-            jax.ShapeDtypeStruct((ff, width), F32),
-            jax.ShapeDtypeStruct((1, LANES), F32),
-        ],
-        scratch_shapes=[pltpu.VMEM((ff, rows), BF), pltpu.VMEM((1, chunk), F32)],
-        compiler_params=params(),
-        name="grad_down",
-    )(hidden, rows_dy)
 
 
 NET_ROWS = 32
@@ -475,7 +461,7 @@
     block = 128
     tile = pl.BlockSpec((block, width), lambda i: (i, 0))
     return pl.pallas_call(
-        functools.partial(step_kernel, rows=128),
+        functools.partial(step_kernel, rows=128 if width % 256 == 0 else 64),
         grid=(height // block,),
         in_specs=[
             pl.BlockSpec(memory_space=pltpu.SMEM),
@@ -607,14 +593,17 @@
     router_across = router_weight.T
 
     routes_across = routes.T
-    sent_x = send_x(tokens, routes_across, experts, index)
+    sent_x = send_x(in_hbm(tokens), routes_across, experts, index)
     own_x = to_experts(sent_x, experts).reshape(-1, LANES)
-    sent_dy, aux = send_dy(tokens, cotangent, routes_across, router_across, index)
+    sent_dy, aux = send_dy(in_hbm(tokens), in_hbm(cotangent), routes_across, router_across, index)
+    sent_dy, perm, perm_t, spread_in, spread_down, scalars, net = together(
+        (sent_dy, perm, perm_t, spread_in, spread_down, scalars, net)
+    )
     msg_x = from_members([own_x] * GROUPS)
     own_dy = to_experts(sent_dy, experts)
     side = own_dy[:, DATA:].transpose(1, 0, 2)
     own_dy = own_dy[:, :DATA].reshape(-1, LANES)
-    msg_x, own_dy = together((msg_x, own_dy))
+    perm, own_dy = together((perm, own_dy))
     msg_dy = from_members([own_dy] * GROUPS)
 
     rows_x, hidden, by_gate, by_up, *parts = expert_forward(
@@ -622,30 +611,30 @@
     )
     swapped = from_members(parts)
 
-    rows_dy, d_gate, d_up, router_part = expert_backward(
+    g_gate, g_up, g_down, squares, router_part = expert_backward(
         index, perm, msg_dy, side, w_down, hidden, by_gate, by_up, rows_x
     )
-    g_down, s_down = grad_down(hidden, rows_dy)
-    g_gate, g_up, s_gate, s_up = grad_in(rows_x, d_gate, d_up)
-    lane = iota((SIDE, LANES), 1)
-    squares = jnp.where(lane == 0, s_gate, jnp.where(lane == 1, s_up, s_down))
-    high = lax.reduce_precision(squares, 8, 7)
-    squares = jnp.where(iota((SIDE, LANES), 0) == 0, high, squares - high)
     swapped, squares = together((swapped, squares))
+    squares = sum(from_members([squares] * GROUPS))
     expert_out = sum(p.astype(F32) for p in swapped).astype(BF).reshape(experts, DATA, LANES)
-    squares = jnp.broadcast_to(squares.astype(BF)[None], (experts, SIDE, LANES))
-    back = to_experts(
-        jnp.concatenate([expert_out, router_part.astype(BF), squares], axis=1), experts
-    )
-    sums = jnp.sum(back[:, DATA:].astype(F32), axis=0)
-    mixed = mix(index, aux, tokens, back.reshape(-1, LANES), experts)
-    sums = sum(from_members([sums] * GROUPS))
+    message = jnp.concatenate([expert_out, router_part.astype(BF)], axis=1)
+    message, squares = together((message, squares))
+    squares = jnp.sum(to_all_experts(squares, experts), axis=0)
     total_count = experts * width * w_gate.shape[1] * groups
-    inverse = 1.0 / jnp.sqrt((sums[SIDE] + sums[SIDE + 1]) / total_count + EPSILON)
-    columns = to_all_experts(sums[:SIDE], experts)
-
+    inverse = 1.0 / jnp.sqrt(squares[0] / total_count + EPSILON)
+
+    message, inverse = together((message, inverse))
+    back = to_experts(message, experts)
     down_update = learned_step(g_down, w_down, inverse[2:3], spread_down, scalars)
     gate_update = learned_step(g_gate, w_gate, inverse[0:1], spread_in, scalars)
+    back, gate_update, down_update = together((back, gate_update, down_update))
+    sums = jnp.sum(back[:, DATA:].astype(F32), axis=0)
+    sums = from_members([sums] * GROUPS)
+    mixed = mix(index, aux, tokens, back.reshape(-1, LANES), experts)
+    mixed, sums = together((mixed, sums))
+    sums = sum(sums)
+    sums, g_up = together((sums, g_up))
+    columns = to_all_experts(sums, experts)
     up_update = learned_step(g_up, w_up, inverse[1:2], spread_in, scalars)
     columns, up_update = together((columns, up_update))
     router_update = router_step(net, columns, router_across).T

time: 197 us -> 195 us (0.990)
  blocking collectives: 0 us -> 23 us
  waiting for transfers between devices: 45.4 us -> 23.7 us
  starting transfers between devices: 55.1 us -> 51.1 us
  local copies, waits for them, and re-layouts: 8.35 us -> 6.33 us
  Pallas kernels: 84.1 us -> 86.1 us
    all_to_all x0 -> x1, blocking collectives: none -> 23 us  [to_all_experts(): lax.all_to_all(jnp.broadcast_to(x[None], (peers, *x.shape)), EXPERT, 0, 0...]
    all_to_all x3, waiting for transfers between devices: 41 us -> 19.6 us  [to_experts(): return lax.all_to_all(sent, EXPERT, 0, 0, tiled=True)]
    pallas_call x5 -> x3, Pallas kernels: 46.1 us -> 38.1 us  [learned_step(): pl.pallas_call(functools.partial(step_kernel, rows=128 if width % 256 ==...]
    all_to_all x3, starting transfers between devices: 30.9 us -> 23.7 us  [to_experts(): return lax.all_to_all(sent, EXPERT, 0, 0, tiled=True)]
    pallas_call x1, Pallas kernels: 9.22 us -> 16 us  [expert_backward(): pl.pallas_call(backward_kernel, grid_spec=pltpu.PrefetchScalarGridSpec(nu...]
    all_to_all x1, starting transfers between devices: 7.57 us -> 12.1 us  [to_all_experts(): lax.all_to_all(jnp.broadcast_to(x[None], (peers, *x.shape)), EXPERT, 0, 0...]
    unnamed x29 -> x17, local copies, waits for them, and re-layouts: 5.96 us -> 2.13 us
    ppermute x12 -> x15, starting transfers between devices: 16.7 us -> 15.4 us  [from_members(): lax.ppermute(pieces[k], 'mp', [(i, (i + k) % GROUPS) for i in range(GROUP...]
  transfers between devices with their start and end apart: 16 -> 19, of which waited for: 5 -> 6; matrix products, arithmetic and copies ran while one was open for 1% -> 3% of each run, Pallas kernels for 40% -> 41%
where the time goes in v1:
time: 195 us; the launch traced here: 194 us
  Pallas kernels  86.1 us (44%)
  starting transfers between devices  51.1 us (26%)
  waiting for transfers between devices  23.7 us (12%)
  blocking collectives  23 us (12%)
  local copies, waits for them, and re-layouts  6.33 us (3%)
  other arithmetic  2.95 us (2%)
    pallas_call x3, Pallas kernels, learned_step(): pl.pallas_call(functools.partial(step_kernel, rows=128 if width % 256 ==...  38.1 us
    all_to_all x3, starting transfers between devices, to_experts(): return lax.all_to_all(sent, EXPERT, 0, 0, tiled=True)  23.7 us
    all_to_all x1, blocking collectives, to_all_experts(): lax.all_to_all(jnp.broadcast_to(x[None], (peers, *x.shape)), EXPERT, 0, 0...  23 us
    all_to_all x3, waiting for transfers between devices, to_experts(): return lax.all_to_all(sent, EXPERT, 0, 0, tiled=True)  19.6 us
    pallas_call x1, Pallas kernels, expert_backward(): pl.pallas_call(backward_kernel, grid_spec=pltpu.PrefetchScalarGridSpec(nu...  16 us
    pallas_call x1, Pallas kernels, expert_forward(): pl.pallas_call(forward_kernel, grid_spec=pltpu.PrefetchScalarGridSpec(num...  15.4 us
    ppermute x15, starting transfers between devices, from_members(): lax.ppermute(pieces[k], 'mp', [(i, (i + k) % GROUPS) for i in range(GROUP...  15.4 us
    all_to_all x1, starting transfers between devices, to_all_experts(): lax.all_to_all(jnp.broadcast_to(x[None], (peers, *x.shape)), EXPERT, 0, 0...  12.1 us
  transfers between devices with their start and end apart: 19, of which 6 were waited for; matrix products, arithmetic and copies ran while one was open for 3% of the time, Pallas kernels for 41%

profile of v1, /device:TPU:1, one launch (start us, length us, event | category | flops | bytes accessed | tf_op | source)
XLA Modules:
  0.0 194.1 jit_solution(12967413069020574474)
XLA Ops:
  1.4 3.8 %send_x.1 = bf16[1536,128]{1,0:T(8,128)(2,1)} custom-call(s32[2]{0:T(128)S(1)} %pad_add_fusion.mp.at, bf16[256,1024]{1,0:T(8,128)(2,1)} %tok_cols.3, s32[2,256]{1,0:T(2,128)S(1)} %bitcast.51), custom_call_target="tpu_custom_call" | custom-call | tf_op jit(solution)/shard_map/send_x/pallas_call | solution.py:120
  5.2 13.1 %all-to-all-start.1 = ((bf16[64,24,128]{2,1,0:T(8,128)(2,1)}), bf16[64,24,128]{2,1,0:T(8,128)(2,1)S(1)}, u32[]{:S(2)}, u32[]{:S(2)}) async-start(bf16[64,24,128]{2,1,0:T(8,128)(2,1)} %bitcast.15), calls=%async_computation.1 | async-start | bytes 786432 | tf_op jit(solution)/shard_map/all_to_all | solution.py:544
  18.3 0.8 multiply_bitcast_fusion
  20.7 0.7 pad.7.clone
  21.4 5.9 %send_dy.1 = (bf16[2048,128]{1,0:T(8,128)(2,1)}, f32[256,128]{1,0:T(8,128)S(1)}) custom-call(s32[2]{0:T(128)S(1)} %pad_add_fusion.mp.at, bf16[256,1024]{1,0:T(8,128)(2,1)} %tok_cols.3, bf16[256,1024]{1,0:T(8,128)(2,1)} %cot_cols.1, s32[2,256]{1,0:T(2,128)S(1)} %bitcast.52, bf16[64,1024]{1,0:T(8,128)(2,1)S(1)} %bitcast.49), custom_call_target="tpu_custom_call" | custom-call | tf_op jit(solution)/shard_map/send_dy/pallas_call | solution.py:142
  27.6 5.8 %all-to-all-done.1 = bf16[64,24,128]{2,1,0:T(8,128)(2,1)S(1)} async-done(((bf16[64,24,128]{2,1,0:T(8,128)(2,1)}), bf16[64,24,128]{2,1,0:T(8,128)(2,1)S(1)}, u32[]{:S(2)}, u32[]{:S(2)}) %all-to-all-start.1) | async-done | bytes 393248 | tf_op jit(solution)/shard_map/all_to_all | solution.py:544
  33.4 5.8 %all-to-all-start = ((bf16[64,32,128]{2,1,0:T(8,128)(2,1)}), bf16[64,32,128]{2,1,0:T(8,128)(2,1)}, u32[]{:S(2)}, u32[]{:S(2)}) async-start(bf16[64,32,128]{2,1,0:T(8,128)(2,1)} %bitcast.13), calls=%async_computation | async-start | bytes 1048576 | tf_op jit(solution)/shard_map/all_to_all | solution.py:544
  39.2 2.8 %collective-permute-start.2 = (bf16[1536,128]{1,0:T(8,128)(2,1)S(1)}, bf16[1536,128]{1,0:T(8,128)(2,1)S(1)}, u32[]{:S(2)}, u32[]{:S(2)}) collective-permute-start(bf16[1536,128]{1,0:T(8,128)(2,1)S(1)} %bitcast.42), channel_id=1, source_target_pairs={{0,3},{1,0},{2,1},{3,2},{4,7},{5,4},{6,5},{7,6},{8,11},{9,8},{10,9... | collective-permute-start | bytes 1179656 | tf_op jit(solution)/shard_map/ppermute | solution.py:549
  43.0 13.8 %all-to-all-done = bf16[64,32,128]{2,1,0:T(8,128)(2,1)} async-done(((bf16[64,32,128]{2,1,0:T(8,128)(2,1)}), bf16[64,32,128]{2,1,0:T(8,128)(2,1)}, u32[]{:S(2)}, u32[]{:S(2)}) %all-to-all-start) | async-done | bytes 524320 | tf_op jit(solution)/shard_map/all_to_all | solution.py:544
  56.8 1.0 slice.39
  57.8 2.8 %collective-permute-start.8 = (bf16[1536,128]{1,0:T(8,128)(2,1)S(1)}, bf16[1536,128]{1,0:T(8,128)(2,1)S(1)}, u32[]{:S(2)}, u32[]{:S(2)}) collective-permute-start(bf16[1536,128]{1,0:T(8,128)(2,1)S(1)} %bitcast.38), channel_id=1, source_target_pairs={{0,3},{1,0},{2,1},{3,2},{4,7},{5,4},{6,5},{7,6},{8,11},{9,8},{10,9... | collective-permute-start | bytes 1179656 | tf_op jit(solution)/shard_map/ppermute | solution.py:549
  61.7 1.2 collective-permute-done.m1
  63.0 15.4 %expert_forward.1 = (bf16[768,1024]{1,0:T(8,128)(2,1)}, bf16[768,896]{1,0:T(8,128)(2,1)S(1)}, f32[768,896]{1,0:T(8,128)}, f32[768,896]{1,0:T(8,128)}, bf16[1536,...) custom-call(s32[2]{0:T(128)S(1)} %pad_add_fusion.mp.at, ...), custom_call_target="tpu_custom_call" | custom-call | tf_op jit(solution)/shard_map/expert_forward/pallas_call | solution.py:232
  78.8 1.6 collective-permute-start.4
  80.3 0.9 collective-permute-start.5
  81.2 0.9 slice.40
  82.2 1.4 copy-done.1
  83.6 16.0 %expert_backward.1 = (f32[1024,896]{1,0:T(8,128)}, f32[1024,896]{1,0:T(8,128)}, f32[896,1024]{1,0:T(8,128)}, f32[1,128]{1,0:T(1,128)S(1)}, f32[64,8,128]{2,1,0:T(8,128)S(1)}) custom-call(s32[2]{0:T(128)S(1)} %pad_add_fusion.mp.at, bf16[384,384]{1,0:T(8,128)(2,1)S(1)} %get-tuple-element.54.perm, bf16[1536,128]{1,0:T(8,128)(2,1)S(1)} %bitcast.41, ...), custom_call_target="tpu_custom_call" | custom-call | tf_op jit(solution)/shard_map/expert_backward/pallas_call | solution.py:346
  99.7 2.1 %collective-permute-start.11 = (f32[1,128]{1,0:T(1,128)S(1)}, f32[1,128]{1,0:T(1,128)S(1)}, u32[]{:S(2)}, u32[]{:S(2)}) collective-permute-start(f32[1,128]{1,0:T(1,128)S(1)} %get-tuple-element.71), channel_id=1, source_target_pairs={{0,3},{1,0},{2,1},{3,2},{4,7},{5,4},{6,5},{7,6},{8,11},{9,8},{10,9... | collective-permute-start | bytes 1544 | tf_op jit(solution)/shard_map/ppermute | solution.py:549
  102.1 0.7 collective-permute-start.9
  103.1 0.9 pad_maximum_fusion
  103.9 1.8 collective-permute-done.10
  105.8 23.0 %all_to_all.25 = f32[64,1,128]{2,1,0:T(1,128)S(1)} all-to-all(f32[64,1,128]{2,1,0:T(1,128)S(1)} %broadcast_in_dim.41), channel_id=1, replica_groups=mesh['expert_0'=8,'expert_1'=4,'expert_2'=2,'mp'=4] {'expert_0','expert_..., dimensions={0} | all-to-all | bytes 65536 | tf_op jit(solution)/shard_map/all_to_all | solution.py:559
  128.8 4.8 %all-to-all-start.3 = ((bf16[64,32,128]{2,1,0:T(8,128)(2,1)}), bf16[64,32,128]{2,1,0:T(8,128)(2,1)S(1)}, u32[]{:S(2)}, u32[]{:S(2)}) async-start(bf16[64,32,128]{2,1,0:T(8,128)(2,1)} %pad_maximum_fusion), calls=%async_computation.3 | async-start | bytes 1048576 | tf_op jit(solution)/shard_map/all_to_all | solution.py:544
  134.2 11.6 %learned_step.4 = bf16[896,1024]{1,0:T(8,128)(2,1)} custom-call(f32[3,16]{1,0:T(4,128)S(1)} %maximum_maximum_fusion.scalars, f32[1]{0:T(128)} %get-tuple-element.104.rms, bf16[512,256]{1,0:T(8,128)(2,1)S(1)} %spread_weights.3.spread, f32[896,1024]{1,0:T(8,128)} %get-tuple-element.80.grad, bf16[896,1024]{1,0:T(8,128)(2,1)} %bitcast.55), custom_call_target="tpu_custom_call" | custom-call | tf_op jit(solution)/shard_map/learned_step/pallas_call | solution.py:463
  145.8 13.2 %learned_step.3 = bf16[1024,896]{1,0:T(8,128)(2,1)} custom-call(f32[3,16]{1,0:T(4,128)S(1)} %maximum_maximum_fusion.scalars, f32[1]{0:T(128)} %get-tuple-element.105.rms, bf16[512,256]{1,0:T(8,128)(2,1)S(1)} %spread_weights.2.spread, f32[1024,896]{1,0:T(8,128)} %get-tuple-element.78.grad, bf16[1024,896]{1,0:T(8,128)(2,1)} %bitcast.57), custom_call_target="tpu_custom_call" | custom-call | tf_op jit(solution)/shard_map/learned_step/pallas_call | solution.py:463
  159.8 1.1 collective-permute-start.13
  160.8 2.6 %mix.1 = bf16[256,256]{1,0:T(8,128)(2,1)} custom-call(s32[2]{0:T(128)S(1)} %pad_add_fusion.mp.at, f32[256,128]{1,0:T(8,128)S(1)} %get-tuple-element.50.aux, bf16[256,1024]{1,0:T(8,128)(2,1)S(1)} %copy-done, bf16[2048,128]{1,0:T(8,128)(2,1)S(1)} %bitcast.37), custom_call_target="tpu_custom_call" | custom-call | tf_op jit(solution)/shard_map/mix/pallas_call | solution.py:499
  163.7 0.8 collective-permute-done.12
  165.2 12.1 %all-to-all-start.4 = ((f32[64,8,128]{2,1,0:T(8,128)}), f32[64,8,128]{2,1,0:T(8,128)S(1)}, u32[]{:S(2)}, u32[]{:S(2)}) async-start(f32[64,8,128]{2,1,0:T(8,128)} %broadcast_in_dim.43), calls=%async_computation.4 | async-start | bytes 524288 | tf_op jit(solution)/shard_map/all_to_all | solution.py:559
  177.3 13.3 %learned_step.5 = bf16[1024,896]{1,0:T(8,128)(2,1)} custom-call(f32[3,16]{1,0:T(4,128)S(1)} %maximum_maximum_fusion.scalars, f32[1]{0:T(128)} %get-tuple-element.103.rms, bf16[512,256]{1,0:T(8,128)(2,1)S(1)} %spread_weights.2.spread, f32[1024,896]{1,0:T(8,128)} %get-tuple-element.90.grad, bf16[1024,896]{1,0:T(8,128)(2,1)} %bitcast.59), custom_call_target="tpu_custom_call" | custom-call | tf_op jit(solution)/shard_map/learned_step/pallas_call | solution.py:463
  190.6 3.5 %router_step.1 = bf16[64,1024]{1,0:T(8,128)(2,1)} custom-call(f32[5,16]{1,0:T(8,128)S(1)} %pad_maximum_fusion.1.net, f32[64,8,128]{2,1,0:T(8,128)S(1)} %all-to-all-done.4.columns, bf16[64,1024]{1,0:T(8,128)(2,1)S(1)} %bitcast.50), custom_call_target="tpu_custom_call" | custom-call | tf_op jit(solution)/shard_map/router_step/pallas_call | solution.py:529
  (61 shorter events, 8.0 us)
Async XLA Ops:
  0.6 20.8 %copy-start.2 = (bf16[1024,64]{0,1:T(8,128)(2,1)S(1)}, bf16[1024,64]{0,1:T(8,128)(2,1)}, u32[]{:S(2)}) copy-start(bf16[1024,64]{0,1:T(8,128)(2,1)} %param.13) | copy-start | bytes 393220
  0.7 0.7 copy-start.3
  1.4 18.7 %copy-start.6 = (f32[16]{0:T(128)S(1)}, f32[16]{0:T(128)}, u32[]{:S(2)}) copy-start(f32[16]{0:T(128)} %param.19) | copy-start | bytes 196
  1.4 18.7 %copy-start.7 = (f32[16]{0:T(128)S(1)}, f32[16]{0:T(128)}, u32[]{:S(2)}) copy-start(f32[16]{0:T(128)} %param.18) | copy-start | bytes 196
  1.4 20.0 %copy-start.4 = (s32[256,2]{0,1:T(2,128)S(1)}, s32[256,2]{0,1:T(2,128)}, u32[]{:S(2)}) copy-start(s32[256,2]{0,1:T(2,128)} %param.12) | copy-start | bytes 6148
  5.2 22.1 %copy-start.5 = (f32[3,16]{1,0:T(4,128)S(1)}, f32[3,16]{1,0:T(4,128)}, u32[]{:S(2)}) copy-start(f32[3,16]{1,0:T(4,128)} %param.17) | copy-start | bytes 580
  5.2 28.2 %all-to-all-start.1 = ((bf16[64,24,128]{2,1,0:T(8,128)(2,1)}), bf16[64,24,128]{2,1,0:T(8,128)(2,1)S(1)}, u32[]{:S(2)}, u32[]{:S(2)}) async-start(bf16[64,24,128]{2,1,0:T(8,128)(2,1)} %bitcast.15), calls=%async_computation.1 | async-start | bytes 786432 | tf_op jit(solution)/shard_map/all_to_all | solution.py:544
  33.4 23.4 %all-to-all-start = ((bf16[64,32,128]{2,1,0:T(8,128)(2,1)}), bf16[64,32,128]{2,1,0:T(8,128)(2,1)}, u32[]{:S(2)}, u32[]{:S(2)}) async-start(bf16[64,32,128]{2,1,0:T(8,128)(2,1)} %bitcast.13), calls=%async_computation | async-start | bytes 1048576 | tf_op jit(solution)/shard_map/all_to_all | solution.py:544
  39.2 21.8 %collective-permute-start.2 = (bf16[1536,128]{1,0:T(8,128)(2,1)S(1)}, bf16[1536,128]{1,0:T(8,128)(2,1)S(1)}, u32[]{:S(2)}, u32[]{:S(2)}) collective-permute-start(bf16[1536,128]{1,0:T(8,128)(2,1)S(1)} %bitcast.42), channel_id=1, source_target_pairs={{0,3},{1,0},{2,1},{3,2},{4,7},{5,4},{6,5},{7,6},{8,11},{9,8},{10,9... | collective-permute-start | bytes 1179656 | tf_op jit(solution)/shard_map/ppermute | solution.py:549
  42.0 19.7 %collective-permute-start.1 = (bf16[1536,128]{1,0:T(8,128)(2,1)S(1)}, bf16[1536,128]{1,0:T(8,128)(2,1)S(1)}, u32[]{:S(2)}, u32[]{:S(2)}) collective-permute-start(bf16[1536,128]{1,0:T(8,128)(2,1)S(1)} %bitcast.43), channel_id=1, source_target_pairs={{0,2},{1,3},{2,0},{3,1},{4,6},{5,7},{6,4},{7,5},{8,10},{9,11},{10,... | collective-permute-start | bytes 1179656 | tf_op jit(solution)/shard_map/ppermute | solution.py:549
  42.3 20.6 %collective-permute-start = (bf16[1536,128]{1,0:T(8,128)(2,1)S(1)}, bf16[1536,128]{1,0:T(8,128)(2,1)S(1)}, u32[]{:S(2)}, u32[]{:S(2)}) collective-permute-start(bf16[1536,128]{1,0:T(8,128)(2,1)S(1)} %bitcast.44), channel_id=1, source_target_pairs={{0,1},{1,2},{2,3},{3,0},{4,5},{5,6},{6,7},{7,4},{8,9},{9,10},{10,1... | collective-permute-start | bytes 1179656 | tf_op jit(solution)/shard_map/ppermute | solution.py:549
  57.8 22.5 %collective-permute-start.8 = (bf16[1536,128]{1,0:T(8,128)(2,1)S(1)}, bf16[1536,128]{1,0:T(8,128)(2,1)S(1)}, u32[]{:S(2)}, u32[]{:S(2)}) collective-permute-start(bf16[1536,128]{1,0:T(8,128)(2,1)S(1)} %bitcast.38), channel_id=1, source_target_pairs={{0,3},{1,0},{2,1},{3,2},{4,7},{5,4},{6,5},{7,6},{8,11},{9,8},{10,9... | collective-permute-start | bytes 1179656 | tf_op jit(solution)/shard_map/ppermute | solution.py:549
  60.7 21.5 %collective-permute-start.7 = (bf16[1536,128]{1,0:T(8,128)(2,1)S(1)}, bf16[1536,128]{1,0:T(8,128)(2,1)S(1)}, u32[]{:S(2)}, u32[]{:S(2)}) collective-permute-start(bf16[1536,128]{1,0:T(8,128)(2,1)S(1)} %bitcast.39), channel_id=1, source_target_pairs={{0,2},{1,3},{2,0},{3,1},{4,6},{5,7},{6,4},{7,5},{8,10},{9,11},{10,... | collective-permute-start | bytes 1179656 | tf_op jit(solution)/shard_map/ppermute | solution.py:549
  61.0 21.2 %collective-permute-start.6 = (bf16[1536,128]{1,0:T(8,128)(2,1)S(1)}, bf16[1536,128]{1,0:T(8,128)(2,1)S(1)}, u32[]{:S(2)}, u32[]{:S(2)}) collective-permute-start(bf16[1536,128]{1,0:T(8,128)(2,1)S(1)} %bitcast.40), channel_id=1, source_target_pairs={{0,1},{1,2},{2,3},{3,0},{4,5},{5,6},{6,7},{7,4},{8,9},{9,10},{10,1... | collective-permute-start | bytes 1179656 | tf_op jit(solution)/shard_map/ppermute | solution.py:549
  78.4 21.3 %collective-permute-start.3 = (bf16[1536,128]{1,0:T(8,128)(2,1)S(1)}, bf16[1536,128]{1,0:T(8,128)(2,1)S(1)}, u32[]{:S(2)}, u32[]{:S(2)}) collective-permute-start(bf16[1536,128]{1,0:T(8,128)(2,1)S(1)} %get-tuple-element.57), channel_id=1, source_target_pairs={{0,1},{1,2},{2,3},{3,0},{4,5},{5,6},{6,7},{7,4},{8,9},{9,10},{10,1... | collective-permute-start | bytes 1179656 | tf_op jit(solution)/shard_map/ppermute | solution.py:549
  78.8 20.9 %collective-permute-start.4 = (bf16[1536,128]{1,0:T(8,128)(2,1)S(1)}, bf16[1536,128]{1,0:T(8,128)(2,1)S(1)}, u32[]{:S(2)}, u32[]{:S(2)}) collective-permute-start(bf16[1536,128]{1,0:T(8,128)(2,1)S(1)} %get-tuple-element.58), channel_id=1, source_target_pairs={{0,2},{1,3},{2,0},{3,1},{4,6},{5,7},{6,4},{7,5},{8,10},{9,11},{10,... | collective-permute-start | bytes 1179656 | tf_op jit(solution)/shard_map/ppermute | solution.py:549
  80.3 19.4 %collective-permute-start.5 = (bf16[1536,128]{1,0:T(8,128)(2,1)S(1)}, bf16[1536,128]{1,0:T(8,128)(2,1)S(1)}, u32[]{:S(2)}, u32[]{:S(2)}) collective-permute-start(bf16[1536,128]{1,0:T(8,128)(2,1)S(1)} %get-tuple-element.59), channel_id=1, source_target_pairs={{0,3},{1,0},{2,1},{3,2},{4,7},{5,4},{6,5},{7,6},{8,11},{9,8},{10,9... | collective-permute-start | bytes 1179656 | tf_op jit(solution)/shard_map/ppermute | solution.py:549
  82.2 1.4 copy-start.1
  99.7 4.2 %collective-permute-start.11 = (f32[1,128]{1,0:T(1,128)S(1)}, f32[1,128]{1,0:T(1,128)S(1)}, u32[]{:S(2)}, u32[]{:S(2)}) collective-permute-start(f32[1,128]{1,0:T(1,128)S(1)} %get-tuple-element.71), channel_id=1, source_target_pairs={{0,3},{1,0},{2,1},{3,2},{4,7},{5,4},{6,5},{7,6},{8,11},{9,8},{10,9... | collective-permute-start | bytes 1544 | tf_op jit(solution)/shard_map/ppermute | solution.py:549
  101.8 3.9 %collective-permute-start.10 = (f32[1,128]{1,0:T(1,128)S(1)}, f32[1,128]{1,0:T(1,128)S(1)}, u32[]{:S(2)}, u32[]{:S(2)}) collective-permute-start(f32[1,128]{1,0:T(1,128)S(1)} %get-tuple-element.71), channel_id=1, source_target_pairs={{0,2},{1,3},{2,0},{3,1},{4,6},{5,7},{6,4},{7,5},{8,10},{9,11},{10,... | collective-permute-start | bytes 1544 | tf_op jit(solution)/shard_map/ppermute | solution.py:549
  102.1 3.6 %collective-permute-start.9 = (f32[1,128]{1,0:T(1,128)S(1)}, f32[1,128]{1,0:T(1,128)S(1)}, u32[]{:S(2)}, u32[]{:S(2)}) collective-permute-start(f32[1,128]{1,0:T(1,128)S(1)} %get-tuple-element.71), channel_id=1, source_target_pairs={{0,1},{1,2},{2,3},{3,0},{4,5},{5,6},{6,7},{7,4},{8,9},{9,10},{10,1... | collective-permute-start | bytes 1544 | tf_op jit(solution)/shard_map/ppermute | solution.py:549
  128.8 30.2 %all-to-all-start.3 = ((bf16[64,32,128]{2,1,0:T(8,128)(2,1)}), bf16[64,32,128]{2,1,0:T(8,128)(2,1)S(1)}, u32[]{:S(2)}, u32[]{:S(2)}) async-start(bf16[64,32,128]{2,1,0:T(8,128)(2,1)} %pad_maximum_fusion), calls=%async_computation.3 | async-start | bytes 1048576 | tf_op jit(solution)/shard_map/all_to_all | solution.py:544
  145.8 15.0 %copy-start = (bf16[256,1024]{1,0:T(8,128)(2,1)S(1)}, bf16[256,1024]{1,0:T(8,128)(2,1)}, u32[]{:S(2)}) copy-start(bf16[256,1024]{1,0:T(8,128)(2,1)} %tok_cols.3) | copy-start | bytes 1572868
  159.1 4.4 %collective-permute-start.14 = (f32[8,128]{1,0:T(8,128)S(1)}, f32[8,128]{1,0:T(8,128)S(1)}, u32[]{:S(2)}, u32[]{:S(2)}) collective-permute-start(f32[8,128]{1,0:T(8,128)S(1)} %convert_reduce_fusion), channel_id=1, source_target_pairs={{0,3},{1,0},{2,1},{3,2},{4,7},{5,4},{6,5},{7,6},{8,11},{9,8},{10,9... | collective-permute-start | bytes 12296 | tf_op jit(solution)/shard_map/ppermute | solution.py:549
  159.8 4.0 %collective-permute-start.13 = (f32[8,128]{1,0:T(8,128)S(1)}, f32[8,128]{1,0:T(8,128)S(1)}, u32[]{:S(2)}, u32[]{:S(2)}) collective-permute-start(f32[8,128]{1,0:T(8,128)S(1)} %convert_reduce_fusion), channel_id=1, source_target_pairs={{0,2},{1,3},{2,0},{3,1},{4,6},{5,7},{6,4},{7,5},{8,10},{9,11},{10,... | collective-permute-start | bytes 12296 | tf_op jit(solution)/shard_map/ppermute | solution.py:549
  160.8 3.7 %collective-permute-start.12 = (f32[8,128]{1,0:T(8,128)S(1)}, f32[8,128]{1,0:T(8,128)S(1)}, u32[]{:S(2)}, u32[]{:S(2)}) collective-permute-start(f32[8,128]{1,0:T(8,128)S(1)} %convert_reduce_fusion), channel_id=1, source_target_pairs={{0,1},{1,2},{2,3},{3,0},{4,5},{5,6},{6,7},{7,4},{8,9},{9,10},{10,1... | collective-permute-start | bytes 12296 | tf_op jit(solution)/shard_map/ppermute | solution.py:549
  165.2 25.4 %all-to-all-start.4 = ((f32[64,8,128]{2,1,0:T(8,128)}), f32[64,8,128]{2,1,0:T(8,128)S(1)}, u32[]{:S(2)}, u32[]{:S(2)}) async-start(f32[64,8,128]{2,1,0:T(8,128)} %broadcast_in_dim.43), calls=%async_computation.4 | async-start | bytes 524288 | tf_op jit(solution)/shard_map/all_to_all | solution.py:559

commit v2 on v1

--- a/solution.py
+++ b/solution.py
@@ -63,15 +63,24 @@
     return (index == iota((index.shape[0], size), 1)).astype(F32).astype(BF)
 
 
-def send_x_kernel(mp, tok_cols, routes, x_out, *, experts):
-    del mp
-    ids, places, _ = routing(routes, experts)
+def send_x_kernel(at, tok_cols, routes, x_out, *, experts):
+    del at
+    n = tok_cols.shape[0]
     rows = x_out.shape[0]
+    ids = [routes[k : k + 1, :] for k in range(2)]
+    hits = [(ids[k] == iota((experts, n), 0)).astype(F32) for k in range(2)]
+    earlier = (iota((n, n), 0) < iota((n, n), 1)).astype(F32).astype(BF)
+    before = dot((hits[0] + hits[1]).astype(BF), earlier)
+    base = [
+        ids[k] * DATA + jnp.sum(before * hits[k], axis=0, keepdims=True).astype(jnp.int32)
+        for k in range(2)
+    ]
+    row = iota((rows, n), 0)
     total = jnp.zeros((rows, LANES), F32)
     for h in range(2):
-        picks = [one_hot(ids[k] * DATA + places[k] + h * CAP, rows) for k in range(2)]
+        picked = (base[0] + h * CAP == row) | (base[1] + h * CAP == row)
         total = total + dot(
-            picks[0] + picks[1], tok_cols[:, h * LANES : (h + 1) * LANES], ((0,), (0,))
+            picked.astype(F32).astype(BF), tok_cols[:, h * LANES : (h + 1) * LANES]
         )
     x_out[...] = total.astype(BF)
 
@@ -181,7 +190,7 @@
     lax.fori_loop(0, blocks, body, 0)
 
 
-def forward_kernel(mp, perm, perm_t, m0, m1, m2, m3, gate, up, down, *refs):
+def forward_kernel(mp, perm, m0, m1, m2, m3, gate, up, down, *refs):
     rows_x, hidden, by_gate, by_up = refs[:4]
     parts = refs[4 : 4 + GROUPS]
     outs = refs[4 + GROUPS]
@@ -204,26 +213,11 @@
     @pl.when(step == pl.num_programs(0) - 1)
     def _():
         outs[...] = dot(hidden[...], down[...]).astype(BF)
-
-        def body(b, carry):
-            at = pl.ds(pl.multiple_of(b * 2 * BLOCK, 2 * BLOCK), 2 * BLOCK)
-            rows = pl.ds(pl.multiple_of(b * BLOCK, BLOCK), BLOCK)
-            halves = [
-                jnp.concatenate(
-                    [outs[rows, pl.ds(column_of(mp[0], k, h), LANES)] for k in range(GROUPS)],
-                    axis=1,
-                )
-                for h in range(2)
-            ]
-            packed = dot(perm_t[...], jnp.concatenate(halves, axis=0)).astype(BF)
-            for k in range(GROUPS):
-                parts[k][at, :] = packed[:, k * LANES : (k + 1) * LANES]
-            return carry
-
-        lax.fori_loop(0, blocks, body, 0)
-
-
-def expert_forward(mp_index, perm, perm_t, messages, w_gate, w_up, w_down):
+        for k in range(GROUPS):
+            parts[k][...] = outs[:, pl.ds(column_of(mp[0], k, 0), 2 * LANES)]
+
+
+def expert_forward(mp_index, perm, messages, w_gate, w_up, w_down):
     sent, _ = messages[0].shape
     rows = sent // 2
     width, ff = w_gate.shape
@@ -234,11 +228,11 @@
         grid_spec=pltpu.PrefetchScalarGridSpec(
             num_scalar_prefetch=1,
             grid=(ff // LANES,),
-            in_specs=[whole(*perm.shape), whole(*perm.shape)]
+            in_specs=[whole(*perm.shape)]
             + [whole(sent, LANES)] * GROUPS
             + [column(width), column(width), whole(ff, width)],
             out_specs=[whole(rows, width), whole(rows, ff), column(rows), column(rows)]
-            + [whole(sent, LANES)] * GROUPS,
+            + [whole(rows, 2 * LANES)] * GROUPS,
             scratch_shapes=[pltpu.VMEM((rows, width), BF)],
         ),
         out_shape=[
@@ -247,10 +241,30 @@
             jax.ShapeDtypeStruct((rows, ff), F32),
             jax.ShapeDtypeStruct((rows, ff), F32),
         ]
-        + [jax.ShapeDtypeStruct((sent, LANES), BF)] * GROUPS,
+        + [jax.ShapeDtypeStruct((rows, 2 * LANES), BF)] * GROUPS,
         compiler_params=params(),
         name="expert_forward",
-    )(mp_index, perm, perm_t, *messages, w_gate, w_up, w_down)
+    )(mp_index, perm, *messages, w_gate, w_up, w_down)
+
+
+def pack_kernel(perm_t, p0, p1, p2, p3, out):
+    for b in range(p0.shape[0] // BLOCK):
+        rows = slice(b * BLOCK, (b + 1) * BLOCK)
+        total = p0[rows, :].astype(F32)
+        for p in (p1, p2, p3):
+            total = total + p[rows, :].astype(F32)
+        total = total.astype(BF)
+        halves = jnp.concatenate([total[:, :LANES], total[:, LANES:]], axis=0)
+        out[b * 2 * BLOCK : (b + 1) * 2 * BLOCK, :] = dot(perm_t[...], halves).astype(BF)
+
+
+def pack_rows(perm_t, pieces):
+    return pl.pallas_call(
+        pack_kernel,
+        out_shape=jax.ShapeDtypeStruct((2 * pieces[0].shape[0], LANES), BF),
+        compiler_params=params(),
+        name="pack_rows",
+    )(perm_t, *pieces)
 
 
 HALVES = 2
@@ -461,7 +475,7 @@
     block = 128
     tile = pl.BlockSpec((block, width), lambda i: (i, 0))
     return pl.pallas_call(
-        functools.partial(step_kernel, rows=128 if width % 256 == 0 else 64),
+        functools.partial(step_kernel, rows=128),
         grid=(height // block,),
         in_specs=[
             pl.BlockSpec(memory_space=pltpu.SMEM),
@@ -553,10 +567,6 @@
 
 def together(values):
     return lax.optimization_barrier(values)
-
-
-def to_all_experts(x, peers):
-    return lax.all_to_all(jnp.broadcast_to(x[None], (peers, *x.shape)), EXPERT, 0, 0, tiled=True)
 
 
 def on_device(
@@ -607,36 +617,37 @@
     msg_dy = from_members([own_dy] * GROUPS)
 
     rows_x, hidden, by_gate, by_up, *parts = expert_forward(
-        index, perm, perm_t, msg_x, w_gate, w_up, w_down
+        index, perm, msg_x, w_gate, w_up, w_down
     )
     swapped = from_members(parts)
 
     g_gate, g_up, g_down, squares, router_part = expert_backward(
         index, perm, msg_dy, side, w_down, hidden, by_gate, by_up, rows_x
     )
-    swapped, squares = together((swapped, squares))
-    squares = sum(from_members([squares] * GROUPS))
-    expert_out = sum(p.astype(F32) for p in swapped).astype(BF).reshape(experts, DATA, LANES)
-    message = jnp.concatenate([expert_out, router_part.astype(BF)], axis=1)
-    message, squares = together((message, squares))
-    squares = jnp.sum(to_all_experts(squares, experts), axis=0)
+    high = lax.reduce_precision(squares, 8, 7)
+    row = iota((SIDE, LANES), 0)
+    squares = jnp.where(row == 0, high, jnp.where(row == 1, squares - high, 0.0))
+    terms = jnp.concatenate(
+        [router_part, jnp.broadcast_to(squares[None], (experts, SIDE, LANES))], axis=1
+    ).astype(BF)
+    swapped, terms = together((swapped, terms))
+    expert_out = pack_rows(perm_t, swapped).reshape(experts, DATA, LANES)
+    sums = jnp.sum(to_experts(terms, experts).astype(F32), axis=0)
+    sums = sum(from_members([sums] * GROUPS))
     total_count = experts * width * w_gate.shape[1] * groups
-    inverse = 1.0 / jnp.sqrt(squares[0] / total_count + EPSILON)
-
-    message, inverse = together((message, inverse))
-    back = to_experts(message, experts)
+    inverse = 1.0 / jnp.sqrt((sums[SIDE] + sums[SIDE + 1]) / total_count + EPSILON)
+    column = sums[:SIDE]
+    high = lax.reduce_precision(column, 8, 7)
+    column = jnp.concatenate([high, column - high], axis=0).astype(BF)
+    column = jnp.broadcast_to(column[None], (experts, 2 * SIDE, LANES))
+    back = to_experts(jnp.concatenate([expert_out, column], axis=1), experts)
+
     down_update = learned_step(g_down, w_down, inverse[2:3], spread_down, scalars)
     gate_update = learned_step(g_gate, w_gate, inverse[0:1], spread_in, scalars)
-    back, gate_update, down_update = together((back, gate_update, down_update))
-    sums = jnp.sum(back[:, DATA:].astype(F32), axis=0)
-    sums = from_members([sums] * GROUPS)
+    up_update = learned_step(g_up, w_up, inverse[1:2], spread_in, scalars)
+    back, up_update = together((back, up_update))
     mixed = mix(index, aux, tokens, back.reshape(-1, LANES), experts)
-    mixed, sums = together((mixed, sums))
-    sums = sum(sums)
-    sums, g_up = together((sums, g_up))
-    columns = to_all_experts(sums, experts)
-    up_update = learned_step(g_up, w_up, inverse[1:2], spread_in, scalars)
-    columns, up_update = together((columns, up_update))
+    columns = back[:, DATA : DATA + SIDE].astype(F32) + back[:, DATA + SIDE :].astype(F32)
     router_update = router_step(net, columns, router_across).T
     return (mixed, gate_update[None], up_update[None], down_update[None], router_update)
 

time: 195 us -> 178 us (0.913)
  starting transfers between devices: 51.1 us -> 40 us
  Pallas kernels: 86.1 us -> 81.7 us
    all_to_all x1 -> x0, starting transfers between devices: 12.1 us -> none  [to_all_experts(): lax.all_to_all(jnp.broadcast_to(x[None], (peers, *x.shape)), EXPERT, 0, 0...]
    pallas_call x3 -> x4, Pallas kernels: 38.1 us -> 35.7 us  [the longest x3 35.2 us: learned_step(): pl.pallas_call(functools.partial(step_kernel, rows=128), grid=(height //...]
    ppermute x15 -> x12, waiting for transfers between devices: 4.1 us -> 3.52 us  [from_members(): lax.ppermute(pieces[k], 'mp', [(i, (i + k) % GROUPS) for i in range(GROUP...]
    ppermute x15 -> x12, starting transfers between devices: 15.4 us -> 15 us  [from_members(): lax.ppermute(pieces[k], 'mp', [(i, (i + k) % GROUPS) for i in range(GROUP...]
  transfers between devices with their start and end apart: 19 -> 15, of which waited for: 6 -> 4; matrix products, arithmetic and copies ran while one was open for 3% -> 3% of each run, Pallas kernels for 41% -> 41%
where the time goes in v2:
time: 178 us; the launch traced here: 177 us
  Pallas kernels  81.7 us (46%)
  starting transfers between devices  40 us (22%)
  blocking collectives  24.1 us (14%)
  waiting for transfers between devices  21.9 us (12%)
  local copies, waits for them, and re-layouts  5.65 us (3%)
  other arithmetic  2.92 us (2%)
    pallas_call x3, Pallas kernels, learned_step(): pl.pallas_call(functools.partial(step_kernel, rows=128), grid=(height //...  35.2 us
    all_to_all x3, starting transfers between devices, to_experts(): return lax.all_to_all(sent, EXPERT, 0, 0, tiled=True)  25 us
    all_to_all x1, blocking collectives, to_experts(): return lax.all_to_all(sent, EXPERT, 0, 0, tiled=True)  24.1 us
    all_to_all x3, waiting for transfers between devices, to_experts(): return lax.all_to_all(sent, EXPERT, 0, 0, tiled=True)  18.4 us
    pallas_call x1, Pallas kernels, expert_backward(): pl.pallas_call(backward_kernel, grid_spec=pltpu.PrefetchScalarGridSpec(nu...  16 us
    ppermute x12, starting transfers between devices, from_members(): lax.ppermute(pieces[k], 'mp', [(i, (i + k) % GROUPS) for i in range(GROUP...  15 us
    pallas_call x1, Pallas kernels, expert_forward(): pl.pallas_call(forward_kernel, grid_spec=pltpu.PrefetchScalarGridSpec(num...  13.9 us
    pallas_call x1, Pallas kernels, send_dy(): pl.pallas_call(send_dy_kernel, grid_spec=pltpu.PrefetchScalarGridSpec(num...  5.9 us
  transfers between devices with their start and end apart: 15, of which 4 were waited for; matrix products, arithmetic and copies ran while one was open for 3% of the time, Pallas kernels for 41%

profile of v2, /device:TPU:1, one launch (start us, length us, event | category | flops | bytes accessed | tf_op | source)
XLA Modules:
  0.0 177.1 jit_solution(11983240329386264499)
XLA Ops:
  1.4 3.1 %send_x.1 = bf16[1536,128]{1,0:T(8,128)(2,1)} custom-call(s32[2]{0:T(128)S(1)} %pad_add_fusion.mp.at, bf16[256,1024]{1,0:T(8,128)(2,1)} %tok_cols.3, s32[2,256]{1,0:T(2,128)S(1)} %bitcast.57), custom_call_target="tpu_custom_call" | custom-call | tf_op jit(solution)/shard_map/send_x/pallas_call | solution.py:129
  4.5 13.1 %all-to-all-start.1 = ((bf16[64,24,128]{2,1,0:T(8,128)(2,1)}), bf16[64,24,128]{2,1,0:T(8,128)(2,1)S(1)}, u32[]{:S(2)}, u32[]{:S(2)}) async-start(bf16[64,24,128]{2,1,0:T(8,128)(2,1)} %bitcast.15), calls=%async_computation.1 | async-start | bytes 786432 | tf_op jit(solution)/shard_map/all_to_all | solution.py:558
  17.7 0.8 multiply_bitcast_fusion
  19.4 5.9 %send_dy.1 = (bf16[2048,128]{1,0:T(8,128)(2,1)}, f32[256,128]{1,0:T(8,128)S(1)}) custom-call(s32[2]{0:T(128)S(1)} %pad_add_fusion.mp.at, bf16[256,1024]{1,0:T(8,128)(2,1)} %tok_cols.3, bf16[256,1024]{1,0:T(8,128)(2,1)} %cot_cols.1, s32[2,256]{1,0:T(2,128)S(1)} %bitcast.58, bf16[64,1024]{1,0:T(8,128)(2,1)S(1)} %bitcast.55), custom_call_target="tpu_custom_call" | custom-call | tf_op jit(solution)/shard_map/send_dy/pallas_call | solution.py:151
  26.9 5.8 %all-to-all-done.1 = bf16[64,24,128]{2,1,0:T(8,128)(2,1)S(1)} async-done(((bf16[64,24,128]{2,1,0:T(8,128)(2,1)}), bf16[64,24,128]{2,1,0:T(8,128)(2,1)S(1)}, u32[]{:S(2)}, u32[]{:S(2)}) %all-to-all-start.1) | async-done | bytes 393248 | tf_op jit(solution)/shard_map/all_to_all | solution.py:558
  32.7 5.8 %all-to-all-start = ((bf16[64,32,128]{2,1,0:T(8,128)(2,1)}), bf16[64,32,128]{2,1,0:T(8,128)(2,1)}, u32[]{:S(2)}, u32[]{:S(2)}) async-start(bf16[64,32,128]{2,1,0:T(8,128)(2,1)} %bitcast.13), calls=%async_computation | async-start | bytes 1048576 | tf_op jit(solution)/shard_map/all_to_all | solution.py:558
  38.5 1.4 collective-permute-start
  39.9 2.6 %collective-permute-start.1 = (bf16[1536,128]{1,0:T(8,128)(2,1)S(1)}, bf16[1536,128]{1,0:T(8,128)(2,1)S(1)}, u32[]{:S(2)}, u32[]{:S(2)}) collective-permute-start(bf16[1536,128]{1,0:T(8,128)(2,1)S(1)} %bitcast.49), channel_id=1, source_target_pairs={{0,2},{1,3},{2,0},{3,1},{4,6},{5,7},{6,4},{7,5},{8,10},{9,11},{10,... | collective-permute-start | bytes 1179656 | tf_op jit(solution)/shard_map/ppermute | solution.py:563
  42.5 1.1 collective-permute-start.2
  43.6 12.6 %all-to-all-done = bf16[64,32,128]{2,1,0:T(8,128)(2,1)} async-done(((bf16[64,32,128]{2,1,0:T(8,128)(2,1)}), bf16[64,32,128]{2,1,0:T(8,128)(2,1)}, u32[]{:S(2)}, u32[]{:S(2)}) %all-to-all-start) | async-done | bytes 524320 | tf_op jit(solution)/shard_map/all_to_all | solution.py:558
  56.1 1.0 slice.67
  57.2 1.4 collective-permute-start.6
  58.6 2.6 %collective-permute-start.7 = (bf16[1536,128]{1,0:T(8,128)(2,1)S(1)}, bf16[1536,128]{1,0:T(8,128)(2,1)S(1)}, u32[]{:S(2)}, u32[]{:S(2)}) collective-permute-start(bf16[1536,128]{1,0:T(8,128)(2,1)S(1)} %bitcast.44), channel_id=1, source_target_pairs={{0,2},{1,3},{2,0},{3,1},{4,6},{5,7},{6,4},{7,5},{8,10},{9,11},{10,... | collective-permute-start | bytes 1179656 | tf_op jit(solution)/shard_map/ppermute | solution.py:563
  61.2 1.1 collective-permute-start.8
  62.3 0.9 slice.68
  63.2 13.9 %expert_forward.1 = (bf16[768,1024]{1,0:T(8,128)(2,1)}, bf16[768,896]{1,0:T(8,128)(2,1)S(1)}, f32[768,896]{1,0:T(8,128)}, f32[768,896]{1,0:T(8,128)}, bf16[768,2...) custom-call(s32[2]{0:T(128)S(1)} %pad_add_fusion.mp.at, ...), custom_call_target="tpu_custom_call" | custom-call | tf_op jit(solution)/shard_map/expert_forward/pallas_call | solution.py:226
  77.5 0.8 collective-permute-start.4
  78.3 1.7 collective-permute-start.5
  80.0 1.4 copy-done.1
  81.4 16.0 %expert_backward.1 = (f32[1024,896]{1,0:T(8,128)}, f32[1024,896]{1,0:T(8,128)}, f32[896,1024]{1,0:T(8,128)}, f32[1,128]{1,0:T(1,128)S(1)}, f32[64,8,128]{2,1,0:T(8,128)S(1)}) custom-call(s32[2]{0:T(128)S(1)} %pad_add_fusion.mp.at, bf16[384,384]{1,0:T(8,128)(2,1)S(1)} %get-tuple-element.41.perm, bf16[1536,128]{1,0:T(8,128)(2,1)S(1)} %bitcast.46, ...), custom_call_target="tpu_custom_call" | custom-call | tf_op jit(solution)/shard_map/expert_backward/pallas_call | solution.py:360
  97.6 24.1 %all_to_all.20 = bf16[64,16,128]{2,1,0:T(8,128)(2,1)S(1)} all-to-all(bf16[64,16,128]{2,1,0:T(8,128)(2,1)S(1)} %pad_maximum_fusion.1), channel_id=1, replica_groups=mesh['expert_0'=8,'expert_1'=4,'expert_2'=2,'mp'=4] {'expert_0','expert_..., dimensions={0} | all-to-all | bytes 524288 | tf_op jit(solution)/shard_map/all_to_all | solution.py:558
  121.7 0.7 collective-permute-start.11
  122.5 1.3 collective-permute-start.10
  124.3 2.2 %collective-permute-done.10 = f32[16,128]{1,0:T(8,128)S(1)} collective-permute-done((f32[16,128]{1,0:T(8,128)S(1)}, f32[16,128]{1,0:T(8,128)S(1)}, u32[]{:S(2)}, u32[]{:S(2)}) %collective-permute-start.10) | collective-permute-done | bytes 8224 | tf_op jit(solution)/shard_map/ppermute | solution.py:563
  126.5 1.3 collective-permute-done.9
  127.9 0.9 pad_maximum_fusion
  128.7 6.1 %all-to-all-start.3 = ((bf16[64,40,128]{2,1,0:T(8,128)(2,1)}), bf16[64,40,128]{2,1,0:T(8,128)(2,1)S(1)}, u32[]{:S(2)}, u32[]{:S(2)}) async-start(bf16[64,40,128]{2,1,0:T(8,128)(2,1)} %pad_maximum_fusion), calls=%async_computation.3 | async-start | bytes 1310720 | tf_op jit(solution)/shard_map/all_to_all | solution.py:558
  135.5 11.8 %learned_step.3 = bf16[1024,896]{1,0:T(8,128)(2,1)} custom-call(f32[3,16]{1,0:T(4,128)S(1)} %maximum_maximum_fusion.scalars, f32[1]{0:T(128)} %bitcast.24.rms, bf16[512,256]{1,0:T(8,128)(2,1)S(1)} %spread_weights.2.spread, f32[1024,896]{1,0:T(8,128)} %get-tuple-element.60.grad, bf16[1024,896]{1,0:T(8,128)(2,1)} %bitcast.63), custom_call_target="tpu_custom_call" | custom-call | tf_op jit(solution)/shard_map/learned_step/pallas_call | solution.py:477
  147.2 11.8 %learned_step.4 = bf16[1024,896]{1,0:T(8,128)(2,1)} custom-call(f32[3,16]{1,0:T(4,128)S(1)} %maximum_maximum_fusion.scalars, f32[1]{0:T(128)} %bitcast.26.rms, bf16[512,256]{1,0:T(8,128)(2,1)S(1)} %spread_weights.2.spread, f32[1024,896]{1,0:T(8,128)} %get-tuple-element.62.grad, bf16[1024,896]{1,0:T(8,128)(2,1)} %bitcast.65), custom_call_target="tpu_custom_call" | custom-call | tf_op jit(solution)/shard_map/learned_step/pallas_call | solution.py:477
  159.0 11.7 %learned_step.5 = bf16[896,1024]{1,0:T(8,128)(2,1)} custom-call(f32[3,16]{1,0:T(4,128)S(1)} %maximum_maximum_fusion.scalars, f32[1]{0:T(128)} %bitcast.29.rms, bf16[512,256]{1,0:T(8,128)(2,1)S(1)} %spread_weights.3.spread, f32[896,1024]{1,0:T(8,128)} %get-tuple-element.65.grad, bf16[896,1024]{1,0:T(8,128)(2,1)} %bitcast.61), custom_call_target="tpu_custom_call" | custom-call | tf_op jit(solution)/shard_map/learned_step/pallas_call | solution.py:477
  170.7 2.9 %mix.1 = bf16[256,256]{1,0:T(8,128)(2,1)} custom-call(s32[2]{0:T(128)S(1)} %pad_add_fusion.mp.at, f32[256,128]{1,0:T(8,128)S(1)} %get-tuple-element.36.aux, bf16[256,1024]{1,0:T(8,128)(2,1)S(1)} %copy-done, bf16[2560,128]{1,0:T(8,128)(2,1)S(1)} %bitcast.42), custom_call_target="tpu_custom_call" | custom-call | tf_op jit(solution)/shard_map/mix/pallas_call | solution.py:513
  173.6 3.5 %router_step.1 = bf16[64,1024]{1,0:T(8,128)(2,1)} custom-call(f32[5,16]{1,0:T(8,128)S(1)} %pad_maximum_fusion.2.net, f32[64,8,128]{2,1,0:T(8,128)S(1)} %convert_add_fusion.columns, bf16[64,1024]{1,0:T(8,128)(2,1)S(1)} %bitcast.56), custom_call_target="tpu_custom_call" | custom-call | tf_op jit(solution)/shard_map/router_step/pallas_call | solution.py:543
  (58 shorter events, 5.2 us)
Async XLA Ops:
  0.6 18.8 %copy-start.2 = (bf16[1024,64]{0,1:T(8,128)(2,1)S(1)}, bf16[1024,64]{0,1:T(8,128)(2,1)}, u32[]{:S(2)}) copy-start(bf16[1024,64]{0,1:T(8,128)(2,1)} %param.13) | copy-start | bytes 393220
  0.7 0.7 copy-start.3
  1.4 18.0 %copy-start.4 = (s32[256,2]{0,1:T(2,128)S(1)}, s32[256,2]{0,1:T(2,128)}, u32[]{:S(2)}) copy-start(s32[256,2]{0,1:T(2,128)} %param.12) | copy-start | bytes 6148
  4.5 20.8 %copy-start.6 = (f32[16]{0:T(128)S(1)}, f32[16]{0:T(128)}, u32[]{:S(2)}) copy-start(f32[16]{0:T(128)} %param.19) | copy-start | bytes 196
  4.5 20.8 %copy-start.7 = (f32[16]{0:T(128)S(1)}, f32[16]{0:T(128)}, u32[]{:S(2)}) copy-start(f32[16]{0:T(128)} %param.18) | copy-start | bytes 196
  4.5 22.1 %copy-start.5 = (f32[3,16]{1,0:T(4,128)S(1)}, f32[3,16]{1,0:T(4,128)}, u32[]{:S(2)}) copy-start(f32[3,16]{1,0:T(4,128)} %param.17) | copy-start | bytes 580
  4.5 28.2 %all-to-all-start.1 = ((bf16[64,24,128]{2,1,0:T(8,128)(2,1)}), bf16[64,24,128]{2,1,0:T(8,128)(2,1)S(1)}, u32[]{:S(2)}, u32[]{:S(2)}) async-start(bf16[64,24,128]{2,1,0:T(8,128)(2,1)} %bitcast.15), calls=%async_computation.1 | async-start | bytes 786432 | tf_op jit(solution)/shard_map/all_to_all | solution.py:558
  32.7 23.4 %all-to-all-start = ((bf16[64,32,128]{2,1,0:T(8,128)(2,1)}), bf16[64,32,128]{2,1,0:T(8,128)(2,1)}, u32[]{:S(2)}, u32[]{:S(2)}) async-start(bf16[64,32,128]{2,1,0:T(8,128)(2,1)} %bitcast.13), calls=%async_computation | async-start | bytes 1048576 | tf_op jit(solution)/shard_map/all_to_all | solution.py:558
  38.5 22.7 %collective-permute-start = (bf16[1536,128]{1,0:T(8,128)(2,1)S(1)}, bf16[1536,128]{1,0:T(8,128)(2,1)S(1)}, u32[]{:S(2)}, u32[]{:S(2)}) collective-permute-start(bf16[1536,128]{1,0:T(8,128)(2,1)S(1)} %bitcast.48), channel_id=1, source_target_pairs={{0,1},{1,2},{2,3},{3,0},{4,5},{5,6},{6,7},{7,4},{8,9},{9,10},{10,1... | collective-permute-start | bytes 1179656 | tf_op jit(solution)/shard_map/ppermute | solution.py:563
  39.9 23.3 %collective-permute-start.1 = (bf16[1536,128]{1,0:T(8,128)(2,1)S(1)}, bf16[1536,128]{1,0:T(8,128)(2,1)S(1)}, u32[]{:S(2)}, u32[]{:S(2)}) collective-permute-start(bf16[1536,128]{1,0:T(8,128)(2,1)S(1)} %bitcast.49), channel_id=1, source_target_pairs={{0,2},{1,3},{2,0},{3,1},{4,6},{5,7},{6,4},{7,5},{8,10},{9,11},{10,... | collective-permute-start | bytes 1179656 | tf_op jit(solution)/shard_map/ppermute | solution.py:563
  42.5 20.7 %collective-permute-start.2 = (bf16[1536,128]{1,0:T(8,128)(2,1)S(1)}, bf16[1536,128]{1,0:T(8,128)(2,1)S(1)}, u32[]{:S(2)}, u32[]{:S(2)}) collective-permute-start(bf16[1536,128]{1,0:T(8,128)(2,1)S(1)} %bitcast.50), channel_id=1, source_target_pairs={{0,3},{1,0},{2,1},{3,2},{4,7},{5,4},{6,5},{7,6},{8,11},{9,8},{10,9... | collective-permute-start | bytes 1179656 | tf_op jit(solution)/shard_map/ppermute | solution.py:563
  57.2 21.1 %collective-permute-start.6 = (bf16[1536,128]{1,0:T(8,128)(2,1)S(1)}, bf16[1536,128]{1,0:T(8,128)(2,1)S(1)}, u32[]{:S(2)}, u32[]{:S(2)}) collective-permute-start(bf16[1536,128]{1,0:T(8,128)(2,1)S(1)} %bitcast.43), channel_id=1, source_target_pairs={{0,1},{1,2},{2,3},{3,0},{4,5},{5,6},{6,7},{7,4},{8,9},{9,10},{10,1... | collective-permute-start | bytes 1179656 | tf_op jit(solution)/shard_map/ppermute | solution.py:563
  58.6 21.4 %collective-permute-start.7 = (bf16[1536,128]{1,0:T(8,128)(2,1)S(1)}, bf16[1536,128]{1,0:T(8,128)(2,1)S(1)}, u32[]{:S(2)}, u32[]{:S(2)}) collective-permute-start(bf16[1536,128]{1,0:T(8,128)(2,1)S(1)} %bitcast.44), channel_id=1, source_target_pairs={{0,2},{1,3},{2,0},{3,1},{4,6},{5,7},{6,4},{7,5},{8,10},{9,11},{10,... | collective-permute-start | bytes 1179656 | tf_op jit(solution)/shard_map/ppermute | solution.py:563
  61.2 18.8 %collective-permute-start.8 = (bf16[1536,128]{1,0:T(8,128)(2,1)S(1)}, bf16[1536,128]{1,0:T(8,128)(2,1)S(1)}, u32[]{:S(2)}, u32[]{:S(2)}) collective-permute-start(bf16[1536,128]{1,0:T(8,128)(2,1)S(1)} %bitcast.45), channel_id=1, source_target_pairs={{0,3},{1,0},{2,1},{3,2},{4,7},{5,4},{6,5},{7,6},{8,11},{9,8},{10,9... | collective-permute-start | bytes 1179656 | tf_op jit(solution)/shard_map/ppermute | solution.py:563
  77.1 20.5 %collective-permute-start.3 = (bf16[768,256]{1,0:T(8,128)(2,1)S(1)}, bf16[768,256]{1,0:T(8,128)(2,1)S(1)}, u32[]{:S(2)}, u32[]{:S(2)}) collective-permute-start(bf16[768,256]{1,0:T(8,128)(2,1)S(1)} %get-tuple-element.43), channel_id=1, source_target_pairs={{0,1},{1,2},{2,3},{3,0},{4,5},{5,6},{6,7},{7,4},{8,9},{9,10},{10,1... | collective-permute-start | bytes 1179656 | tf_op jit(solution)/shard_map/ppermute | solution.py:563
  77.5 20.1 %collective-permute-start.4 = (bf16[768,256]{1,0:T(8,128)(2,1)S(1)}, bf16[768,256]{1,0:T(8,128)(2,1)S(1)}, u32[]{:S(2)}, u32[]{:S(2)}) collective-permute-start(bf16[768,256]{1,0:T(8,128)(2,1)S(1)} %get-tuple-element.44), channel_id=1, source_target_pairs={{0,2},{1,3},{2,0},{3,1},{4,6},{5,7},{6,4},{7,5},{8,10},{9,11},{10,... | collective-permute-start | bytes 1179656 | tf_op jit(solution)/shard_map/ppermute | solution.py:563
  78.3 19.3 %collective-permute-start.5 = (bf16[768,256]{1,0:T(8,128)(2,1)S(1)}, bf16[768,256]{1,0:T(8,128)(2,1)S(1)}, u32[]{:S(2)}, u32[]{:S(2)}) collective-permute-start(bf16[768,256]{1,0:T(8,128)(2,1)S(1)} %get-tuple-element.45), channel_id=1, source_target_pairs={{0,3},{1,0},{2,1},{3,2},{4,7},{5,4},{6,5},{7,6},{8,11},{9,8},{10,9... | collective-permute-start | bytes 1179656 | tf_op jit(solution)/shard_map/ppermute | solution.py:563
  80.0 1.4 copy-start.1
  121.7 2.6 %collective-permute-start.11 = (f32[16,128]{1,0:T(8,128)S(1)}, f32[16,128]{1,0:T(8,128)S(1)}, u32[]{:S(2)}, u32[]{:S(2)}) collective-permute-start(f32[16,128]{1,0:T(8,128)S(1)} %convert_reduce_fusion), channel_id=1, source_target_pairs={{0,3},{1,0},{2,1},{3,2},{4,7},{5,4},{6,5},{7,6},{8,11},{9,8},{10,9... | collective-permute-start | bytes 24584 | tf_op jit(solution)/shard_map/ppermute | solution.py:563
  122.5 4.0 %collective-permute-start.10 = (f32[16,128]{1,0:T(8,128)S(1)}, f32[16,128]{1,0:T(8,128)S(1)}, u32[]{:S(2)}, u32[]{:S(2)}) collective-permute-start(f32[16,128]{1,0:T(8,128)S(1)} %convert_reduce_fusion), channel_id=1, source_target_pairs={{0,2},{1,3},{2,0},{3,1},{4,6},{5,7},{6,4},{7,5},{8,10},{9,11},{10,... | collective-permute-start | bytes 24584 | tf_op jit(solution)/shard_map/ppermute | solution.py:563
  123.8 4.0 %collective-permute-start.9 = (f32[16,128]{1,0:T(8,128)S(1)}, f32[16,128]{1,0:T(8,128)S(1)}, u32[]{:S(2)}, u32[]{:S(2)}) collective-permute-start(f32[16,128]{1,0:T(8,128)S(1)} %convert_reduce_fusion), channel_id=1, source_target_pairs={{0,1},{1,2},{2,3},{3,0},{4,5},{5,6},{6,7},{7,4},{8,9},{9,10},{10,1... | collective-permute-start | bytes 24584 | tf_op jit(solution)/shard_map/ppermute | solution.py:563
  128.7 41.9 %all-to-all-start.3 = ((bf16[64,40,128]{2,1,0:T(8,128)(2,1)}), bf16[64,40,128]{2,1,0:T(8,128)(2,1)S(1)}, u32[]{:S(2)}, u32[]{:S(2)}) async-start(bf16[64,40,128]{2,1,0:T(8,128)(2,1)} %pad_maximum_fusion), calls=%async_computation.3 | async-start | bytes 1310720 | tf_op jit(solution)/shard_map/all_to_all | solution.py:558
  159.0 11.7 %copy-start = (bf16[256,1024]{1,0:T(8,128)(2,1)S(1)}, bf16[256,1024]{1,0:T(8,128)(2,1)}, u32[]{:S(2)}) copy-start(bf16[256,1024]{1,0:T(8,128)(2,1)} %tok_cols.3) | copy-start | bytes 1572868

commit v3 on v2

--- a/solution.py
+++ b/solution.py
@@ -236,12 +236,12 @@
             scratch_shapes=[pltpu.VMEM((rows, width), BF)],
         ),
         out_shape=[
-            jax.ShapeDtypeStruct((rows, width), BF),
-            jax.ShapeDtypeStruct((rows, ff), BF),
-            jax.ShapeDtypeStruct((rows, ff), F32),
-            jax.ShapeDtypeStruct((rows, ff), F32),
+            pltpu.HBM((rows, width), BF),
+            pltpu.HBM((rows, ff), BF),
+            pltpu.HBM((rows, ff), F32),
+            pltpu.HBM((rows, ff), F32),
         ]
-        + [jax.ShapeDtypeStruct((rows, 2 * LANES), BF)] * GROUPS,
+        + [pltpu.HBM((rows, 2 * LANES), BF)] * GROUPS,
         compiler_params=params(),
         name="expert_forward",
     )(mp_index, perm, *messages, w_gate, w_up, w_down)
@@ -278,7 +278,9 @@
     source = ((row >= first) & (row < first + CAP)).astype(F32)
     place = (iota((part, 1), 0).astype(F32) - row_sum(source * first.astype(F32))).astype(jnp.int32)
     slot = (place == iota((part, LANES), 1)).astype(F32)
-    spread = dot(source.astype(BF), jnp.concatenate([side[i] for i in range(5)], axis=1))
+    both = side[...].astype(F32)
+    both = jnp.concatenate([both[:, DATA + i, :] for i in range(5)], axis=1).astype(BF)
+    spread = dot(source.astype(BF), both)
     values = [row_sum(spread[:, i * LANES : (i + 1) * LANES] * slot) for i in range(5)]
     own = q * (values[0] + values[1])
     other = q * (values[2] + values[3])
@@ -364,7 +366,7 @@
             grid=(HALVES + CHUNKS,),
             in_specs=[whole(*perm.shape)]
             + [row(sent // HALVES, LANES)] * GROUPS
-            + [pl.BlockSpec((SIDE, part // CAP, LANES), lambda i, at: (0, first(i), 0))]
+            + [pl.BlockSpec((part // CAP, DATA + SIDE, LANES), lambda i, at: (first(i), 0, 0))]
             + [whole(ff, width), row(part, ff), row(part, ff), row(part, ff), row(part, width)],
             out_specs=[
                 out(width, ff),
@@ -384,15 +386,18 @@
             ],
         ),
         out_shape=[
-            jax.ShapeDtypeStruct((width, ff), F32),
-            jax.ShapeDtypeStruct((width, ff), F32),
-            jax.ShapeDtypeStruct((ff, width), F32),
+            pltpu.HBM((width, ff), F32),
+            pltpu.HBM((width, ff), F32),
+            pltpu.HBM((ff, width), F32),
             jax.ShapeDtypeStruct((1, LANES), F32),
             jax.ShapeDtypeStruct((experts, width // LANES, LANES), F32),
         ],
         compiler_params=params(),
         name="expert_backward",
-    )(index, perm, *messages, side, w_down, hidden, by_gate, by_up, rows_x)
+    )(
+        index, perm, *messages, side, in_hbm(w_down), in_hbm(hidden), in_hbm(by_gate), in_hbm(by_up),
+        in_hbm(rows_x),
+    )
 
 
 NET_ROWS = 32
@@ -494,15 +499,13 @@
 def mix_kernel(at, aux, tok_cols, back, out, *, size):
     del at
     rows = back.shape[0]
-    for h in range(2):
-        cols = slice(h * LANES, (h + 1) * LANES)
-        total = tok_cols[:, cols].astype(F32)
-        for k in range(2):
-            base = aux[:, 2 + k : 3 + k] * size + aux[:, 4 + k : 5 + k] + h * CAP
-            total = total + aux[:, k : k + 1] * dot(
-                one_hot(base.astype(jnp.int32), rows), back[...]
-            )
-        out[:, cols] = total.astype(BF)
+    later = jnp.concatenate([back[CAP:, :], back[:CAP, :]], axis=0)
+    both = jnp.concatenate([back[...], later], axis=1)
+    total = tok_cols[...].astype(F32)
+    for k in range(2):
+        base = aux[:, 2 + k : 3 + k] * size + aux[:, 4 + k : 5 + k]
+        total = total + aux[:, k : k + 1] * dot(one_hot(base.astype(jnp.int32), rows), both)
+    out[...] = total.astype(BF)
 
 
 def mix(index, aux, tokens, back, experts):
@@ -602,7 +605,7 @@
     net = jnp.concatenate([mlp_in, mlp_bias[None], mlp_out[None]], axis=0)
     router_across = router_weight.T
 
-    routes_across = routes.T
+    routes_across = in_hbm(routes.T)
     sent_x = send_x(in_hbm(tokens), routes_across, experts, index)
     own_x = to_experts(sent_x, experts).reshape(-1, LANES)
     sent_dy, aux = send_dy(in_hbm(tokens), in_hbm(cotangent), routes_across, router_across, index)
@@ -610,19 +613,17 @@
         (sent_dy, perm, perm_t, spread_in, spread_down, scalars, net)
     )
     msg_x = from_members([own_x] * GROUPS)
-    own_dy = to_experts(sent_dy, experts)
-    side = own_dy[:, DATA:].transpose(1, 0, 2)
-    own_dy = own_dy[:, :DATA].reshape(-1, LANES)
+    all_dy = to_experts(sent_dy, experts)
+    own_dy = all_dy[:, :DATA].reshape(-1, LANES)
     perm, own_dy = together((perm, own_dy))
     msg_dy = from_members([own_dy] * GROUPS)
 
     rows_x, hidden, by_gate, by_up, *parts = expert_forward(
         index, perm, msg_x, w_gate, w_up, w_down
     )
-    swapped = from_members(parts)
 
     g_gate, g_up, g_down, squares, router_part = expert_backward(
-        index, perm, msg_dy, side, w_down, hidden, by_gate, by_up, rows_x
+        index, perm, msg_dy, all_dy, w_down, hidden, by_gate, by_up, rows_x
     )
     high = lax.reduce_precision(squares, 8, 7)
     row = iota((SIDE, LANES), 0)
@@ -630,8 +631,8 @@
     terms = jnp.concatenate(
         [router_part, jnp.broadcast_to(squares[None], (experts, SIDE, LANES))], axis=1
     ).astype(BF)
-    swapped, terms = together((swapped, terms))
-    expert_out = pack_rows(perm_t, swapped).reshape(experts, DATA, LANES)
+    parts, terms = together((parts, terms))
+    swapped = from_members(parts)
     sums = jnp.sum(to_experts(terms, experts).astype(F32), axis=0)
     sums = sum(from_members([sums] * GROUPS))
     total_count = experts * width * w_gate.shape[1] * groups
@@ -640,9 +641,13 @@
     high = lax.reduce_precision(column, 8, 7)
     column = jnp.concatenate([high, column - high], axis=0).astype(BF)
     column = jnp.broadcast_to(column[None], (experts, 2 * SIDE, LANES))
-    back = to_experts(jnp.concatenate([expert_out, column], axis=1), experts)
 
     down_update = learned_step(g_down, w_down, inverse[2:3], spread_down, scalars)
+    swapped, down_update = together((swapped, down_update))
+    expert_out = pack_rows(perm_t, swapped).reshape(experts, DATA, LANES)
+    back = jnp.concatenate([expert_out, column], axis=1)
+    back, g_gate, g_up = together((back, g_gate, g_up))
+    back = to_experts(back, experts)
     gate_update = learned_step(g_gate, w_gate, inverse[0:1], spread_in, scalars)
     up_update = learned_step(g_up, w_up, inverse[1:2], spread_in, scalars)
     back, up_update = together((back, up_update))

time: 178 us -> 179 us (level)
  starting transfers between devices: 40 us -> 42.9 us
    ppermute x12, starting transfers between devices: 15 us -> 17.6 us  [from_members(): lax.ppermute(pieces[k], 'mp', [(i, (i + k) % GROUPS) for i in range(GROUP...]
    slice x3 -> x2, local copies, waits for them, and re-layouts: 2.54 us -> 0.71 us  [the longest x1 0.67 us: on_device(): gate_update = learned_step(g_gate, w_gate, inverse[0:1], spread_in, scalars)]
  transfers between devices with their start and end apart: 15 -> 15, of which waited for: 4 -> 4; matrix products, arithmetic and copies ran while one was open for 3% -> 2% of each run, Pallas kernels for 41% -> 31%
where the time goes in v3:
time: 179 us
  Pallas kernels  81.4 us (45%)
  starting transfers between devices  42.9 us (24%)
  blocking collectives  23.4 us (13%)
  waiting for transfers between devices  21.6 us (12%)
  local copies, waits for them, and re-layouts  4.58 us (3%)
  other arithmetic  3.8 us (2%)
    pallas_call x3, Pallas kernels, learned_step(): pl.pallas_call(functools.partial(step_kernel, rows=128), grid=(height //...  35.3 us
    all_to_all x3, starting transfers between devices, to_experts(): return lax.all_to_all(sent, EXPERT, 0, 0, tiled=True)  25.3 us
    all_to_all x1, blocking collectives, to_experts(): return lax.all_to_all(sent, EXPERT, 0, 0, tiled=True)  23.4 us
    ppermute x12, starting transfers between devices, from_members(): lax.ppermute(pieces[k], 'mp', [(i, (i + k) % GROUPS) for i in range(GROUP...  17.6 us
    all_to_all x3, waiting for transfers between devices, to_experts(): return lax.all_to_all(sent, EXPERT, 0, 0, tiled=True)  17 us
    pallas_call x1, Pallas kernels, expert_backward(): pl.pallas_call(backward_kernel, grid_spec=pltpu.PrefetchScalarGridSpec(nu...  16.8 us
    pallas_call x1, Pallas kernels, expert_forward(): pl.pallas_call(forward_kernel, grid_spec=pltpu.PrefetchScalarGridSpec(num...  14.1 us
    pallas_call x1, Pallas kernels, send_dy(): pl.pallas_call(send_dy_kernel, grid_spec=pltpu.PrefetchScalarGridSpec(num...  5.2 us
  transfers between devices with their start and end apart: 15, of which 4 were waited for; matrix products, arithmetic and copies ran while one was open for 2% of the time, Pallas kernels for 31%

profile of v3, /device:TPU:1, one launch (start us, length us, event | category | flops | bytes accessed | tf_op | source)
XLA Modules:
  0.0 178.5 jit_solution(4379517942117261351)
XLA Ops:
  0.7 3.1 %send_x.1 = bf16[1536,128]{1,0:T(8,128)(2,1)} custom-call(s32[2]{0:T(128)S(1)} %pad_add_fusion.mp.at, bf16[256,1024]{1,0:T(8,128)(2,1)} %tok_cols.3, s32[2,256]{1,0:T(2,128)} %bitcast.65), custom_call_target="tpu_custom_call" | custom-call | tf_op jit(solution)/shard_map/send_x/pallas_call | solution.py:129
  3.9 13.1 %all-to-all-start.1 = ((bf16[64,24,128]{2,1,0:T(8,128)(2,1)}), bf16[64,24,128]{2,1,0:T(8,128)(2,1)S(1)}, u32[]{:S(2)}, u32[]{:S(2)}) async-start(bf16[64,24,128]{2,1,0:T(8,128)(2,1)} %bitcast.15), calls=%async_computation.1 | async-start | bytes 786432 | tf_op jit(solution)/shard_map/all_to_all | solution.py:561
  17.0 0.8 multiply_bitcast_fusion
  18.7 0.7 copy-done.4
  19.4 5.2 %send_dy.1 = (bf16[2048,128]{1,0:T(8,128)(2,1)S(1)}, f32[256,128]{1,0:T(8,128)S(1)}) custom-call(s32[2]{0:T(128)S(1)} %pad_add_fusion.mp.at, bf16[256,1024]{1,0:T(8,128)(2,1)} %tok_cols.3, bf16[256,1024]{1,0:T(8,128)(2,1)} %cot_cols.1, s32[2,256]{1,0:T(2,128)} %bitcast.66, bf16[64,1024]{1,0:T(8,128)(2,1)S(1)} %bitcast.56), custom_call_target="tpu_custom_call" | custom-call | tf_op jit(solution)/shard_map/send_dy/pallas_call | solution.py:151
  26.0 0.7 pad.11.clone
  26.8 0.9 fusion.1
  27.7 4.3 %all-to-all-done.1 = bf16[64,24,128]{2,1,0:T(8,128)(2,1)S(1)} async-done(((bf16[64,24,128]{2,1,0:T(8,128)(2,1)}), bf16[64,24,128]{2,1,0:T(8,128)(2,1)S(1)}, u32[]{:S(2)}, u32[]{:S(2)}) %all-to-all-start.1) | async-done | bytes 393248 | tf_op jit(solution)/shard_map/all_to_all | solution.py:561
  32.1 6.0 %all-to-all-start = ((bf16[64,32,128]{2,1,0:T(8,128)(2,1)}), bf16[64,32,128]{2,1,0:T(8,128)(2,1)S(1)}, u32[]{:S(2)}, u32[]{:S(2)}) async-start(bf16[64,32,128]{2,1,0:T(8,128)(2,1)} %bitcast.55), calls=%async_computation | async-start | bytes 1048576 | tf_op jit(solution)/shard_map/all_to_all | solution.py:561
  38.0 1.4 collective-permute-start
  39.4 2.6 %collective-permute-start.1 = (bf16[1536,128]{1,0:T(8,128)(2,1)S(1)}, bf16[1536,128]{1,0:T(8,128)(2,1)}, u32[]{:S(2)}, u32[]{:S(2)}) collective-permute-start(bf16[1536,128]{1,0:T(8,128)(2,1)S(1)} %bitcast.50), channel_id=1, source_target_pairs={{0,2},{1,3},{2,0},{3,1},{4,6},{5,7},{6,4},{7,5},{8,10},{9,11},{10,... | collective-permute-start | bytes 1179656 | tf_op jit(solution)/shard_map/ppermute | solution.py:566
  42.0 1.1 collective-permute-start.2
  43.1 12.7 %all-to-all-done.side = bf16[64,32,128]{2,1,0:T(8,128)(2,1)S(1)} async-done(((bf16[64,32,128]{2,1,0:T(8,128)(2,1)}), bf16[64,32,128]{2,1,0:T(8,128)(2,1)S(1)}, u32[]{:S(2)}, u32[]{:S(2)}) %all-to-all-start) | async-done | bytes 524320 | tf_op jit(solution)/shard_map/all_to_all | solution.py:561
  55.8 1.4 collective-permute-start.3
  57.2 2.6 %collective-permute-start.4 = (bf16[1536,128]{1,0:T(8,128)(2,1)S(1)}, bf16[1536,128]{1,0:T(8,128)(2,1)S(1)}, u32[]{:S(2)}, u32[]{:S(2)}) collective-permute-start(bf16[1536,128]{1,0:T(8,128)(2,1)S(1)} %bitcast.45), channel_id=1, source_target_pairs={{0,2},{1,3},{2,0},{3,1},{4,6},{5,7},{6,4},{7,5},{8,10},{9,11},{10,... | collective-permute-start | bytes 1179656 | tf_op jit(solution)/shard_map/ppermute | solution.py:566
  59.8 1.1 collective-permute-start.5
  60.9 1.5 copy-done.1
  62.4 14.1 %expert_forward.1 = (bf16[768,1024]{1,0:T(8,128)(2,1)}, bf16[768,896]{1,0:T(8,128)(2,1)}, f32[768,896]{1,0:T(8,128)}, f32[768,896]{1,0:T(8,128)}, bf16[768,256]{...) custom-call(s32[2]{0:T(128)S(1)} %pad_add_fusion.mp.at, ...), custom_call_target="tpu_custom_call" | custom-call | tf_op jit(solution)/shard_map/expert_forward/pallas_call | solution.py:226
  77.0 16.8 %expert_backward.1 = (f32[1024,896]{1,0:T(8,128)}, f32[1024,896]{1,0:T(8,128)}, f32[896,1024]{1,0:T(8,128)}, f32[1,128]{1,0:T(1,128)S(1)}, f32[64,8,128]{2,1,0:T(8,128)S(1)}) custom-call(s32[2]{0:T(128)S(1)} %pad_add_fusion.mp.at, bf16[384,384]{1,0:T(8,128)(2,1)S(1)} %get-tuple-element.49.perm, bf16[1536,128]{1,0:T(8,128)(2,1)S(1)} %bitcast.47, ...), custom_call_target="tpu_custom_call" | custom-call | tf_op jit(solution)/shard_map/expert_backward/pallas_call | solution.py:362
  94.1 23.4 %all_to_all.20 = bf16[64,16,128]{2,1,0:T(8,128)(2,1)S(1)} all-to-all(bf16[64,16,128]{2,1,0:T(8,128)(2,1)S(1)} %pad_maximum_fusion.1), channel_id=1, replica_groups=mesh['expert_0'=8,'expert_1'=4,'expert_2'=2,'mp'=4] {'expert_0','expert_..., dimensions={0} | all-to-all | bytes 524288 | tf_op jit(solution)/shard_map/all_to_all | solution.py:561
  117.5 1.9 %collective-permute-start.11 = (f32[16,128]{1,0:T(8,128)S(1)}, f32[16,128]{1,0:T(8,128)S(1)}, u32[]{:S(2)}, u32[]{:S(2)}) collective-permute-start(f32[16,128]{1,0:T(8,128)S(1)} %convert_reduce_fusion), channel_id=1, source_target_pairs={{0,3},{1,0},{2,1},{3,2},{4,7},{5,4},{6,5},{7,6},{8,11},{9,8},{10,9... | collective-permute-start | bytes 24584 | tf_op jit(solution)/shard_map/ppermute | solution.py:566
  119.4 1.6 collective-permute-start.10
  121.1 1.0 collective-permute-start.6
  122.1 2.8 %collective-permute-start.7 = (bf16[768,256]{1,0:T(8,128)(2,1)S(1)}, bf16[768,256]{1,0:T(8,128)(2,1)S(1)}, u32[]{:S(2)}, u32[]{:S(2)}) collective-permute-start(bf16[768,256]{1,0:T(8,128)(2,1)S(1)} %copy-done.15), channel_id=1, source_target_pairs={{0,2},{1,3},{2,0},{3,1},{4,6},{5,7},{6,4},{7,5},{8,10},{9,11},{10,... | collective-permute-start | bytes 1179656 | tf_op jit(solution)/shard_map/ppermute | solution.py:566
  125.7 11.7 %learned_step.3 = bf16[896,1024]{1,0:T(8,128)(2,1)} custom-call(f32[3,16]{1,0:T(4,128)S(1)} %maximum_maximum_fusion.scalars, f32[1]{0:T(128)} %bitcast.22.rms, bf16[512,256]{1,0:T(8,128)(2,1)S(1)} %copy-done.5, f32[896,1024]{1,0:T(8,128)} %get-tuple-element.68.grad, bf16[896,1024]{1,0:T(8,128)(2,1)} %bitcast.60), custom_call_target="tpu_custom_call" | custom-call | tf_op jit(solution)/shard_map/learned_step/pallas_call | solution.py:482
  137.4 4.0 %collective-permute-done.7.p2 = bf16[768,256]{1,0:T(8,128)(2,1)S(1)} collective-permute-done((bf16[768,256]{1,0:T(8,128)(2,1)S(1)}, bf16[768,256]{1,0:T(8,128)(2,1)S(1)}, u32[]{:S(2)}, u32[]{:S(2)}) %collective-permute-start.7) | collective-permute-done | bytes 393248 | tf_op jit(solution)/shard_map/ppermute | solution.py:566
  141.9 1.0 pad_maximum_fusion
  142.9 6.2 %all-to-all-start.3 = ((bf16[64,40,128]{2,1,0:T(8,128)(2,1)}), bf16[64,40,128]{2,1,0:T(8,128)(2,1)S(1)}, u32[]{:S(2)}, u32[]{:S(2)}) async-start(bf16[64,40,128]{2,1,0:T(8,128)(2,1)} %pad_maximum_fusion), calls=%async_computation.3 | async-start | bytes 1310720 | tf_op jit(solution)/shard_map/all_to_all | solution.py:561
  149.1 11.8 %learned_step.4 = bf16[1024,896]{1,0:T(8,128)(2,1)} custom-call(f32[3,16]{1,0:T(4,128)S(1)} %maximum_maximum_fusion.scalars, f32[1]{0:T(128)} %bitcast.24.rms, bf16[512,256]{1,0:T(8,128)(2,1)S(1)} %spread_weights.2.spread, f32[1024,896]{1,0:T(8,128)} %get-tuple-element.77.grad, bf16[1024,896]{1,0:T(8,128)(2,1)} %bitcast.39), custom_call_target="tpu_custom_call" | custom-call | tf_op jit(solution)/shard_map/learned_step/pallas_call | solution.py:482
  160.9 11.8 %learned_step.5 = bf16[1024,896]{1,0:T(8,128)(2,1)} custom-call(f32[3,16]{1,0:T(4,128)S(1)} %maximum_maximum_fusion.scalars, f32[1]{0:T(128)} %bitcast.26.rms, bf16[512,256]{1,0:T(8,128)(2,1)S(1)} %spread_weights.2.spread, f32[1024,896]{1,0:T(8,128)} %get-tuple-element.79.grad, bf16[1024,896]{1,0:T(8,128)(2,1)} %bitcast.41), custom_call_target="tpu_custom_call" | custom-call | tf_op jit(solution)/shard_map/learned_step/pallas_call | solution.py:482
  172.8 2.2 %mix.1 = bf16[256,256]{1,0:T(8,128)(2,1)} custom-call(s32[2]{0:T(128)S(1)} %pad_add_fusion.mp.at, f32[256,128]{1,0:T(8,128)S(1)} %copy-done.10, bf16[256,1024]{1,0:T(8,128)(2,1)S(1)} %copy-done.2, bf16[2560,128]{1,0:T(8,128)(2,1)S(1)} %bitcast.43), custom_call_target="tpu_custom_call" | custom-call | tf_op jit(solution)/shard_map/mix/pallas_call | solution.py:516
  175.0 3.5 %router_step.1 = bf16[64,1024]{1,0:T(8,128)(2,1)} custom-call(f32[5,16]{1,0:T(8,128)S(1)} %pad_maximum_fusion.2.net, f32[64,8,128]{2,1,0:T(8,128)S(1)} %convert_add_fusion.columns, bf16[64,1024]{1,0:T(8,128)(2,1)S(1)} %bitcast.57), custom_call_target="tpu_custom_call" | custom-call | tf_op jit(solution)/shard_map/router_step/pallas_call | solution.py:546
  (74 shorter events, 4.7 us)
Async XLA Ops:
  0.6 18.8 %copy-start.7 = (bf16[1024,64]{0,1:T(8,128)(2,1)S(1)}, bf16[1024,64]{0,1:T(8,128)(2,1)}, u32[]{:S(2)}) copy-start(bf16[1024,64]{0,1:T(8,128)(2,1)} %param.13) | copy-start | bytes 393220
  3.9 21.4 %copy-start.12 = (f32[16]{0:T(128)S(1)}, f32[16]{0:T(128)}, u32[]{:S(2)}) copy-start(f32[16]{0:T(128)} %param.19) | copy-start | bytes 196
  3.9 21.4 %copy-start.13 = (f32[16]{0:T(128)S(1)}, f32[16]{0:T(128)}, u32[]{:S(2)}) copy-start(f32[16]{0:T(128)} %param.18) | copy-start | bytes 196
  3.9 22.9 %copy-start.11 = (f32[3,16]{1,0:T(4,128)S(1)}, f32[3,16]{1,0:T(4,128)}, u32[]{:S(2)}) copy-start(f32[3,16]{1,0:T(4,128)} %param.17) | copy-start | bytes 580
  3.9 28.2 %all-to-all-start.1 = ((bf16[64,24,128]{2,1,0:T(8,128)(2,1)}), bf16[64,24,128]{2,1,0:T(8,128)(2,1)S(1)}, u32[]{:S(2)}, u32[]{:S(2)}) async-start(bf16[64,24,128]{2,1,0:T(8,128)(2,1)} %bitcast.15), calls=%async_computation.1 | async-start | bytes 786432 | tf_op jit(solution)/shard_map/all_to_all | solution.py:561
  18.7 0.7 copy-start.4
  19.4 41.4 %copy-start = (bf16[1,1024,896]{2,1,0:T(8,128)(2,1)S(1)}, bf16[1,1024,896]{2,1,0:T(8,128)(2,1)}, u32[]{:S(2)}) copy-start(bf16[1,1024,896]{2,1,0:T(8,128)(2,1)} %param.15) | copy-start | bytes 5505028
  24.6 0.7 copy-start.9
  25.3 2.4 %copy-start.6 = (bf16[2048,128]{1,0:T(8,128)(2,1)}, bf16[2048,128]{1,0:T(8,128)(2,1)S(1)}, u32[]{:S(2)}) copy-start(bf16[2048,128]{1,0:T(8,128)(2,1)S(1)} %get-tuple-element.48) | copy-start | bytes 1572868
  32.1 23.7 %all-to-all-start = ((bf16[64,32,128]{2,1,0:T(8,128)(2,1)}), bf16[64,32,128]{2,1,0:T(8,128)(2,1)S(1)}, u32[]{:S(2)}, u32[]{:S(2)}) async-start(bf16[64,32,128]{2,1,0:T(8,128)(2,1)} %bitcast.55), calls=%async_computation | async-start | bytes 1048576 | tf_op jit(solution)/shard_map/all_to_all | solution.py:561
  38.0 21.8 %collective-permute-start = (bf16[1536,128]{1,0:T(8,128)(2,1)S(1)}, bf16[1536,128]{1,0:T(8,128)(2,1)}, u32[]{:S(2)}, u32[]{:S(2)}) collective-permute-start(bf16[1536,128]{1,0:T(8,128)(2,1)S(1)} %bitcast.49), channel_id=1, source_target_pairs={{0,1},{1,2},{2,3},{3,0},{4,5},{5,6},{6,7},{7,4},{8,9},{9,10},{10,1... | collective-permute-start | bytes 1179656 | tf_op jit(solution)/shard_map/ppermute | solution.py:566
  39.4 21.5 %collective-permute-start.1 = (bf16[1536,128]{1,0:T(8,128)(2,1)S(1)}, bf16[1536,128]{1,0:T(8,128)(2,1)}, u32[]{:S(2)}, u32[]{:S(2)}) collective-permute-start(bf16[1536,128]{1,0:T(8,128)(2,1)S(1)} %bitcast.50), channel_id=1, source_target_pairs={{0,2},{1,3},{2,0},{3,1},{4,6},{5,7},{6,4},{7,5},{8,10},{9,11},{10,... | collective-permute-start | bytes 1179656 | tf_op jit(solution)/shard_map/ppermute | solution.py:566
  42.0 18.8 %collective-permute-start.2 = (bf16[1536,128]{1,0:T(8,128)(2,1)S(1)}, bf16[1536,128]{1,0:T(8,128)(2,1)}, u32[]{:S(2)}, u32[]{:S(2)}) collective-permute-start(bf16[1536,128]{1,0:T(8,128)(2,1)S(1)} %bitcast.51), channel_id=1, source_target_pairs={{0,3},{1,0},{2,1},{3,2},{4,7},{5,4},{6,5},{7,6},{8,11},{9,8},{10,9... | collective-permute-start | bytes 1179656 | tf_op jit(solution)/shard_map/ppermute | solution.py:566
  55.8 20.7 %collective-permute-start.3 = (bf16[1536,128]{1,0:T(8,128)(2,1)S(1)}, bf16[1536,128]{1,0:T(8,128)(2,1)S(1)}, u32[]{:S(2)}, u32[]{:S(2)}) collective-permute-start(bf16[1536,128]{1,0:T(8,128)(2,1)S(1)} %bitcast.44), channel_id=1, source_target_pairs={{0,1},{1,2},{2,3},{3,0},{4,5},{5,6},{6,7},{7,4},{8,9},{9,10},{10,1... | collective-permute-start | bytes 1179656 | tf_op jit(solution)/shard_map/ppermute | solution.py:566
  57.2 19.9 %collective-permute-start.4 = (bf16[1536,128]{1,0:T(8,128)(2,1)S(1)}, bf16[1536,128]{1,0:T(8,128)(2,1)S(1)}, u32[]{:S(2)}, u32[]{:S(2)}) collective-permute-start(bf16[1536,128]{1,0:T(8,128)(2,1)S(1)} %bitcast.45), channel_id=1, source_target_pairs={{0,2},{1,3},{2,0},{3,1},{4,6},{5,7},{6,4},{7,5},{8,10},{9,11},{10,... | collective-permute-start | bytes 1179656 | tf_op jit(solution)/shard_map/ppermute | solution.py:566
  59.8 17.3 %collective-permute-start.5 = (bf16[1536,128]{1,0:T(8,128)(2,1)S(1)}, bf16[1536,128]{1,0:T(8,128)(2,1)S(1)}, u32[]{:S(2)}, u32[]{:S(2)}) collective-permute-start(bf16[1536,128]{1,0:T(8,128)(2,1)S(1)} %bitcast.46), channel_id=1, source_target_pairs={{0,3},{1,0},{2,1},{3,2},{4,7},{5,4},{6,5},{7,6},{8,11},{9,8},{10,9... | collective-permute-start | bytes 1179656 | tf_op jit(solution)/shard_map/ppermute | solution.py:566
  60.9 1.5 copy-start.1
  93.8 27.2 %copy-start.16 = (bf16[768,256]{1,0:T(8,128)(2,1)S(1)}, bf16[768,256]{1,0:T(8,128)(2,1)}, u32[]{:S(2)}) copy-start(bf16[768,256]{1,0:T(8,128)(2,1)} %get-tuple-element.62) | copy-start | bytes 1179652
  93.8 28.3 %copy-start.15 = (bf16[768,256]{1,0:T(8,128)(2,1)S(1)}, bf16[768,256]{1,0:T(8,128)(2,1)}, u32[]{:S(2)}) copy-start(bf16[768,256]{1,0:T(8,128)(2,1)} %get-tuple-element.63) | copy-start | bytes 1179652
  93.8 31.1 %copy-start.14 = (bf16[768,256]{1,0:T(8,128)(2,1)S(1)}, bf16[768,256]{1,0:T(8,128)(2,1)}, u32[]{:S(2)}) copy-start(bf16[768,256]{1,0:T(8,128)(2,1)} %get-tuple-element.64) | copy-start | bytes 1179652
  93.9 31.9 %copy-start.5 = (bf16[512,256]{1,0:T(8,128)(2,1)S(1)}, bf16[512,256]{1,0:T(8,128)(2,1)}, u32[]{:S(2)}) copy-start(bf16[512,256]{1,0:T(8,128)(2,1)} %copy-done.4) | copy-start | bytes 786436
  117.5 7.4 %collective-permute-start.11 = (f32[16,128]{1,0:T(8,128)S(1)}, f32[16,128]{1,0:T(8,128)S(1)}, u32[]{:S(2)}, u32[]{:S(2)}) collective-permute-start(f32[16,128]{1,0:T(8,128)S(1)} %convert_reduce_fusion), channel_id=1, source_target_pairs={{0,3},{1,0},{2,1},{3,2},{4,7},{5,4},{6,5},{7,6},{8,11},{9,8},{10,9... | collective-permute-start | bytes 24584 | tf_op jit(solution)/shard_map/ppermute | solution.py:566
  119.4 5.6 %collective-permute-start.10 = (f32[16,128]{1,0:T(8,128)S(1)}, f32[16,128]{1,0:T(8,128)S(1)}, u32[]{:S(2)}, u32[]{:S(2)}) collective-permute-start(f32[16,128]{1,0:T(8,128)S(1)} %convert_reduce_fusion), channel_id=1, source_target_pairs={{0,2},{1,3},{2,0},{3,1},{4,6},{5,7},{6,4},{7,5},{8,10},{9,11},{10,... | collective-permute-start | bytes 24584 | tf_op jit(solution)/shard_map/ppermute | solution.py:566
  121.0 4.0 %collective-permute-start.9 = (f32[16,128]{1,0:T(8,128)S(1)}, f32[16,128]{1,0:T(8,128)S(1)}, u32[]{:S(2)}, u32[]{:S(2)}) collective-permute-start(f32[16,128]{1,0:T(8,128)S(1)} %convert_reduce_fusion), channel_id=1, source_target_pairs={{0,1},{1,2},{2,3},{3,0},{4,5},{5,6},{6,7},{7,4},{8,9},{9,10},{10,1... | collective-permute-start | bytes 24584 | tf_op jit(solution)/shard_map/ppermute | solution.py:566
  121.1 16.4 %collective-permute-start.6 = (bf16[768,256]{1,0:T(8,128)(2,1)S(1)}, bf16[768,256]{1,0:T(8,128)(2,1)S(1)}, u32[]{:S(2)}, u32[]{:S(2)}) collective-permute-start(bf16[768,256]{1,0:T(8,128)(2,1)S(1)} %copy-done.16), channel_id=1, source_target_pairs={{0,1},{1,2},{2,3},{3,0},{4,5},{5,6},{6,7},{7,4},{8,9},{9,10},{10,1... | collective-permute-start | bytes 1179656 | tf_op jit(solution)/shard_map/ppermute | solution.py:566
  122.1 19.3 %collective-permute-start.7 = (bf16[768,256]{1,0:T(8,128)(2,1)S(1)}, bf16[768,256]{1,0:T(8,128)(2,1)S(1)}, u32[]{:S(2)}, u32[]{:S(2)}) collective-permute-start(bf16[768,256]{1,0:T(8,128)(2,1)S(1)} %copy-done.15), channel_id=1, source_target_pairs={{0,2},{1,3},{2,0},{3,1},{4,6},{5,7},{6,4},{7,5},{8,10},{9,11},{10,... | collective-permute-start | bytes 1179656 | tf_op jit(solution)/shard_map/ppermute | solution.py:566
  124.9 16.5 %collective-permute-start.8 = (bf16[768,256]{1,0:T(8,128)(2,1)S(1)}, bf16[768,256]{1,0:T(8,128)(2,1)S(1)}, u32[]{:S(2)}, u32[]{:S(2)}) collective-permute-start(bf16[768,256]{1,0:T(8,128)(2,1)S(1)} %copy-done.14), channel_id=1, source_target_pairs={{0,3},{1,0},{2,1},{3,2},{4,7},{5,4},{6,5},{7,6},{8,11},{9,8},{10,9... | collective-permute-start | bytes 1179656 | tf_op jit(solution)/shard_map/ppermute | solution.py:566
  125.7 15.7 %copy-start.3 = (bf16[384,384]{1,0:T(8,128)(2,1)S(1)}, bf16[384,384]{1,0:T(8,128)(2,1)}, u32[]{:S(2)}) copy-start(bf16[384,384]{1,0:T(8,128)(2,1)} %get-tuple-element.46.perm_t) | copy-start | bytes 884740
  125.7 15.7 %copy-start.8 = (bf16[768,256]{1,0:T(8,128)(2,1)S(1)}, bf16[768,256]{1,0:T(8,128)(2,1)}, u32[]{:S(2)}) copy-start(bf16[768,256]{1,0:T(8,128)(2,1)} %get-tuple-element.69.p0) | copy-start | bytes 1179652
  142.9 29.9 %all-to-all-start.3 = ((bf16[64,40,128]{2,1,0:T(8,128)(2,1)}), bf16[64,40,128]{2,1,0:T(8,128)(2,1)S(1)}, u32[]{:S(2)}, u32[]{:S(2)}) async-start(bf16[64,40,128]{2,1,0:T(8,128)(2,1)} %pad_maximum_fusion), calls=%async_computation.3 | async-start | bytes 1310720 | tf_op jit(solution)/shard_map/all_to_all | solution.py:561
  160.9 11.9 %copy-start.2 = (bf16[256,1024]{1,0:T(8,128)(2,1)S(1)}, bf16[256,1024]{1,0:T(8,128)(2,1)}, u32[]{:S(2)}) copy-start(bf16[256,1024]{1,0:T(8,128)(2,1)} %tok_cols.3) | copy-start | bytes 1572868
  160.9 11.9 %copy-start.10 = (f32[256,128]{1,0:T(8,128)S(1)}, f32[256,128]{1,0:T(8,128)}, u32[]{:S(2)}) copy-start(f32[256,128]{1,0:T(8,128)} %copy-done.9) | copy-start | bytes 393220

commit v4 on v3

--- a/solution.py
+++ b/solution.py
@@ -244,7 +244,7 @@
         + [pltpu.HBM((rows, 2 * LANES), BF)] * GROUPS,
         compiler_params=params(),
         name="expert_forward",
-    )(mp_index, perm, *messages, w_gate, w_up, w_down)
+    )(mp_index, perm, *messages, in_hbm(w_gate), in_hbm(w_up), in_hbm(w_down))
 
 
 def pack_kernel(perm_t, p0, p1, p2, p3, out):
@@ -622,6 +622,8 @@
         index, perm, msg_x, w_gate, w_up, w_down
     )
 
+    swapped = from_members(parts)
+
     g_gate, g_up, g_down, squares, router_part = expert_backward(
         index, perm, msg_dy, all_dy, w_down, hidden, by_gate, by_up, rows_x
     )
@@ -631,8 +633,8 @@
     terms = jnp.concatenate(
         [router_part, jnp.broadcast_to(squares[None], (experts, SIDE, LANES))], axis=1
     ).astype(BF)
-    parts, terms = together((parts, terms))
-    swapped = from_members(parts)
+    swapped, terms = together((swapped, terms))
+    expert_out = pack_rows(perm_t, swapped).reshape(experts, DATA, LANES)
     sums = jnp.sum(to_experts(terms, experts).astype(F32), axis=0)
     sums = sum(from_members([sums] * GROUPS))
     total_count = experts * width * w_gate.shape[1] * groups
@@ -641,13 +643,9 @@
     high = lax.reduce_precision(column, 8, 7)
     column = jnp.concatenate([high, column - high], axis=0).astype(BF)
     column = jnp.broadcast_to(column[None], (experts, 2 * SIDE, LANES))
+    back = to_experts(jnp.concatenate([expert_out, column], axis=1), experts)
 
     down_update = learned_step(g_down, w_down, inverse[2:3], spread_down, scalars)
-    swapped, down_update = together((swapped, down_update))
-    expert_out = pack_rows(perm_t, swapped).reshape(experts, DATA, LANES)
-    back = jnp.concatenate([expert_out, column], axis=1)
-    back, g_gate, g_up = together((back, g_gate, g_up))
-    back = to_experts(back, experts)
     gate_update = learned_step(g_gate, w_gate, inverse[0:1], spread_in, scalars)
     up_update = learned_step(g_up, w_up, inverse[1:2], spread_in, scalars)
     back, up_update = together((back, up_update))

time: 179 us -> 177 us (0.989)
  starting transfers between devices: 42.9 us -> 39.9 us
  local copies, waits for them, and re-layouts: 4.58 us -> 1.64 us
  blocking collectives: 23.4 us -> 25.5 us
    unnamed x34 -> x12, local copies, waits for them, and re-layouts: 2.89 us -> 0.02 us
    ppermute x12, starting transfers between devices: 17.6 us -> 15.1 us  [from_members(): lax.ppermute(pieces[k], 'mp', [(i, (i + k) % GROUPS) for i in range(GROUP...]
    all_to_all x1, blocking collectives: 23.4 us -> 25.5 us  [to_experts(): return lax.all_to_all(sent, EXPERT, 0, 0, tiled=True)]
  transfers between devices with their start and end apart: 15 -> 15, of which waited for: 4 -> 5; matrix products, arithmetic and copies ran while one was open for 2% -> 2% of each run, Pallas kernels for 31% -> 42%
where the time goes in v4:
time: 177 us; the launch traced here: 176 us
  Pallas kernels  82.9 us (47%)
  starting transfers between devices  39.9 us (23%)
  blocking collectives  25.5 us (14%)
  waiting for transfers between devices  22.4 us (13%)
  other arithmetic  2.91 us (2%)
    pallas_call x3, Pallas kernels, learned_step(): pl.pallas_call(functools.partial(step_kernel, rows=128), grid=(height //...  35.2 us
    all_to_all x1, blocking collectives, to_experts(): return lax.all_to_all(sent, EXPERT, 0, 0, tiled=True)  25.5 us
    all_to_all x3, starting transfers between devices, to_experts(): return lax.all_to_all(sent, EXPERT, 0, 0, tiled=True)  24.8 us
    all_to_all x3, waiting for transfers between devices, to_experts(): return lax.all_to_all(sent, EXPERT, 0, 0, tiled=True)  18.4 us
    pallas_call x1, Pallas kernels, expert_backward(): pl.pallas_call(backward_kernel, grid_spec=pltpu.PrefetchScalarGridSpec(nu...  16.8 us
    ppermute x12, starting transfers between devices, from_members(): lax.ppermute(pieces[k], 'mp', [(i, (i + k) % GROUPS) for i in range(GROUP...  15.1 us
    pallas_call x1, Pallas kernels, expert_forward(): pl.pallas_call(forward_kernel, grid_spec=pltpu.PrefetchScalarGridSpec(num...  14.9 us
    pallas_call x1, Pallas kernels, send_dy(): pl.pallas_call(send_dy_kernel, grid_spec=pltpu.PrefetchScalarGridSpec(num...  5.96 us
  transfers between devices with their start and end apart: 15, of which 5 were waited for; matrix products, arithmetic and copies ran while one was open for 2% of the time, Pallas kernels for 42%

profile of v4, /device:TPU:1, one launch (start us, length us, event | category | flops | bytes accessed | tf_op | source)
XLA Modules:
  0.0 176.0 jit_solution(4682622051652840429)
XLA Ops:
  0.7 3.1 %send_x.1 = bf16[1536,128]{1,0:T(8,128)(2,1)} custom-call(s32[2]{0:T(128)S(1)} %pad_add_fusion.mp.at, bf16[256,1024]{1,0:T(8,128)(2,1)} %tok_cols.3, s32[2,256]{1,0:T(2,128)} %bitcast.64), custom_call_target="tpu_custom_call" | custom-call | tf_op jit(solution)/shard_map/send_x/pallas_call | solution.py:129
  3.9 13.1 %all-to-all-start.1 = ((bf16[64,24,128]{2,1,0:T(8,128)(2,1)}), bf16[64,24,128]{2,1,0:T(8,128)(2,1)S(1)}, u32[]{:S(2)}, u32[]{:S(2)}) async-start(bf16[64,24,128]{2,1,0:T(8,128)(2,1)} %bitcast.15), calls=%async_computation.1 | async-start | bytes 786432 | tf_op jit(solution)/shard_map/all_to_all | solution.py:561
  17.0 0.8 multiply_bitcast_fusion
  18.7 6.0 %send_dy.1 = (bf16[2048,128]{1,0:T(8,128)(2,1)}, f32[256,128]{1,0:T(8,128)S(1)}) custom-call(s32[2]{0:T(128)S(1)} %pad_add_fusion.mp.at, bf16[256,1024]{1,0:T(8,128)(2,1)} %tok_cols.3, bf16[256,1024]{1,0:T(8,128)(2,1)} %cot_cols.1, s32[2,256]{1,0:T(2,128)} %bitcast.65, bf16[64,1024]{1,0:T(8,128)(2,1)S(1)} %bitcast.51), custom_call_target="tpu_custom_call" | custom-call | tf_op jit(solution)/shard_map/send_dy/pallas_call | solution.py:151
  24.7 0.6 multiply_reduce_fusion
  25.3 0.7 pad.11.clone
  26.3 5.7 %all-to-all-done.1 = bf16[64,24,128]{2,1,0:T(8,128)(2,1)S(1)} async-done(((bf16[64,24,128]{2,1,0:T(8,128)(2,1)}), bf16[64,24,128]{2,1,0:T(8,128)(2,1)S(1)}, u32[]{:S(2)}, u32[]{:S(2)}) %all-to-all-start.1) | async-done | bytes 393248 | tf_op jit(solution)/shard_map/all_to_all | solution.py:561
  32.1 5.6 %all-to-all-start = ((bf16[64,32,128]{2,1,0:T(8,128)(2,1)}), bf16[64,32,128]{2,1,0:T(8,128)(2,1)S(1)}, u32[]{:S(2)}, u32[]{:S(2)}) async-start(bf16[64,32,128]{2,1,0:T(8,128)(2,1)} %bitcast.13), calls=%async_computation | async-start | bytes 1048576 | tf_op jit(solution)/shard_map/all_to_all | solution.py:561
  37.7 1.4 collective-permute-start
  39.0 2.6 %collective-permute-start.1 = (bf16[1536,128]{1,0:T(8,128)(2,1)S(1)}, bf16[1536,128]{1,0:T(8,128)(2,1)S(1)}, u32[]{:S(2)}, u32[]{:S(2)}) collective-permute-start(bf16[1536,128]{1,0:T(8,128)(2,1)S(1)} %bitcast.46), channel_id=1, source_target_pairs={{0,2},{1,3},{2,0},{3,1},{4,6},{5,7},{6,4},{7,5},{8,10},{9,11},{10,... | collective-permute-start | bytes 1179656 | tf_op jit(solution)/shard_map/ppermute | solution.py:566
  41.6 1.1 collective-permute-start.2
  42.7 12.7 %all-to-all-done.side = bf16[64,32,128]{2,1,0:T(8,128)(2,1)S(1)} async-done(((bf16[64,32,128]{2,1,0:T(8,128)(2,1)}), bf16[64,32,128]{2,1,0:T(8,128)(2,1)S(1)}, u32[]{:S(2)}, u32[]{:S(2)}) %all-to-all-start) | async-done | bytes 524320 | tf_op jit(solution)/shard_map/all_to_all | solution.py:561
  55.4 1.4 collective-permute-start.6
  56.8 2.6 %collective-permute-start.7 = (bf16[1536,128]{1,0:T(8,128)(2,1)S(1)}, bf16[1536,128]{1,0:T(8,128)(2,1)S(1)}, u32[]{:S(2)}, u32[]{:S(2)}) collective-permute-start(bf16[1536,128]{1,0:T(8,128)(2,1)S(1)} %bitcast.41), channel_id=1, source_target_pairs={{0,2},{1,3},{2,0},{3,1},{4,6},{5,7},{6,4},{7,5},{8,10},{9,11},{10,... | collective-permute-start | bytes 1179656 | tf_op jit(solution)/shard_map/ppermute | solution.py:566
  59.4 1.1 collective-permute-start.8
  60.5 14.9 %expert_forward.1 = (bf16[768,1024]{1,0:T(8,128)(2,1)}, bf16[768,896]{1,0:T(8,128)(2,1)}, f32[768,896]{1,0:T(8,128)}, f32[768,896]{1,0:T(8,128)}, bf16[768,256]{...) custom-call(s32[2]{0:T(128)S(1)} %pad_add_fusion.mp.at, ...), custom_call_target="tpu_custom_call" | custom-call | tf_op jit(solution)/shard_map/expert_forward/pallas_call | solution.py:226
  75.9 1.8 %collective-permute-start.4 = (bf16[768,256]{1,0:T(8,128)(2,1)}, bf16[768,256]{1,0:T(8,128)(2,1)S(1)}, u32[]{:S(2)}, u32[]{:S(2)}) collective-permute-start(bf16[768,256]{1,0:T(8,128)(2,1)} %get-tuple-element.44), channel_id=1, source_target_pairs={{0,2},{1,3},{2,0},{3,1},{4,6},{5,7},{6,4},{7,5},{8,10},{9,11},{10,... | collective-permute-start | bytes 1179656 | tf_op jit(solution)/shard_map/ppermute | solution.py:566
  77.7 0.7 collective-permute-start.5
  78.4 16.8 %expert_backward.1 = (f32[1024,896]{1,0:T(8,128)}, f32[1024,896]{1,0:T(8,128)}, f32[896,1024]{1,0:T(8,128)}, f32[1,128]{1,0:T(1,128)S(1)}, f32[64,8,128]{2,1,0:T(8,128)S(1)}) custom-call(s32[2]{0:T(128)S(1)} %pad_add_fusion.mp.at, bf16[384,384]{1,0:T(8,128)(2,1)S(1)} %get-tuple-element.41.perm, bf16[1536,128]{1,0:T(8,128)(2,1)S(1)} %bitcast.43, ...), custom_call_target="tpu_custom_call" | custom-call | tf_op jit(solution)/shard_map/expert_backward/pallas_call | solution.py:362
  95.9 25.5 %all_to_all.20 = bf16[64,16,128]{2,1,0:T(8,128)(2,1)S(1)} all-to-all(bf16[64,16,128]{2,1,0:T(8,128)(2,1)S(1)} %pad_maximum_fusion.1), channel_id=1, replica_groups=mesh['expert_0'=8,'expert_1'=4,'expert_2'=2,'mp'=4] {'expert_0','expert_..., dimensions={0} | all-to-all | bytes 524288 | tf_op jit(solution)/shard_map/all_to_all | solution.py:561
  121.4 0.7 collective-permute-start.11
  122.1 1.3 collective-permute-start.10
  124.0 2.2 %collective-permute-done.10 = f32[16,128]{1,0:T(8,128)S(1)} collective-permute-done((f32[16,128]{1,0:T(8,128)S(1)}, f32[16,128]{1,0:T(8,128)S(1)}, u32[]{:S(2)}, u32[]{:S(2)}) %collective-permute-start.10) | collective-permute-done | bytes 8224 | tf_op jit(solution)/shard_map/ppermute | solution.py:566
  126.2 1.3 collective-permute-done.9
  127.5 0.9 pad_maximum_fusion
  128.4 6.1 %all-to-all-start.3 = ((bf16[64,40,128]{2,1,0:T(8,128)(2,1)}), bf16[64,40,128]{2,1,0:T(8,128)(2,1)S(1)}, u32[]{:S(2)}, u32[]{:S(2)}) async-start(bf16[64,40,128]{2,1,0:T(8,128)(2,1)} %pad_maximum_fusion), calls=%async_computation.3 | async-start | bytes 1310720 | tf_op jit(solution)/shard_map/all_to_all | solution.py:561
  134.5 0.6 fusion.15
  135.1 11.8 %learned_step.3 = bf16[1024,896]{1,0:T(8,128)(2,1)} custom-call(f32[3,16]{1,0:T(4,128)S(1)} %maximum_maximum_fusion.scalars, f32[1]{0:T(128)} %bitcast.23.rms, bf16[512,256]{1,0:T(8,128)(2,1)S(1)} %spread_weights.2.spread, f32[1024,896]{1,0:T(8,128)} %get-tuple-element.60.grad, bf16[1024,896]{1,0:T(8,128)(2,1)} %bitcast.57), custom_call_target="tpu_custom_call" | custom-call | tf_op jit(solution)/shard_map/learned_step/pallas_call | solution.py:482
  146.9 11.8 %learned_step.4 = bf16[1024,896]{1,0:T(8,128)(2,1)} custom-call(f32[3,16]{1,0:T(4,128)S(1)} %maximum_maximum_fusion.scalars, f32[1]{0:T(128)} %bitcast.25.rms, bf16[512,256]{1,0:T(8,128)(2,1)S(1)} %spread_weights.2.spread, f32[1024,896]{1,0:T(8,128)} %get-tuple-element.62.grad, bf16[1024,896]{1,0:T(8,128)(2,1)} %bitcast.59), custom_call_target="tpu_custom_call" | custom-call | tf_op jit(solution)/shard_map/learned_step/pallas_call | solution.py:482
  158.7 11.7 %learned_step.5 = bf16[896,1024]{1,0:T(8,128)(2,1)} custom-call(f32[3,16]{1,0:T(4,128)S(1)} %maximum_maximum_fusion.scalars, f32[1]{0:T(128)} %bitcast.28.rms, bf16[512,256]{1,0:T(8,128)(2,1)S(1)} %spread_weights.3.spread, f32[896,1024]{1,0:T(8,128)} %get-tuple-element.65.grad, bf16[896,1024]{1,0:T(8,128)(2,1)} %bitcast.55), custom_call_target="tpu_custom_call" | custom-call | tf_op jit(solution)/shard_map/learned_step/pallas_call | solution.py:482
  170.4 2.2 %mix.1 = bf16[256,256]{1,0:T(8,128)(2,1)} custom-call(s32[2]{0:T(128)S(1)} %pad_add_fusion.mp.at, f32[256,128]{1,0:T(8,128)S(1)} %get-tuple-element.36.aux, bf16[256,1024]{1,0:T(8,128)(2,1)S(1)} %copy-done, bf16[2560,128]{1,0:T(8,128)(2,1)S(1)} %bitcast.39), custom_call_target="tpu_custom_call" | custom-call | tf_op jit(solution)/shard_map/mix/pallas_call | solution.py:516
  172.5 3.5 %router_step.1 = bf16[64,1024]{1,0:T(8,128)(2,1)} custom-call(f32[5,16]{1,0:T(8,128)S(1)} %pad_maximum_fusion.2.net, f32[64,8,128]{2,1,0:T(8,128)S(1)} %convert_add_fusion.columns, bf16[64,1024]{1,0:T(8,128)(2,1)S(1)} %bitcast.52), custom_call_target="tpu_custom_call" | custom-call | tf_op jit(solution)/shard_map/router_step/pallas_call | solution.py:546
  (52 shorter events, 3.1 us)
Async XLA Ops:
  0.6 18.1 %copy-start.1 = (bf16[1024,64]{0,1:T(8,128)(2,1)S(1)}, bf16[1024,64]{0,1:T(8,128)(2,1)}, u32[]{:S(2)}) copy-start(bf16[1024,64]{0,1:T(8,128)(2,1)} %param.13) | copy-start | bytes 393220
  3.9 20.8 %copy-start.4 = (f32[16]{0:T(128)S(1)}, f32[16]{0:T(128)}, u32[]{:S(2)}) copy-start(f32[16]{0:T(128)} %param.19) | copy-start | bytes 196
  3.9 20.8 %copy-start.5 = (f32[16]{0:T(128)S(1)}, f32[16]{0:T(128)}, u32[]{:S(2)}) copy-start(f32[16]{0:T(128)} %param.18) | copy-start | bytes 196
  3.9 22.2 %copy-start.3 = (f32[3,16]{1,0:T(4,128)S(1)}, f32[3,16]{1,0:T(4,128)}, u32[]{:S(2)}) copy-start(f32[3,16]{1,0:T(4,128)} %param.17) | copy-start | bytes 580
  3.9 28.2 %all-to-all-start.1 = ((bf16[64,24,128]{2,1,0:T(8,128)(2,1)}), bf16[64,24,128]{2,1,0:T(8,128)(2,1)S(1)}, u32[]{:S(2)}, u32[]{:S(2)}) async-start(bf16[64,24,128]{2,1,0:T(8,128)(2,1)} %bitcast.15), calls=%async_computation.1 | async-start | bytes 786432 | tf_op jit(solution)/shard_map/all_to_all | solution.py:561
  32.1 23.3 %all-to-all-start = ((bf16[64,32,128]{2,1,0:T(8,128)(2,1)}), bf16[64,32,128]{2,1,0:T(8,128)(2,1)S(1)}, u32[]{:S(2)}, u32[]{:S(2)}) async-start(bf16[64,32,128]{2,1,0:T(8,128)(2,1)} %bitcast.13), calls=%async_computation | async-start | bytes 1048576 | tf_op jit(solution)/shard_map/all_to_all | solution.py:561
  37.7 21.8 %collective-permute-start = (bf16[1536,128]{1,0:T(8,128)(2,1)S(1)}, bf16[1536,128]{1,0:T(8,128)(2,1)S(1)}, u32[]{:S(2)}, u32[]{:S(2)}) collective-permute-start(bf16[1536,128]{1,0:T(8,128)(2,1)S(1)} %bitcast.45), channel_id=1, source_target_pairs={{0,1},{1,2},{2,3},{3,0},{4,5},{5,6},{6,7},{7,4},{8,9},{9,10},{10,1... | collective-permute-start | bytes 1179656 | tf_op jit(solution)/shard_map/ppermute | solution.py:566
  39.0 21.5 %collective-permute-start.1 = (bf16[1536,128]{1,0:T(8,128)(2,1)S(1)}, bf16[1536,128]{1,0:T(8,128)(2,1)S(1)}, u32[]{:S(2)}, u32[]{:S(2)}) collective-permute-start(bf16[1536,128]{1,0:T(8,128)(2,1)S(1)} %bitcast.46), channel_id=1, source_target_pairs={{0,2},{1,3},{2,0},{3,1},{4,6},{5,7},{6,4},{7,5},{8,10},{9,11},{10,... | collective-permute-start | bytes 1179656 | tf_op jit(solution)/shard_map/ppermute | solution.py:566
  41.6 18.8 %collective-permute-start.2 = (bf16[1536,128]{1,0:T(8,128)(2,1)S(1)}, bf16[1536,128]{1,0:T(8,128)(2,1)S(1)}, u32[]{:S(2)}, u32[]{:S(2)}) collective-permute-start(bf16[1536,128]{1,0:T(8,128)(2,1)S(1)} %bitcast.47), channel_id=1, source_target_pairs={{0,3},{1,0},{2,1},{3,2},{4,7},{5,4},{6,5},{7,6},{8,11},{9,8},{10,9... | collective-permute-start | bytes 1179656 | tf_op jit(solution)/shard_map/ppermute | solution.py:566
  55.4 22.3 %collective-permute-start.6 = (bf16[1536,128]{1,0:T(8,128)(2,1)S(1)}, bf16[1536,128]{1,0:T(8,128)(2,1)S(1)}, u32[]{:S(2)}, u32[]{:S(2)}) collective-permute-start(bf16[1536,128]{1,0:T(8,128)(2,1)S(1)} %bitcast.40), channel_id=1, source_target_pairs={{0,1},{1,2},{2,3},{3,0},{4,5},{5,6},{6,7},{7,4},{8,9},{9,10},{10,1... | collective-permute-start | bytes 1179656 | tf_op jit(solution)/shard_map/ppermute | solution.py:566
  56.8 21.6 %collective-permute-start.7 = (bf16[1536,128]{1,0:T(8,128)(2,1)S(1)}, bf16[1536,128]{1,0:T(8,128)(2,1)S(1)}, u32[]{:S(2)}, u32[]{:S(2)}) collective-permute-start(bf16[1536,128]{1,0:T(8,128)(2,1)S(1)} %bitcast.41), channel_id=1, source_target_pairs={{0,2},{1,3},{2,0},{3,1},{4,6},{5,7},{6,4},{7,5},{8,10},{9,11},{10,... | collective-permute-start | bytes 1179656 | tf_op jit(solution)/shard_map/ppermute | solution.py:566
  59.4 19.0 %collective-permute-start.8 = (bf16[1536,128]{1,0:T(8,128)(2,1)S(1)}, bf16[1536,128]{1,0:T(8,128)(2,1)S(1)}, u32[]{:S(2)}, u32[]{:S(2)}) collective-permute-start(bf16[1536,128]{1,0:T(8,128)(2,1)S(1)} %bitcast.42), channel_id=1, source_target_pairs={{0,3},{1,0},{2,1},{3,2},{4,7},{5,4},{6,5},{7,6},{8,11},{9,8},{10,9... | collective-permute-start | bytes 1179656 | tf_op jit(solution)/shard_map/ppermute | solution.py:566
  75.4 20.0 %collective-permute-start.3 = (bf16[768,256]{1,0:T(8,128)(2,1)}, bf16[768,256]{1,0:T(8,128)(2,1)S(1)}, u32[]{:S(2)}, u32[]{:S(2)}) collective-permute-start(bf16[768,256]{1,0:T(8,128)(2,1)} %get-tuple-element.43), channel_id=1, source_target_pairs={{0,1},{1,2},{2,3},{3,0},{4,5},{5,6},{6,7},{7,4},{8,9},{9,10},{10,1... | collective-permute-start | bytes 1179656 | tf_op jit(solution)/shard_map/ppermute | solution.py:566
  75.9 19.5 %collective-permute-start.4 = (bf16[768,256]{1,0:T(8,128)(2,1)}, bf16[768,256]{1,0:T(8,128)(2,1)S(1)}, u32[]{:S(2)}, u32[]{:S(2)}) collective-permute-start(bf16[768,256]{1,0:T(8,128)(2,1)} %get-tuple-element.44), channel_id=1, source_target_pairs={{0,2},{1,3},{2,0},{3,1},{4,6},{5,7},{6,4},{7,5},{8,10},{9,11},{10,... | collective-permute-start | bytes 1179656 | tf_op jit(solution)/shard_map/ppermute | solution.py:566
  77.7 18.2 %collective-permute-start.5 = (bf16[768,256]{1,0:T(8,128)(2,1)}, bf16[768,256]{1,0:T(8,128)(2,1)S(1)}, u32[]{:S(2)}, u32[]{:S(2)}) collective-permute-start(bf16[768,256]{1,0:T(8,128)(2,1)} %get-tuple-element.45), channel_id=1, source_target_pairs={{0,3},{1,0},{2,1},{3,2},{4,7},{5,4},{6,5},{7,6},{8,11},{9,8},{10,9... | collective-permute-start | bytes 1179656 | tf_op jit(solution)/shard_map/ppermute | solution.py:566
  95.2 28.2 %copy-start.2 = (bf16[768,256]{1,0:T(8,128)(2,1)S(1)}, bf16[768,256]{1,0:T(8,128)(2,1)}, u32[]{:S(2)}) copy-start(bf16[768,256]{1,0:T(8,128)(2,1)} %get-tuple-element.53.p0) | copy-start | bytes 1179652
  121.4 2.6 %collective-permute-start.11 = (f32[16,128]{1,0:T(8,128)S(1)}, f32[16,128]{1,0:T(8,128)S(1)}, u32[]{:S(2)}, u32[]{:S(2)}) collective-permute-start(f32[16,128]{1,0:T(8,128)S(1)} %convert_reduce_fusion), channel_id=1, source_target_pairs={{0,3},{1,0},{2,1},{3,2},{4,7},{5,4},{6,5},{7,6},{8,11},{9,8},{10,9... | collective-permute-start | bytes 24584 | tf_op jit(solution)/shard_map/ppermute | solution.py:566
  122.1 4.0 %collective-permute-start.10 = (f32[16,128]{1,0:T(8,128)S(1)}, f32[16,128]{1,0:T(8,128)S(1)}, u32[]{:S(2)}, u32[]{:S(2)}) collective-permute-start(f32[16,128]{1,0:T(8,128)S(1)} %convert_reduce_fusion), channel_id=1, source_target_pairs={{0,2},{1,3},{2,0},{3,1},{4,6},{5,7},{6,4},{7,5},{8,10},{9,11},{10,... | collective-permute-start | bytes 24584 | tf_op jit(solution)/shard_map/ppermute | solution.py:566
  123.4 4.0 %collective-permute-start.9 = (f32[16,128]{1,0:T(8,128)S(1)}, f32[16,128]{1,0:T(8,128)S(1)}, u32[]{:S(2)}, u32[]{:S(2)}) collective-permute-start(f32[16,128]{1,0:T(8,128)S(1)} %convert_reduce_fusion), channel_id=1, source_target_pairs={{0,1},{1,2},{2,3},{3,0},{4,5},{5,6},{6,7},{7,4},{8,9},{9,10},{10,1... | collective-permute-start | bytes 24584 | tf_op jit(solution)/shard_map/ppermute | solution.py:566
  128.4 41.9 %all-to-all-start.3 = ((bf16[64,40,128]{2,1,0:T(8,128)(2,1)}), bf16[64,40,128]{2,1,0:T(8,128)(2,1)S(1)}, u32[]{:S(2)}, u32[]{:S(2)}) async-start(bf16[64,40,128]{2,1,0:T(8,128)(2,1)} %pad_maximum_fusion), calls=%async_computation.3 | async-start | bytes 1310720 | tf_op jit(solution)/shard_map/all_to_all | solution.py:561
  158.7 11.7 %copy-start = (bf16[256,1024]{1,0:T(8,128)(2,1)S(1)}, bf16[256,1024]{1,0:T(8,128)(2,1)}, u32[]{:S(2)}) copy-start(bf16[256,1024]{1,0:T(8,128)(2,1)} %tok_cols.3) | copy-start | bytes 1572868
